TPU v7x, 32 devices: a whole 2x2x4 slice. The times are simulated.
32 devices in a mesh: blk: 4 (over x, core), smp: 8 (over z, y).
Axes of the slice: x: 2, y: 2, z: 4, core: 2. Of those that a mesh axis runs over, the one named last changes fastest.
Arguments:
- scaled_genotype_counts: bfloat16 [16384, 2048], P('smp', 'blk'), may hold values from -6 to 6
- adjusted_trait_scores: bfloat16 [16384, 8], P('smp'), may hold values from -6 to 6
- subset_membership: int32 [16384], P('smp'), may hold values from 0 to 4, as said below
- regularizer_lambdas: float32 [2], replicated, may hold values from 0.01 to 0.1
- unseen_subset_guesses: bfloat16 [8, 2048, 8, 8], P('smp', 'blk'), may hold values from -6 to 6
Outputs:
- oof: bfloat16 [16384, 8, 8], P('smp', None, 'blk')
- cross: float32 [8, 8, 16], P(None, 'blk', 'smp')
Inputs may be any that keep to these rules, and one draw needn't show every extreme that they name: `subset_membership`: every fold holds some samples.
All inputs are finite; a program needn't handle non-finite values.
Results may differ from a plain program's by a relative error of at most 0.0047.
Values may be sent and summed in bfloat16 or wider, within the bound.
No kernel may reach another device: no remote copies, remote signals or barrier semaphores. Data moves between devices by JAX's collectives and lax.ppermute only.
A program may use at most 128 MiB of HBM per device.

v0:
```python
import math

import jax
import jax.numpy as jnp
from jax import lax
from jax.sharding import PartitionSpec as P

BLOCK = 512
PHENOTYPIC_MEASURES = 8
FOLDS = 5
SHRINK_STRENGTH = 2


def invert_all_equations(
    normal_equation_stack, equation_targets, regularizer_lambdas, person_entries
):
    unit_diagonal = jnp.eye(BLOCK, dtype=jnp.float32)
    solved = []
    for position_number in range(SHRINK_STRENGTH):
        regressor_array = (
            normal_equation_stack
            + regularizer_lambdas[position_number] * person_entries * unit_diagonal
        )
        factor = jnp.linalg.cholesky(regressor_array)
        solved.append(
            jax.vmap(lambda c, b: jax.scipy.linalg.cho_solve((c, True), b))(
                factor, equation_targets
            )
        )
    return jnp.stack(solved, axis=-1)


def local(
    scaled_genotype_counts,
    adjusted_trait_scores,
    subset_membership,
    regularizer_lambdas,
    unseen_subset_guesses,
):
    rows = scaled_genotype_counts.shape[0]
    blocks = scaled_genotype_counts.shape[1] // BLOCK
    person_entries = rows * lax.axis_size("smp")
    scale = 1.0 / person_entries
    partial_pieces = [scaled_genotype_counts]
    groups = lax.axis_size("smp")
    per_dev = (FOLDS + groups - 1) // groups
    padded = per_dev * groups
    slot_fold = jnp.arange(padded, dtype=jnp.int32) % FOLDS
    away = (subset_membership[:, None] != slot_fold[None, :]).astype(jnp.bfloat16)
    twins = jnp.sum((slot_fold[:, None] == slot_fold[None, :]).astype(jnp.float32), axis=1)
    pick = (subset_membership[:, None] == slot_fold[None, :]).astype(jnp.float32) / twins[None, :]
    widened = [jnp.concatenate([piece, adjusted_trait_scores], axis=1) for piece in partial_pieces]
    stride = blocks * BLOCK
    chosen = away
    b = 0
    masked_values = partial_pieces[b][:, None, :] * chosen[:, :, None]
    terms = [
        jnp.einsum("rpe,ro->peo", masked_values, widened[b], preferred_element_type=jnp.float32)
    ]
    owned = lax.psum_scatter(
        jnp.stack(terms, axis=1).reshape(
            per_dev * stride * lax.axis_size("smp"), BLOCK + PHENOTYPIC_MEASURES
        ),
        "smp",
        scatter_dimension=0,
        tiled=True,
    )
    owned = owned.reshape(per_dev * blocks, BLOCK, BLOCK + PHENOTYPIC_MEASURES)
    weight_array = invert_all_equations(
        owned[:, :, :BLOCK], owned[:, :, BLOCK:], regularizer_lambdas, person_entries
    )
    coeffs_half = weight_array.reshape(
        per_dev, blocks, BLOCK, PHENOTYPIC_MEASURES * SHRINK_STRENGTH
    ).astype(jnp.bfloat16)
    piece = lax.all_gather(coeffs_half, "smp", axis=0, tiled=True)
    number = piece.shape[0]
    b = 0
    weights = jnp.transpose(piece[:, b], (1, 0, 2)).reshape(
        BLOCK, number * PHENOTYPIC_MEASURES * SHRINK_STRENGTH
    )
    product = jnp.dot(partial_pieces[b], weights, preferred_element_type=jnp.float32)
    outputs = [product.reshape(rows, number, PHENOTYPIC_MEASURES * SHRINK_STRENGTH)]
    fitted = jnp.stack(outputs, axis=0)
    chosen = jnp.sum(fitted * pick[None, :, :, None], axis=2)
    chosen = jnp.transpose(
        chosen.reshape(blocks, rows, PHENOTYPIC_MEASURES, SHRINK_STRENGTH), (1, 2, 0, 3)
    ).reshape(rows, PHENOTYPIC_MEASURES, blocks * SHRINK_STRENGTH)
    fold_predictions = (chosen * math.sqrt(person_entries / BLOCK)).astype(jnp.bfloat16)
    new_part = (
        jnp.einsum(
            "stf,stc->tfc",
            fold_predictions,
            lax.all_gather(fold_predictions, "blk", axis=2, tiled=True),
            preferred_element_type=jnp.float32,
        )
        * scale
    )
    old_part = (
        jnp.einsum(
            "stf,stc->tfc",
            fold_predictions,
            lax.all_gather(unseen_subset_guesses, "blk", axis=1, tiled=True)[0],
            preferred_element_type=jnp.float32,
        )
        * scale
    )
    partial_value = jnp.concatenate([old_part, new_part], axis=2)
    cross = lax.psum_scatter(partial_value, "smp", scatter_dimension=2, tiled=True)
    return (fold_predictions, cross)


def solution(mesh):
    return jax.shard_map(
        local,
        mesh=mesh,
        in_specs=(P("smp", "blk"), P("smp", None), P("smp"), P(), P("smp", "blk", None, None)),
        out_specs=(P("smp", None, "blk"), P(None, "blk", "smp")),
        check_vma=False,
    )
```

profile of v0, /device:TPU:0, one launch (start us, length us, event | category | flops | bytes accessed | tf_op | source)
XLA Modules:
  0.0 559.2 jit_solution(2177760942301147031)
XLA Ops:
  11.3 14.9 %fusion.4 = f32[8,65,8,512]{3,2,1,0:T(8,128)S(1)} fusion(bf16[2048,8]{0,1:T(8,128)(2,1)S(1)} %compare_convert_fusion, bf16[2048,512]{1,0:T(8,128)(2,1)} %param.8, bf16[2048,8]{0,1:T(8,128)(2,1)S(1)} %copy-done.7, bf16[2048,512]{0,1:T(8,128)(2,1)} %copy.38), kind=kOutput, calls=%fused_computation.8 | convolution fusion | flops 8736800768 | bytes 12779520 | tf_op jit(solution)/shard_map/rpe,ro->peo/dot_general | solution.py:58
  34.2 7.2 %all_gather.10 = bf16[1,2048,8,8]{1,3,2,0:T(8,128)(2,1)S(1)} all-gather(bf16[1,512,8,8]{1,3,2,0:T(8,128)(2,1)S(1)} %copy-done.4), channel_id=1, replica_groups=mesh['blk'=4,'smp'=8] {'blk'}, dimensions={1}, use_global_device_ids=true | all-gather | bytes 327680 | tf_op jit(solution)/shard_map/all_gather | solution.py:102
  41.7 141.6 %reduce-scatter.2.cloned.1.call-done = f32[512,520]{0,1:T(8,128)} async-done(((f32[4096,520]{0,1:T(8,128)}), f32[512,520]{0,1:T(8,128)}) %reduce-scatter.2.cloned.1.call-update) | async-done | bytes 1064976 | tf_op jit(solution)/shard_map/reduce_scatter | solution.py:60
  190.2 11.7 %custom-call.37 = f32[1,128,128]{2,1,0:T(8,128)S(1)} custom-call(f32[1,128,128]{2,1,0:T(8,128)S(1)} %cholesky.425), custom_call_target="Cholesky" | custom-call | tf_op jit(solution)/shard_map/jit(cholesky)/cholesky | solution.py:24
  202.0 9.8 %custom-call.38 = f32[1,1,128,128]{2,3,1,0:T(8,128)S(1)} custom-call(f32[1,1,128,128]{3,2,1,0:T(8,128)S(1)} %get-tuple-element.61), custom_call_target="InvertDiagBlocksLowerTriangular" | custom-call | tf_op jit(solution)/shard_map/jit(cholesky)/cholesky | solution.py:24
  214.5 11.7 %custom-call.39 = f32[1,128,128]{2,1,0:T(8,128)S(1)} custom-call(f32[1,128,128]{2,1,0:T(8,128)S(1)} %cholesky.429), custom_call_target="Cholesky" | custom-call | tf_op jit(solution)/shard_map/jit(cholesky)/cholesky | solution.py:24
  227.6 9.8 %custom-call.40 = f32[1,1,128,128]{2,3,1,0:T(8,128)S(1)} custom-call(f32[1,1,128,128]{3,2,1,0:T(8,128)S(1)} %get-tuple-element.58), custom_call_target="InvertDiagBlocksLowerTriangular" | custom-call | tf_op jit(solution)/shard_map/jit(cholesky)/cholesky | solution.py:24
  239.0 11.7 %custom-call.41 = f32[1,128,128]{2,1,0:T(8,128)S(1)} custom-call(f32[1,128,128]{2,1,0:T(8,128)S(1)} %cholesky.434), custom_call_target="Cholesky" | custom-call | tf_op jit(solution)/shard_map/jit(cholesky)/cholesky | solution.py:24
  251.5 9.8 %custom-call.42 = f32[1,1,128,128]{2,3,1,0:T(8,128)S(1)} custom-call(f32[1,1,128,128]{3,2,1,0:T(8,128)S(1)} %get-tuple-element.55), custom_call_target="InvertDiagBlocksLowerTriangular" | custom-call | tf_op jit(solution)/shard_map/jit(cholesky)/cholesky | solution.py:24
  262.7 12.1 %custom-call.43 = f32[1,128,128]{2,1,0:T(8,128)S(1)} custom-call(f32[1,128,128]{2,1,0:T(8,128)S(1)} %fusion.17), custom_call_target="Cholesky" | custom-call | tf_op jit(solution)/shard_map/jit(cholesky)/cholesky | solution.py:24
  278.3 8.5 %while.4 = (s32[]{:T(128)}, f32[1,512,512]{2,1,0:T(8,128)S(1)}, s32[4,2]{0,1:T(2,128)S(1)}, f32[4,1,128,128]{3,2,1,0:T(8,128)S(1)}, s32[]{:T(128)}) while((s32[]{:T(128)}, f32[1,512,512]{2,1,0:T(8,128)S(1)}, s32[4,2]{0,1:T(2,128)S(1)}, f32[4,1,128,128]{3,2,1,0:T(8,128)S(1)}, s32[]{:T(128)}) %tuple.65), condition=%wide.while_cond, body=%wide.while_body.sunk | while | flops 2 | bytes 131181 | solution.py:26
  286.8 39.3 %custom-call.44 = f32[1,4,128,128]{2,3,1,0:T(8,128)S(1)} custom-call(f32[1,4,128,128]{3,2,1,0:T(8,128)S(1)} %bitcast.387), custom_call_target="InvertDiagBlocksLowerTriangular" | custom-call | tf_op jit(solution)/shard_map/vmap(jit(_cho_solve))/triangular_solve | solution.py:26
  332.6 11.7 %custom-call.45 = f32[1,128,128]{2,1,0:T(8,128)S(1)} custom-call(f32[1,128,128]{2,1,0:T(8,128)S(1)} %cholesky.438), custom_call_target="Cholesky" | custom-call | tf_op jit(solution)/shard_map/jit(cholesky)/cholesky | solution.py:24
  344.4 9.8 %custom-call.46 = f32[1,1,128,128]{2,3,1,0:T(8,128)S(1)} custom-call(f32[1,1,128,128]{3,2,1,0:T(8,128)S(1)} %get-tuple-element.71), custom_call_target="InvertDiagBlocksLowerTriangular" | custom-call | tf_op jit(solution)/shard_map/jit(cholesky)/cholesky | solution.py:24
  355.0 11.7 %custom-call.47 = f32[1,128,128]{2,1,0:T(8,128)S(1)} custom-call(f32[1,128,128]{2,1,0:T(8,128)S(1)} %cholesky.442), custom_call_target="Cholesky" | custom-call | tf_op jit(solution)/shard_map/jit(cholesky)/cholesky | solution.py:24
  368.1 10.0 %custom-call.48 = f32[1,1,128,128]{2,3,1,0:T(8,128)S(1)} custom-call(f32[1,1,128,128]{3,2,1,0:T(8,128)S(1)} %get-tuple-element.68), custom_call_target="InvertDiagBlocksLowerTriangular" | custom-call | tf_op jit(solution)/shard_map/jit(cholesky)/cholesky | solution.py:24
  378.7 11.7 %custom-call.49 = f32[1,128,128]{2,1,0:T(8,128)S(1)} custom-call(f32[1,128,128]{2,1,0:T(8,128)S(1)} %cholesky.447), custom_call_target="Cholesky" | custom-call | tf_op jit(solution)/shard_map/jit(cholesky)/cholesky | solution.py:24
  391.1 9.8 %custom-call.50 = f32[1,1,128,128]{2,3,1,0:T(8,128)S(1)} custom-call(f32[1,1,128,128]{3,2,1,0:T(8,128)S(1)} %get-tuple-element.65), custom_call_target="InvertDiagBlocksLowerTriangular" | custom-call | tf_op jit(solution)/shard_map/jit(cholesky)/cholesky | solution.py:24
  401.5 11.9 %custom-call.51 = f32[1,128,128]{2,1,0:T(8,128)S(1)} custom-call(f32[1,128,128]{2,1,0:T(8,128)S(1)} %fusion.18), custom_call_target="Cholesky" | custom-call | tf_op jit(solution)/shard_map/jit(cholesky)/cholesky | solution.py:24
  417.8 12.0 %while.5 = (s32[]{:T(128)}, f32[1,512,512]{2,1,0:T(8,128)}, s32[4,2]{0,1:T(2,128)S(1)}, f32[4,1,128,128]{3,2,1,0:T(8,128)S(1)}, s32[]{:T(128)}) while((s32[]{:T(128)}, f32[1,512,512]{2,1,0:T(8,128)}, s32[4,2]{0,1:T(2,128)S(1)}, f32[4,1,128,128]{3,2,1,0:T(8,128)S(1)}, s32[]{:T(128)}) %tuple.70), condition=%wide.while_cond.clone, body=%wide.while_body.clone.sunk | while | flops 2 | bytes 131181 | solution.py:26
  429.9 39.3 %custom-call.52 = f32[1,4,128,128]{2,3,1,0:T(8,128)S(1)} custom-call(f32[1,4,128,128]{3,2,1,0:T(8,128)S(1)} %bitcast.386), custom_call_target="InvertDiagBlocksLowerTriangular" | custom-call | tf_op jit(solution)/shard_map/vmap(jit(_cho_solve))/triangular_solve | solution.py:26
  478.2 30.5 %all_gather.9 = bf16[8,1,512,16]{2,3,1,0:T(8,128)(2,1)S(1)} all-gather(bf16[1,1,512,16]{2,3,1,0:T(8,128)(2,1)S(1)} %convert_element_type.37), channel_id=1, replica_groups=mesh['blk'=4,'smp'=8] {'smp'}, dimensions={0}, use_global_device_ids=true | all-gather | bytes 147456 | tf_op jit(solution)/shard_map/all_gather | solution.py:75
  509.8 5.8 %all_gather.11 = bf16[2048,8,8]{0,1,2:T(8,128)(2,1)S(1)} all-gather(bf16[2048,8,2]{0,1,2:T(8,128)(2,1)S(1)} %copy.43), channel_id=1, replica_groups=mesh['blk'=4,'smp'=8] {'blk'}, dimensions={2}, use_global_device_ids=true | all-gather | bytes 327680 | tf_op jit(solution)/shard_map/all_gather | solution.py:93
  516.3 35.2 %all-reduce.1 = f32[8,2,16]{0,1,2:T(2,128)S(1)} all-reduce(f32[8,2,16]{0,1,2:T(2,128)S(1)} %copy.45), channel_id=3, replica_groups=mesh['blk'=4,'smp'=8] {'smp'}, use_global_device_ids=true, to_apply=%region_11.14.clone | all-reduce | flops 256 | bytes 2048
  (142 shorter events, 70.3 us)
Async XLA Ops:
  7.2 176.1 %reduce-scatter.2.cloned.1.call-start = ((), (), s32[]{:S(2)}) async-start(), calls=%async_computation.1 | async-start | bytes 9584640 | tf_op jit(solution)/shard_map/reduce_scatter | solution.py:60
  7.2 4.0 copy-start.5
  7.2 4.1 copy-start.7
  30.6 0.7 copy-start.6
  30.6 2.4 copy-start.8
  30.6 3.6 copy-start.4
  189.2 1.0 copy-start.2
  278.3 76.1 %copy-start.1 = (f32[1,512,512]{2,1,0:T(8,128)S(1)}, f32[1,512,512]{2,1,0:T(8,128)}, u32[]{:S(2)}) copy-start(f32[1,512,512]{2,1,0:T(8,128)} %get-tuple-element.78) | copy-start | bytes 3145732
  416.7 92.1 %copy-start = (bf16[2048,512]{1,0:T(8,128)(2,1)S(1)}, bf16[2048,512]{1,0:T(8,128)(2,1)}, u32[]{:S(2)}) copy-start(bf16[2048,512]{1,0:T(8,128)(2,1)} %param.8) | copy-start | bytes 6291460
  509.7 42.4 %copy-start.3 = (bf16[2048,8,2]{0,2,1:T(2,128)(2,1)}, bf16[2048,8,2]{0,2,1:T(2,128)(2,1)S(1)}, u32[]{:S(2)}) copy-start(bf16[2048,8,2]{0,2,1:T(2,128)(2,1)S(1)} %convert_element_type.41) | copy-start | bytes 196612
Sparse Core Ops, SparseCore 0:
  30.7 152.5 reduce-scatter.1
where the time goes:
time: 569 us; the launch traced here: 559 us
  other arithmetic  244 us (43%)
  waiting for transfers between devices  142 us (25%)
  blocking collectives  78.7 us (14%)
  matrix products  38.2 us (7%)
  local copies, waits for them, and re-layouts  35.1 us (6%)
  between operations  21.6 us (4%)
    another operation x30, other arithmetic, invert_all_equations(): factor = jnp.linalg.cholesky(regressor_array)  159 us
    reduce_scatter x1, waiting for transfers between devices, local(): lax.psum_scatter(jnp.stack(terms, axis=1).reshape(per_dev * stride * lax....  142 us
    another operation x5, other arithmetic, invert_all_equations(): jax.scipy.linalg.cho_solve((c, True), b)  79.9 us
    unnamed x1, blocking collectives  35.2 us
    all_gather x1, blocking collectives, local(): piece = lax.all_gather(coeffs_half, 'smp', axis=0, tiled=True)  30.5 us
    another operation x27, local copies, waits for them, and re-layouts, invert_all_equations(): jax.scipy.linalg.cho_solve((c, True), b)  20.4 us
    dot_general x1, matrix products, local(): jnp.einsum('rpe,ro->peo', masked_values, widened[b], preferred_element_ty...  14.9 us
    another operation x28, matrix products, invert_all_equations(): jax.scipy.linalg.cho_solve((c, True), b)  14.5 us
  transfers between devices with their start and end apart: 1, of which 1 were waited for; matrix products, arithmetic and copies ran while one was open for 0% of the time, Pallas kernels for 0%

commit v1 on v0

v1 whole, which is shorter than its diff:
```python
import math

import jax
import jax.numpy as jnp
from jax import lax
from jax.experimental import pallas as pl
from jax.experimental.pallas import tpu as pltpu
from jax.sharding import PartitionSpec as P

BLOCK = 512
PHENOTYPIC_MEASURES = 8
FOLDS = 5
SHRINK_STRENGTH = 2

LANES = 128
TILE = 8
HALF = 64
PACKED = 272
WIRE = 288
DIGIT = 32766.0
BOUND = 36.0
OWNERS = (0, 2, 3, 4, 6)

f32 = jnp.float32
bf16 = jnp.bfloat16
VMEM = pl.BlockSpec(memory_space=pltpu.VMEM)
SMEM = pl.BlockSpec(memory_space=pltpu.SMEM)
PARAMS = pltpu.CompilerParams(vmem_limit_bytes=60 * 1024 * 1024)


def mm(a, b, precision=lax.Precision.HIGHEST):
    return lax.dot_general(a, b, (((1,), (0,)), ((), ())), precision=precision, preferred_element_type=f32)


def nt(a, b, precision=None):
    return lax.dot_general(a, b, (((1,), (1,)), ((), ())), precision=precision, preferred_element_type=f32)


def iota(shape, dim):
    return lax.broadcasted_iota(jnp.int32, shape, dim)


def square_masks():
    row, col = iota((LANES, LANES), 0), iota((LANES, LANES), 1)
    return row == col, col < row


def column(row_vector, eye):
    return jnp.sum(jnp.where(eye, jnp.broadcast_to(row_vector, (LANES, LANES)), 0.0), axis=1, keepdims=True)


LAYOUT = (((0, 1), (1, 0), (2, 3), (3, 2)), ((2, 0), (2, 1), (3, 0), (3, 1)))


def place(r, c):
    return slice(r * LANES, (r + 1) * LANES), slice(c * LANES, (c + 1) * LANES)


def pair_scale(r, c, rows, cols, low):
    i, j = LAYOUT[r][c]
    if (r, c) in ((0, 0), (0, 2)):
        return jnp.where(low, cols[i] * rows[i], cols[j] * rows[j])
    return cols[i] * rows[j]


def split(vector):
    return [vector[:, i * LANES : (i + 1) * LANES] for i in range(BLOCK // LANES)]


def to_int(x):
    return jnp.floor(x + 0.5).astype(jnp.int32).astype(jnp.int16)


def digits(value, bound):
    u = value * (DIGIT / bound)
    high = jnp.floor(u)
    return high, (u - high) * DIGIT


def undigits(high, low, bound):
    return (high + low * (1.0 / DIGIT)) * (bound / DIGIT)


def encode(get, msg_ref, bound, eye, low):
    diag = get(slice(264, 265), slice(0, BLOCK))
    dh, dl = digits(diag, bound)
    dl = jnp.floor(dl + 0.5)
    scale = lax.rsqrt(undigits(dh, dl, bound) + 1e-3)
    rows = split(scale)
    cols = [column(r, eye) for r in rows]
    for r in range(2):
        for c in range(4):
            rs, cs = place(r, c)
            msg_ref[rs, cs] = to_int(get(rs, cs) * (pair_scale(r, c, rows, cols, low) * DIGIT))
    xh, xl = digits(get(slice(256, 264), slice(0, BLOCK)), bound)
    msg_ref[256:272, :] = to_int(jnp.concatenate([xh, xl], axis=0))
    spare = jnp.zeros((14, BLOCK), f32)
    msg_ref[272:288, :] = to_int(jnp.concatenate([dh, dl, spare], axis=0))


def decode(msg_ref, bound, eye, low):
    tail = msg_ref[272:288, :].astype(f32)
    diag = undigits(tail[0:1], tail[1:2], bound)
    scale = jnp.sqrt(diag + 1e-3)
    rows = split(scale)
    cols = [column(r, eye) for r in rows]

    def matrix(r, c):
        rs, cs = place(r, c)
        return msg_ref[rs, cs].astype(f32) * (pair_scale(r, c, rows, cols, low) * (1.0 / DIGIT))

    def rest():
        x = msg_ref[256:272, :].astype(f32)
        return undigits(x[0:8], x[8:16], bound), diag

    return matrix, rest


def add_message(dst_ref, src_ref, msg_ref, bound, eye, low):
    matrix, rest = decode(msg_ref, bound, eye, low)
    for r in range(2):
        for c in range(4):
            rs, cs = place(r, c)
            dst_ref[rs, cs] = src_ref[rs, cs] + matrix(r, c)
    xy, diag = rest()
    dst_ref[256:264, :] = src_ref[256:264, :] + xy
    dst_ref[264:272, :] = src_ref[264:272, :] + jnp.concatenate([diag, jnp.zeros((7, BLOCK), f32)], axis=0)


def reader(ref):
    return lambda rows, cols: ref[rows, cols]


def gram_one(fold, x_ref, xt_ref, f_ref, out_ref, eye, low):
    mask = jnp.where(f_ref[...] != fold, 1.0, 0.0).astype(bf16)
    g0 = jnp.dot(xt_ref[0:256, :] * mask, x_ref[:, 0:256], preferred_element_type=f32)
    g1 = jnp.dot(xt_ref[256:528, :] * mask, x_ref[...], preferred_element_type=f32)

    def block(i, j):
        rs, cs = place(i, j)
        return g0[rs, cs] if i < 2 else g1[(i - 2) * LANES : (i - 1) * LANES, cs]

    for r in range(2):
        for c in range(4):
            i, j = LAYOUT[r][c]
            rs, cs = place(r, c)
            if (r, c) in ((0, 0), (0, 2)):
                out_ref[rs, cs] = jnp.where(low, block(i, i), jnp.where(eye, 0.0, block(j, j)))
            else:
                out_ref[rs, cs] = block(i, j)
    diag = [jnp.sum(jnp.where(eye, block(i, i), 0.0), axis=0, keepdims=True) for i in range(4)]
    out_ref[256:264, :] = g1[256:264, :]
    out_ref[264:272, :] = jnp.concatenate([jnp.concatenate(diag, axis=1), jnp.zeros((7, BLOCK), f32)], axis=0)


def load_transposed(x_ref, yt_ref, xt_ref):
    xt_ref[0:BLOCK, :] = x_ref[...].T
    xt_ref[BLOCK : BLOCK + 16, :] = jnp.concatenate([yt_ref[...], jnp.zeros_like(yt_ref[...])], axis=0)


def gram_send_kernel(info_ref, x_ref, yt_ref, f_ref, msg_ref, keep_ref, xt_ref, work_ref, *, bound):
    eye, low = square_masks()
    load_transposed(x_ref, yt_ref, xt_ref)
    for slot, dst in ((0, work_ref), (1, keep_ref), (3, work_ref)):
        gram_one(info_ref[slot], x_ref, xt_ref, f_ref, dst, eye, low)
        encode(reader(dst), msg_ref.at[{0: 0, 1: 1, 3: 2}[slot]], bound, eye, low)


def gram_keep_kernel(info_ref, x_ref, yt_ref, f_ref, keep_ref, xt_ref):
    eye, low = square_masks()
    load_transposed(x_ref, yt_ref, xt_ref)
    for n, slot in enumerate((2, 4)):
        gram_one(info_ref[slot], x_ref, xt_ref, f_ref, keep_ref.at[n], eye, low)


def second_kernel(info_ref, k1_ref, k24_ref, p1_ref, p2_ref, p3_ref, msg_ref, keep_ref, s1_ref, s2_ref, *, bound):
    eye, low = square_masks()
    add_message(s2_ref, k24_ref.at[0], p1_ref, bound, eye, low)
    add_message(s1_ref, k1_ref, p2_ref, bound, eye, low)
    add_message(keep_ref.at[1], k24_ref.at[1], p3_ref, bound, eye, low)
    first = info_ref[5] == 1
    encode(lambda r, c: jnp.where(first, s1_ref[r, c], s2_ref[r, c]), msg_ref.at[0], bound, eye, low)
    encode(reader(keep_ref.at[1]), msg_ref.at[1], bound, eye, low)
    keep_ref[0] = jnp.where(first, s2_ref[...], s1_ref[...])


def third_kernel(info_ref, k_ref, p4_ref, p5_ref, msg_ref, keep_ref, sa_ref, sb_ref, *, bound):
    eye, low = square_masks()
    add_message(sa_ref, k_ref.at[0], p4_ref, bound, eye, low)
    add_message(sb_ref, k_ref.at[1], p5_ref, bound, eye, low)
    upper = info_ref[6] == 1
    encode(lambda r, c: jnp.where(upper, sa_ref[r, c], sb_ref[r, c]), msg_ref, bound, eye, low)
    keep_ref[...] = jnp.where(upper, sb_ref[...], sa_ref[...])


def sublane(x, p):
    return jnp.broadcast_to(x[p : p + 1, :], (TILE, LANES))


def tree(terms):
    terms = list(terms)
    while len(terms) > 1:
        terms = [terms[i] + terms[i + 1] if i + 1 < len(terms) else terms[i] for i in range(0, len(terms), 2)]
    return terms[0]


def invert_pair(tiles):
    lane, sub = iota((TILE, LANES), 1), iota((TILE, LANES), 0)
    col = lane % HALF
    half = lane - col
    here = [sub == p for p in range(TILE)]
    tiles = list(tiles)
    count = len(tiles)
    for g in range(count):
        inside = (col >= g * TILE) & (col < (g + 1) * TILE)
        index = [half + (g * TILE + q) for q in range(TILE)]

        def spread(t, q):
            return jnp.take_along_axis(t, index[q], axis=1)

        c = [spread(tiles[g], q) for q in range(TILE)]
        r = jnp.where(inside, jnp.where(col - g * TILE == sub, 1.0, 0.0), tiles[g])
        for p in range(0, TILE, 2):
            cp, cn = c[p], c[p + 1]
            a, b, d = sublane(cp, p), sublane(cp, p + 1), sublane(cn, p + 1)
            inv = 1.0 / (a * d - b * b)

            def eliminate(x):
                e0, e1 = sublane(x, p), sublane(x, p + 1)
                f0, f1 = d * e0 - b * e1, a * e1 - b * e0
                return jnp.where(here[p], f0 * inv, jnp.where(here[p + 1], f1 * inv, x - (cp * f0 + cn * f1) * inv))

            for q in range(p + 2, TILE):
                c[q] = eliminate(c[q])
            r = eliminate(r)
        rows = [sublane(r, p) for p in range(TILE)]
        for i in [(g + 1) % count] + [i for i in range(count) if i != g and i != (g + 1) % count]:
            t = tiles[i]
            tiles[i] = jnp.where(inside, 0.0, t) - tree([spread(t, p) * rows[p] for p in range(TILE)])
        tiles[g] = r
    return tiles


def block_diagonal(t):
    left = iota(t.shape, 1) < HALF
    return jnp.concatenate([jnp.where(left, t, 0.0), jnp.where(left, 0.0, t)], axis=0)


def solve_kernel(shift_ref, k_ref, p_ref, o_ref, m_ref, w_ref, x_ref, *, bound):
    eye, low = square_masks()
    matrix, rest = decode(p_ref, bound, eye, low)
    n = BLOCK

    def put(rows, t, c):
        u = pltpu.roll(t, HALF, 1)
        left = iota(t.shape, 1) < HALF
        m_ref[rows, 2 * c * LANES : (2 * c + 1) * LANES] = jnp.where(left, t, u)
        m_ref[rows, (2 * c + 1) * LANES : (2 * c + 2) * LANES] = jnp.where(left, u, t)

    xy, extra = rest()
    diag = split(k_ref[264:265, :] + extra)
    for r in range(2):
        for c in range(4):
            i, j = LAYOUT[r][c]
            t = k_ref[place(r, c)] + matrix(r, c)
            u = t.T
            if (r, c) in ((0, 0), (0, 2)):
                put(place(i, 0)[0], jnp.where(eye, diag[i], jnp.where(low, t, u)), i)
                put(place(j, 0)[0], jnp.where(eye, diag[j], jnp.where(low, u, t)), j)
            else:
                put(place(i, 0)[0], t, j)
                put(place(j, 0)[0], u, i)
    right = k_ref[256:264, :] + xy
    for c in range(4):
        put(slice(n, n + 8), right[:, c * LANES : (c + 1) * LANES], c)

    lane, sub = iota((HALF, LANES), 1), iota((HALF, LANES), 0)
    shift = jnp.where(lane % HALF == sub, jnp.where(lane < HALF, shift_ref[0], shift_ref[1]), 0.0)
    blocks = n // HALF
    for b in range(blocks):
        rs, cs = slice(b * HALF, (b + 1) * HALF), slice(b * LANES, (b + 1) * LANES)
        top = m_ref[rs, cs] + shift
        tiles = invert_pair([top[i * TILE : (i + 1) * TILE] for i in range(HALF // TILE)])
        inverse = block_diagonal(jnp.concatenate(tiles, axis=0))
        nx = (b + 1) * HALF
        w = mm(m_ref[nx:, cs], inverse)
        w_ref[nx:, cs] = w
        for j in range(b + 1, blocks):
            js = slice(j * LANES, (j + 1) * LANES)
            m_ref[nx:, js] = m_ref[nx:, js] - mm(w, block_diagonal(m_ref[rs, js]))
    for b in reversed(range(blocks)):
        cs = slice(b * LANES, (b + 1) * LANES)
        x = w_ref[n:, cs]
        if b + 1 < blocks:
            below = [block_diagonal(w_ref[i * HALF : (i + 1) * HALF, cs]) for i in range(b + 1, blocks)]
            x = x - mm(x_ref[:, (b + 1) * LANES :], jnp.concatenate(below, axis=0))
        x_ref[:, cs] = x
    left = iota((8, LANES), 1) < HALF
    for c in range(4):
        even, odd = x_ref[:, 2 * c * LANES : (2 * c + 1) * LANES], x_ref[:, (2 * c + 1) * LANES : (2 * c + 2) * LANES]
        first = jnp.where(left, even, pltpu.roll(odd, HALF, 1))
        second = jnp.where(left, pltpu.roll(even, HALF, 1), odd)
        o_ref[:, c * LANES : (c + 1) * LANES] = jnp.concatenate([first, second], axis=0).astype(bf16)


def predict_kernel(info_ref, x_ref, b_ref, f_ref, o_ref, *, scale):
    weights = jnp.concatenate([b_ref[info_ref[8 + k]] for k in range(FOLDS)], axis=0)
    fitted = nt(weights, x_ref[...])
    folds = f_ref[...]
    total = jnp.zeros((16, folds.shape[1]), f32)
    for k in range(FOLDS):
        total = jnp.where(folds == k, fitted[16 * k : 16 * (k + 1)], total)
    o_ref[...] = (total * scale).astype(bf16)


def cross_kernel(o_ref, j_ref, g_ref, c_ref, *, scale):
    own = o_ref[...]
    count, width = g_ref.shape[0], g_ref.shape[2]
    prior = g_ref.shape[1] // 8
    old = tree([nt(own[:, b * width : (b + 1) * width], g_ref[b]) for b in range(count)])
    new = nt(own, j_ref[...])
    t_row, t_old = iota(old.shape, 0) % 8, iota(old.shape, 1) // prior
    t_new = iota(new.shape, 1) % 8
    old = jnp.where(t_row == t_old, old, 0.0)
    new = jnp.where(iota(new.shape, 0) % 8 == t_new, new, 0.0)
    pick_old = jnp.where(iota((prior, old.shape[1]), 1) % prior == iota((prior, old.shape[1]), 0), 1.0, 0.0)
    features = new.shape[1] // 8
    pick_new = jnp.where(iota((features, new.shape[1]), 1) // 8 == iota((features, new.shape[1]), 0), 1.0, 0.0)
    high = lax.Precision.HIGHEST
    c_ref[0:prior, :] = nt(pick_old, old, high) * scale
    c_ref[prior : prior + features, :] = nt(pick_new, new, high) * scale


def make_local(mesh):
    n_blk, n_smp = mesh.shape["blk"], mesh.shape["smp"]
    if n_smp != 8:
        raise NotImplementedError(n_smp)

    def pairs(bit, sends):
        out = []
        for b in range(n_blk):
            for s in range(n_smp):
                role = s ^ (7 if b & 1 else 0)
                if sends(role & 1, role >> 1 & 1, role >> 2):
                    out.append((b * n_smp + s, b * n_smp + (s ^ bit)))
        return out

    def move(x, bit, sends):
        return lax.ppermute(x, ("blk", "smp"), pairs(bit, sends))

    def local(x, traits, folds, lambdas, guesses):
        rows = x.shape[0]
        total = rows * n_smp
        bound = BOUND * total
        mirror = 7 * (lax.axis_index("blk") & 1)
        role = lax.axis_index("smp") ^ mirror
        b0, b1, b2 = role & 1, role >> 1 & 1, role >> 2
        info = jnp.stack(
            [
                jnp.where(b0 == 0, 2, 0),
                jnp.int32(1) + 0 * b0,
                jnp.where(b0 == 0, 0, 2),
                jnp.where(b1 == 0, 4, 3),
                jnp.where(b1 == 0, 3, 4),
                jnp.where(b0 == b1, 1, 0),
                b2,
                b2,
            ]
            + [o ^ mirror for o in OWNERS]
            + [b2] * 3
        ).astype(jnp.int32)
        shift = lambdas * total
        yt = traits.T
        f_row = folds.reshape(1, rows)
        prior = jnp.transpose(guesses[0], (1, 2, 0)).reshape(-1, guesses.shape[1])

        def call(kernel, outs, specs, scratch, *args, **static):
            import functools

            return pl.pallas_call(
                functools.partial(kernel, **static),
                out_shape=outs,
                in_specs=specs,
                out_specs=jax.tree.map(lambda _: VMEM, outs),
                scratch_shapes=scratch,
                compiler_params=PARAMS,
            )(*args)

        def packed(*lead):
            return jax.ShapeDtypeStruct((*lead, PACKED, BLOCK), f32)

        def wire(*lead):
            return jax.ShapeDtypeStruct((*lead, WIRE, BLOCK), jnp.int16)

        xt = pltpu.VMEM((BLOCK + 16, rows), bf16)
        work = pltpu.VMEM((PACKED, BLOCK), f32)
        msg, k1 = call(
            gram_send_kernel, (wire(3), packed()), [SMEM, VMEM, VMEM, VMEM], [xt, work], info, x, yt, f_row, bound=bound
        )
        p1 = move(msg[0], 1, lambda u, v, w: True)
        p2 = move(msg[1], 1, lambda u, v, w: u == 1)
        p3 = move(msg[2], 2, lambda u, v, w: True)
        k24 = call(gram_keep_kernel, packed(2), [SMEM, VMEM, VMEM, VMEM], [xt], info, x, yt, f_row)
        msg, keep = call(
            second_kernel, (wire(2), packed(2)), [SMEM] + [VMEM] * 5, [work, work], info, k1, k24, p1, p2, p3, bound=bound
        )
        p4 = move(msg[0], 2, lambda u, v, w: (u, v) != (1, 1))
        p5 = move(msg[1], 1, lambda u, v, w: u == 1)
        msg, keep = call(
            third_kernel, (wire(), packed()), [SMEM] + [VMEM] * 3, [work, work], info, keep, p4, p5, bound=bound
        )
        p6 = move(msg, 4, lambda u, v, w: u == 0 or (u, v, w) == (1, 1, 1))
        beta = call(
            solve_kernel,
            jax.ShapeDtypeStruct((16, BLOCK), bf16),
            [SMEM, VMEM, VMEM],
            [pltpu.VMEM((BLOCK + 8, 2 * BLOCK), f32), pltpu.VMEM((BLOCK + 8, 2 * BLOCK), f32), pltpu.VMEM((8, 2 * BLOCK), f32)],
            shift,
            keep,
            p6,
            bound=bound,
        )
        betas = lax.all_to_all(jnp.broadcast_to(beta[None], (n_smp, 16, BLOCK)), "smp", 0, 0)
        oof = call(
            predict_kernel,
            jax.ShapeDtypeStruct((16, rows), bf16),
            [SMEM, VMEM, VMEM, VMEM],
            [],
            info,
            x,
            betas,
            f_row,
            scale=math.sqrt(total / BLOCK),
        )
        prior_all = lax.all_gather(prior, "blk", axis=0)
        oof_all = lax.all_gather(oof, "blk", axis=0, tiled=True)
        n_cross = prior.shape[0] // 8 + 2 * n_blk
        part = call(
            cross_kernel,
            jax.ShapeDtypeStruct((n_cross, 16), f32),
            [VMEM] * 3,
            [],
            oof,
            oof_all,
            prior_all,
            scale=1.0 / total,
        )
        part = lax.all_to_all(part.reshape(n_smp, n_cross // n_smp, 16), "smp", 0, 0)
        cross = jnp.sum(part, axis=0).reshape(n_cross // n_smp, 2, 8)
        return (
            jnp.transpose(oof.reshape(2, 8, rows), (2, 1, 0)),
            jnp.transpose(cross, (2, 1, 0)),
        )

    return local


def solution(mesh):
    return jax.shard_map(
        make_local(mesh),
        mesh=mesh,
        in_specs=(P("smp", "blk"), P("smp", None), P("smp"), P(), P("smp", "blk", None, None)),
        out_specs=(P("smp", None, "blk"), P(None, "blk", "smp")),
        check_vma=False,
    )
```

time: 569 us -> 120 us (0.21); the launches traced: 559 us -> 119 us
  other arithmetic: 244 us -> 0.53 us
  waiting for transfers between devices: 142 us -> 23.9 us
  blocking collectives: 78.7 us -> 13.5 us
  Pallas kernels: 0 us -> 45.4 us
  matrix products: 38.2 us -> 0 us
  local copies, waits for them, and re-layouts: 35.1 us -> 9.27 us
  starting transfers between devices: 0.04 us -> 25.6 us
  between operations: 21.6 us -> 0.74 us
    another operation x38 -> x0, other arithmetic: 239 us -> none  [the longest x30 159 us: invert_all_equations(): factor = jnp.linalg.cholesky(regressor_array)]
    reduce_scatter x1 -> x0, waiting for transfers between devices: 142 us -> none  [local(): lax.psum_scatter(jnp.stack(terms, axis=1).reshape(per_dev * stride * lax....]
    pallas_call x0 -> x7, Pallas kernels: none -> 45.4 us  [call(): pl.pallas_call(functools.partial(kernel, **static), out_shape=outs, in_sp...]
    unnamed x1 -> x0, blocking collectives: 35.2 us -> none
    all_gather x3 -> x2, blocking collectives: 43.5 us -> 13.5 us  [the longest x1 7.32 us: local(): oof_all = lax.all_gather(oof, 'blk', axis=0, tiled=True)]
    another operation x37 -> x1, local copies, waits for them, and re-layouts: 25.9 us -> 0.63 us  [local(): jnp.stack([jnp.where(b0 == 0, 2, 0), jnp.int32(1) + 0 * b0, jnp.where(b0...]
    another operation x40 -> x0, matrix products: 21.9 us -> none  [the longest x28 14.5 us: invert_all_equations(): jax.scipy.linalg.cho_solve((c, True), b)]
    ppermute x0 -> x6, waiting for transfers between devices: none -> 17.8 us  [move(): return lax.ppermute(x, ('blk', 'smp'), pairs(bit, sends))]
  transfers between devices with their start and end apart: 1 -> 8, of which waited for: 1 -> 7; matrix products, arithmetic and copies ran while one was open for 0% -> 2% of each run, Pallas kernels for 0% -> 4%
where the time goes in v1:
time: 120 us; the launch traced here: 119 us
  Pallas kernels  45.4 us (38%)
  starting transfers between devices  25.6 us (21%)
  waiting for transfers between devices  23.9 us (20%)
  blocking collectives  13.5 us (11%)
  local copies, waits for them, and re-layouts  9.27 us (8%)
    pallas_call x7, Pallas kernels, call(): pl.pallas_call(functools.partial(kernel, **static), out_shape=outs, in_sp...  45.4 us
    ppermute x6, waiting for transfers between devices, move(): return lax.ppermute(x, ('blk', 'smp'), pairs(bit, sends))  17.8 us
    ppermute x6, starting transfers between devices, move(): return lax.ppermute(x, ('blk', 'smp'), pairs(bit, sends))  15.6 us
    all_gather x1, blocking collectives, local(): oof_all = lax.all_gather(oof, 'blk', axis=0, tiled=True)  7.32 us
    all_gather x1, blocking collectives, local(): prior_all = lax.all_gather(prior, 'blk', axis=0)  6.23 us
    all_to_all x1, starting transfers between devices, local(): lax.all_to_all(part.reshape(n_smp, n_cross // n_smp, 16), 'smp', 0, 0)  5.23 us
    all_to_all x1, waiting for transfers between devices, local(): lax.all_to_all(part.reshape(n_smp, n_cross // n_smp, 16), 'smp', 0, 0)  4.98 us
    all_to_all x1, starting transfers between devices, local(): lax.all_to_all(jnp.broadcast_to(beta[None], (n_smp, 16, BLOCK)), 'smp', 0...  4.78 us
  transfers between devices with their start and end apart: 8, of which 7 were waited for; matrix products, arithmetic and copies ran while one was open for 2% of the time, Pallas kernels for 4%

profile of v1, /device:TPU:0, one launch (start us, length us, event | category | flops | bytes accessed | tf_op | source)
XLA Modules:
  0.0 118.9 jit_solution(4387775638404471420)
XLA Ops:
  1.3 5.7 %shard_map.68 = (s16[3,288,512]{2,1,0:T(8,128)(2,1)}, f32[272,512]{1,0:T(8,128)}) custom-call(s32[16]{0:T(128)} %stack.51.info_ref, bf16[2048,512]{1,0:T(8,128)(2,1)} %x_ref.5, bf16[8,2048]{1,0:T(8,128)(2,1)} %bitcast.35, s32[1,2048]{1,0:T(1,128)} %bitcast.37), custom_call_target="tpu_custom_call" | custom-call | tf_op jit(solution)/shard_map/pallas_call | solution.py:380
  8.2 3.1 %collective-permute-start = (s16[288,512]{1,0:T(8,128)(2,1)S(1)}, s16[288,512]{1,0:T(8,128)(2,1)S(1)}, u32[]{:S(2)}, u32[]{:S(2)}) collective-permute-start(s16[288,512]{1,0:T(8,128)(2,1)S(1)} %get-tuple-element.20), channel_id=1, source_target_pairs={{0,1},{1,0},{2,3},{3,2},{4,5},{5,4},{6,7},{7,6},{8,9},{9,8},{10,11... | collective-permute-start | bytes 884744 | tf_op jit(solution)/shard_map/ppermute | solution.py:349
  11.2 1.3 %collective-permute-start.1 = (s16[288,512]{1,0:T(8,128)(2,1)S(1)}, s16[288,512]{1,0:T(8,128)(2,1)S(1)}, u32[]{:S(2)}, u32[]{:S(2)}) collective-permute-start(s16[288,512]{1,0:T(8,128)(2,1)S(1)} %get-tuple-element.19), channel_id=1, source_target_pairs={{1,0},{3,2},{5,4},{7,6},{8,9},{10,11},{12,13},{14,15},{17,16},{19,... | collective-permute-start | bytes 884744 | tf_op jit(solution)/shard_map/ppermute | solution.py:349
  12.5 1.6 %collective-permute-start.2 = (s16[288,512]{1,0:T(8,128)(2,1)S(1)}, s16[288,512]{1,0:T(8,128)(2,1)S(1)}, u32[]{:S(2)}, u32[]{:S(2)}) collective-permute-start(s16[288,512]{1,0:T(8,128)(2,1)S(1)} %get-tuple-element.18), channel_id=1, source_target_pairs={{0,2},{1,3},{2,0},{3,1},{4,6},{5,7},{6,4},{7,5},{8,10},{9,11},{10,... | collective-permute-start | bytes 884744 | tf_op jit(solution)/shard_map/ppermute | solution.py:349
  14.2 4.5 %shard_map.69.k24_ref = f32[2,272,512]{2,1,0:T(8,128)} custom-call(s32[16]{0:T(128)} %stack.51.info_ref, bf16[2048,512]{1,0:T(8,128)(2,1)} %x_ref.5, bf16[8,2048]{1,0:T(8,128)(2,1)} %bitcast.36, s32[1,2048]{1,0:T(1,128)} %bitcast.38), custom_call_target="tpu_custom_call" | custom-call | tf_op jit(solution)/shard_map/pallas_call | solution.py:380
  18.7 2.7 %collective-permute-done.1.p2_ref = s16[288,512]{1,0:T(8,128)(2,1)S(1)} collective-permute-done((s16[288,512]{1,0:T(8,128)(2,1)S(1)}, s16[288,512]{1,0:T(8,128)(2,1)S(1)}, u32[]{:S(2)}, u32[]{:S(2)}) %collective-permute-start.1) | collective-permute-done | bytes 294944 | tf_op jit(solution)/shard_map/ppermute | solution.py:349
  22.4 3.7 %shard_map.70 = (s16[2,288,512]{2,1,0:T(8,128)(2,1)}, f32[2,272,512]{2,1,0:T(8,128)}) custom-call(s32[16]{0:T(128)} %stack.51.info_ref, f32[272,512]{1,0:T(8,128)} %get-tuple-element.8.k1_ref, f32[2,272,512]{2,1,0:T(8,128)} %shard_map.69.k24_ref, s16[288,512]{1,0:T(8,128)(2,1)} %copy-done.2, s16[288,512]{1,0:T(8,128)(2,1)} %copy-done.3, ...), custom_call_target="tpu_custom_call" | custom-call | tf_op jit(solution)/shard_map/pallas_call | solution.py:380
  27.2 3.6 %collective-permute-start.3 = (s16[288,512]{1,0:T(8,128)(2,1)S(1)}, s16[288,512]{1,0:T(8,128)(2,1)S(1)}, u32[]{:S(2)}, u32[]{:S(2)}) collective-permute-start(s16[288,512]{1,0:T(8,128)(2,1)S(1)} %get-tuple-element.22), channel_id=1, source_target_pairs={{0,2},{1,3},{2,0},{4,6},{5,7},{6,4},{9,11},{10,8},{11,9},{13,15},{... | collective-permute-start | bytes 884744 | tf_op jit(solution)/shard_map/ppermute | solution.py:349
  30.9 1.3 %collective-permute-start.4 = (s16[288,512]{1,0:T(8,128)(2,1)S(1)}, s16[288,512]{1,0:T(8,128)(2,1)S(1)}, u32[]{:S(2)}, u32[]{:S(2)}) collective-permute-start(s16[288,512]{1,0:T(8,128)(2,1)S(1)} %get-tuple-element.21), channel_id=1, source_target_pairs={{1,0},{3,2},{5,4},{7,6},{8,9},{10,11},{12,13},{14,15},{17,16},{19,... | collective-permute-start | bytes 884744 | tf_op jit(solution)/shard_map/ppermute | solution.py:349
  32.2 5.2 %collective-permute-done.3.p4_ref = s16[288,512]{1,0:T(8,128)(2,1)S(1)} collective-permute-done((s16[288,512]{1,0:T(8,128)(2,1)S(1)}, s16[288,512]{1,0:T(8,128)(2,1)S(1)}, u32[]{:S(2)}, u32[]{:S(2)}) %collective-permute-start.3) | collective-permute-done | bytes 294944 | tf_op jit(solution)/shard_map/ppermute | solution.py:349
  37.4 2.1 %collective-permute-done.4.p5_ref = s16[288,512]{1,0:T(8,128)(2,1)S(1)} collective-permute-done((s16[288,512]{1,0:T(8,128)(2,1)S(1)}, s16[288,512]{1,0:T(8,128)(2,1)S(1)}, u32[]{:S(2)}, u32[]{:S(2)}) %collective-permute-start.4) | collective-permute-done | bytes 294944 | tf_op jit(solution)/shard_map/ppermute | solution.py:349
  40.2 2.9 %shard_map.71 = (s16[288,512]{1,0:T(8,128)(2,1)}, f32[272,512]{1,0:T(8,128)}) custom-call(s32[16]{0:T(128)} %stack.51.info_ref, f32[2,272,512]{2,1,0:T(8,128)} %get-tuple-element.10.k_ref, s16[288,512]{1,0:T(8,128)(2,1)} %copy-done.5, s16[288,512]{1,0:T(8,128)(2,1)} %copy-done.6), custom_call_target="tpu_custom_call" | custom-call | tf_op jit(solution)/shard_map/pallas_call | solution.py:380
  43.1 4.7 %collective-permute-start.5 = (s16[288,512]{1,0:T(8,128)(2,1)}, s16[288,512]{1,0:T(8,128)(2,1)S(1)}, u32[]{:S(2)}, u32[]{:S(2)}) collective-permute-start(s16[288,512]{1,0:T(8,128)(2,1)} %get-tuple-element.13), channel_id=1, source_target_pairs={{0,4},{2,6},{4,0},{6,2},{7,3},{8,12},{9,13},{11,15},{13,9},{15,11}... | collective-permute-start | bytes 884744 | tf_op jit(solution)/shard_map/ppermute | solution.py:349
  48.3 7.4 %collective-permute-done.5.p_ref = s16[288,512]{1,0:T(8,128)(2,1)S(1)} collective-permute-done((s16[288,512]{1,0:T(8,128)(2,1)}, s16[288,512]{1,0:T(8,128)(2,1)S(1)}, u32[]{:S(2)}, u32[]{:S(2)}) %collective-permute-start.5) | collective-permute-done | bytes 294944 | tf_op jit(solution)/shard_map/ppermute | solution.py:349
  56.4 23.5 %shard_map.72 = bf16[16,512]{1,0:T(8,128)(2,1)} custom-call(f32[2]{0:T(128)} %broadcast_multiply_fusion.shift_ref, f32[272,512]{1,0:T(8,128)} %get-tuple-element.12.k_ref, s16[288,512]{1,0:T(8,128)(2,1)} %copy-done.1), custom_call_target="tpu_custom_call" | custom-call | tf_op jit(solution)/shard_map/pallas_call | solution.py:380
  79.9 1.4 %broadcast_in_dim.2 = bf16[8,16,512]{2,1,0:T(8,128)(2,1)} broadcast(bf16[16,512]{1,0:T(8,128)(2,1)} %shard_map.72), dimensions={1,2} | broadcast | bytes 147456 | tf_op jit(solution)/shard_map/broadcast_in_dim | solution.py:423
  81.3 4.8 %all-to-all-start = ((bf16[8,16,512]{2,1,0:T(8,128)(2,1)}), bf16[8,16,512]{2,1,0:T(8,128)(2,1)S(1)}, u32[]{:S(2)}, u32[]{:S(2)}) async-start(bf16[8,16,512]{2,1,0:T(8,128)(2,1)} %broadcast_in_dim.2), calls=%async_computation | async-start | bytes 262144 | tf_op jit(solution)/shard_map/all_to_all | solution.py:423
  86.0 6.2 %all_gather.7.g_ref = bf16[4,64,512]{2,1,0:T(8,128)(2,1)} all-gather(bf16[1,64,512]{2,1,0:T(8,128)(2,1)S(1)} %bitcast.40), channel_id=1, replica_groups=mesh['blk'=4,'smp'=8] {'blk'}, dimensions={0}, use_global_device_ids=true | all-gather | bytes 327680 | tf_op jit(solution)/shard_map/all_gather | solution.py:435
  94.0 3.1 %shard_map.73.o_ref = bf16[16,2048]{1,0:T(8,128)(2,1)} custom-call(s32[16]{0:T(128)} %stack.51.info_ref, bf16[2048,512]{1,0:T(8,128)(2,1)} %x_ref.5, bf16[8,16,512]{2,1,0:T(8,128)(2,1)} %copy-done, s32[1,2048]{1,0:T(1,128)} %bitcast.39), custom_call_target="tpu_custom_call" | custom-call | tf_op jit(solution)/shard_map/pallas_call | solution.py:380
  97.1 7.3 %all_gather.6.j_ref = bf16[64,2048]{1,0:T(8,128)(2,1)} all-gather(bf16[16,2048]{1,0:T(8,128)(2,1)} %shard_map.73.o_ref), channel_id=1, replica_groups=mesh['blk'=4,'smp'=8] {'blk'}, dimensions={0}, use_global_device_ids=true | all-gather | bytes 327680 | tf_op jit(solution)/shard_map/all_gather | solution.py:436
  104.4 2.1 %shard_map.74 = f32[16,16]{1,0:T(8,128)} custom-call(bf16[16,2048]{1,0:T(8,128)(2,1)} %shard_map.73.o_ref, bf16[64,2048]{1,0:T(8,128)(2,1)} %all_gather.6.j_ref, bf16[4,64,512]{2,1,0:T(8,128)(2,1)} %all_gather.7.g_ref), custom_call_target="tpu_custom_call" | custom-call | tf_op jit(solution)/shard_map/pallas_call | solution.py:380
  106.5 5.2 %all-to-all-start.1 = ((f32[8,2,16]{2,1,0:T(2,128)}), f32[8,2,16]{2,1,0:T(2,128)S(1)}, u32[]{:S(2)}, u32[]{:S(2)}) async-start(f32[8,2,16]{2,1,0:T(2,128)} %bitcast.42), calls=%async_computation.1 | async-start | bytes 16384 | tf_op jit(solution)/shard_map/all_to_all | solution.py:448
  111.7 1.5 %copy.12 = bf16[2,8,2048]{2,0,1:T(2,128)(2,1)} copy(bf16[2,8,2048]{2,1,0:T(8,128)(2,1)} %bitcast.34) | data formatting | bytes 131072 | tf_op jit(solution)/shard_map/reshape | solution.py:451
  113.2 5.0 %all-to-all-done.1 = f32[8,2,16]{2,1,0:T(2,128)S(1)} async-done(((f32[8,2,16]{2,1,0:T(2,128)}), f32[8,2,16]{2,1,0:T(2,128)S(1)}, u32[]{:S(2)}, u32[]{:S(2)}) %all-to-all-start.1) | async-done | bytes 1056 | tf_op jit(solution)/shard_map/all_to_all | solution.py:448
  (28 shorter events, 8.4 us)
Async XLA Ops:
  8.2 10.5 %collective-permute-start = (s16[288,512]{1,0:T(8,128)(2,1)S(1)}, s16[288,512]{1,0:T(8,128)(2,1)S(1)}, u32[]{:S(2)}, u32[]{:S(2)}) collective-permute-start(s16[288,512]{1,0:T(8,128)(2,1)S(1)} %get-tuple-element.20), channel_id=1, source_target_pairs={{0,1},{1,0},{2,3},{3,2},{4,5},{5,4},{6,7},{7,6},{8,9},{9,8},{10,11... | collective-permute-start | bytes 884744 | tf_op jit(solution)/shard_map/ppermute | solution.py:349
  11.2 10.2 %collective-permute-start.1 = (s16[288,512]{1,0:T(8,128)(2,1)S(1)}, s16[288,512]{1,0:T(8,128)(2,1)S(1)}, u32[]{:S(2)}, u32[]{:S(2)}) collective-permute-start(s16[288,512]{1,0:T(8,128)(2,1)S(1)} %get-tuple-element.19), channel_id=1, source_target_pairs={{1,0},{3,2},{5,4},{7,6},{8,9},{10,11},{12,13},{14,15},{17,16},{19,... | collective-permute-start | bytes 884744 | tf_op jit(solution)/shard_map/ppermute | solution.py:349
  12.5 9.2 %collective-permute-start.2 = (s16[288,512]{1,0:T(8,128)(2,1)S(1)}, s16[288,512]{1,0:T(8,128)(2,1)S(1)}, u32[]{:S(2)}, u32[]{:S(2)}) collective-permute-start(s16[288,512]{1,0:T(8,128)(2,1)S(1)} %get-tuple-element.18), channel_id=1, source_target_pairs={{0,2},{1,3},{2,0},{3,1},{4,6},{5,7},{6,4},{7,5},{8,10},{9,11},{10,... | collective-permute-start | bytes 884744 | tf_op jit(solution)/shard_map/ppermute | solution.py:349
  18.7 3.1 %copy-start.2 = (s16[288,512]{1,0:T(8,128)(2,1)}, s16[288,512]{1,0:T(8,128)(2,1)S(1)}, u32[]{:S(2)}) copy-start(s16[288,512]{1,0:T(8,128)(2,1)S(1)} %collective-permute-done.p1_ref) | copy-start | bytes 884740
  21.4 0.7 copy-start.3
  21.7 0.7 copy-start.4
  27.2 20.5 %copy-start.8 = (f32[2]{0:T(128)S(1)}, f32[2]{0:T(128)}, u32[]{:S(2)}) copy-start(f32[2]{0:T(128)} %param.8) | copy-start | bytes 28
  27.2 10.2 %collective-permute-start.3 = (s16[288,512]{1,0:T(8,128)(2,1)S(1)}, s16[288,512]{1,0:T(8,128)(2,1)S(1)}, u32[]{:S(2)}, u32[]{:S(2)}) collective-permute-start(s16[288,512]{1,0:T(8,128)(2,1)S(1)} %get-tuple-element.22), channel_id=1, source_target_pairs={{0,2},{1,3},{2,0},{4,6},{5,7},{6,4},{9,11},{10,8},{11,9},{13,15},{... | collective-permute-start | bytes 884744 | tf_op jit(solution)/shard_map/ppermute | solution.py:349
  30.9 8.6 %collective-permute-start.4 = (s16[288,512]{1,0:T(8,128)(2,1)S(1)}, s16[288,512]{1,0:T(8,128)(2,1)S(1)}, u32[]{:S(2)}, u32[]{:S(2)}) collective-permute-start(s16[288,512]{1,0:T(8,128)(2,1)S(1)} %get-tuple-element.21), channel_id=1, source_target_pairs={{1,0},{3,2},{5,4},{7,6},{8,9},{10,11},{12,13},{14,15},{17,16},{19,... | collective-permute-start | bytes 884744 | tf_op jit(solution)/shard_map/ppermute | solution.py:349
  37.4 2.1 %copy-start.5 = (s16[288,512]{1,0:T(8,128)(2,1)}, s16[288,512]{1,0:T(8,128)(2,1)S(1)}, u32[]{:S(2)}) copy-start(s16[288,512]{1,0:T(8,128)(2,1)S(1)} %collective-permute-done.3.p4_ref) | copy-start | bytes 884740
  39.5 0.7 copy-start.6
  40.2 45.8 %copy-start.7 = (bf16[1,512,8,8]{1,3,2,0:T(8,128)(2,1)S(1)}, bf16[1,512,8,8]{1,3,2,0:T(8,128)(2,1)}, u32[]{:S(2)}) copy-start(bf16[1,512,8,8]{1,3,2,0:T(8,128)(2,1)} %param.9) | copy-start | bytes 196612
  43.1 12.6 %collective-permute-start.5 = (s16[288,512]{1,0:T(8,128)(2,1)}, s16[288,512]{1,0:T(8,128)(2,1)S(1)}, u32[]{:S(2)}, u32[]{:S(2)}) collective-permute-start(s16[288,512]{1,0:T(8,128)(2,1)} %get-tuple-element.13), channel_id=1, source_target_pairs={{0,4},{2,6},{4,0},{6,2},{7,3},{8,12},{9,13},{11,15},{13,9},{15,11}... | collective-permute-start | bytes 884744 | tf_op jit(solution)/shard_map/ppermute | solution.py:349
  55.7 0.7 copy-start.1
  81.3 12.1 %all-to-all-start = ((bf16[8,16,512]{2,1,0:T(8,128)(2,1)}), bf16[8,16,512]{2,1,0:T(8,128)(2,1)S(1)}, u32[]{:S(2)}, u32[]{:S(2)}) async-start(bf16[8,16,512]{2,1,0:T(8,128)(2,1)} %broadcast_in_dim.2), calls=%async_computation | async-start | bytes 262144 | tf_op jit(solution)/shard_map/all_to_all | solution.py:423
  93.4 0.6 copy-start
  106.5 11.8 %all-to-all-start.1 = ((f32[8,2,16]{2,1,0:T(2,128)}), f32[8,2,16]{2,1,0:T(2,128)S(1)}, u32[]{:S(2)}, u32[]{:S(2)}) async-start(f32[8,2,16]{2,1,0:T(2,128)} %bitcast.42), calls=%async_computation.1 | async-start | bytes 16384 | tf_op jit(solution)/shard_map/all_to_all | solution.py:448

commit v2 on v1

--- a/solution.py
+++ b/solution.py
@@ -26,10 +26,6 @@
 VMEM = pl.BlockSpec(memory_space=pltpu.VMEM)
 SMEM = pl.BlockSpec(memory_space=pltpu.SMEM)
 PARAMS = pltpu.CompilerParams(vmem_limit_bytes=60 * 1024 * 1024)
-
-
-def mm(a, b, precision=lax.Precision.HIGHEST):
-    return lax.dot_general(a, b, (((1,), (0,)), ((), ())), precision=precision, preferred_element_type=f32)
 
 
 def nt(a, b, precision=None):
@@ -158,36 +154,38 @@
     xt_ref[BLOCK : BLOCK + 16, :] = jnp.concatenate([yt_ref[...], jnp.zeros_like(yt_ref[...])], axis=0)
 
 
-def gram_send_kernel(info_ref, x_ref, yt_ref, f_ref, msg_ref, keep_ref, xt_ref, work_ref, *, bound):
+def gram_send_kernel(info_ref, x_ref, yt_ref, f_ref, m0_ref, m1_ref, m3_ref, keep_ref, xt_ref, work_ref, *, bound):
     eye, low = square_masks()
     load_transposed(x_ref, yt_ref, xt_ref)
-    for slot, dst in ((0, work_ref), (1, keep_ref), (3, work_ref)):
+    for slot, dst, msg_ref in ((0, work_ref, m0_ref), (1, keep_ref, m1_ref), (3, work_ref, m3_ref)):
         gram_one(info_ref[slot], x_ref, xt_ref, f_ref, dst, eye, low)
-        encode(reader(dst), msg_ref.at[{0: 0, 1: 1, 3: 2}[slot]], bound, eye, low)
-
-
-def gram_keep_kernel(info_ref, x_ref, yt_ref, f_ref, keep_ref, xt_ref):
+        encode(reader(dst), msg_ref, bound, eye, low)
+
+
+def gram_keep_kernel(info_ref, x_ref, yt_ref, f_ref, k2_ref, k4_ref, xt_ref):
     eye, low = square_masks()
     load_transposed(x_ref, yt_ref, xt_ref)
-    for n, slot in enumerate((2, 4)):
-        gram_one(info_ref[slot], x_ref, xt_ref, f_ref, keep_ref.at[n], eye, low)
-
-
-def second_kernel(info_ref, k1_ref, k24_ref, p1_ref, p2_ref, p3_ref, msg_ref, keep_ref, s1_ref, s2_ref, *, bound):
+    for slot, dst in ((2, k2_ref), (4, k4_ref)):
+        gram_one(info_ref[slot], x_ref, xt_ref, f_ref, dst, eye, low)
+
+
+def second_kernel(
+    info_ref, k1_ref, k2_ref, k4_ref, p1_ref, p2_ref, p3_ref, ma_ref, mb_ref, ka_ref, kb_ref, s1_ref, s2_ref, *, bound
+):
     eye, low = square_masks()
-    add_message(s2_ref, k24_ref.at[0], p1_ref, bound, eye, low)
+    add_message(s2_ref, k2_ref, p1_ref, bound, eye, low)
     add_message(s1_ref, k1_ref, p2_ref, bound, eye, low)
-    add_message(keep_ref.at[1], k24_ref.at[1], p3_ref, bound, eye, low)
+    add_message(kb_ref, k4_ref, p3_ref, bound, eye, low)
     first = info_ref[5] == 1
-    encode(lambda r, c: jnp.where(first, s1_ref[r, c], s2_ref[r, c]), msg_ref.at[0], bound, eye, low)
-    encode(reader(keep_ref.at[1]), msg_ref.at[1], bound, eye, low)
-    keep_ref[0] = jnp.where(first, s2_ref[...], s1_ref[...])
-
-
-def third_kernel(info_ref, k_ref, p4_ref, p5_ref, msg_ref, keep_ref, sa_ref, sb_ref, *, bound):
+    encode(lambda r, c: jnp.where(first, s1_ref[r, c], s2_ref[r, c]), ma_ref, bound, eye, low)
+    encode(reader(kb_ref), mb_ref, bound, eye, low)
+    ka_ref[...] = jnp.where(first, s2_ref[...], s1_ref[...])
+
+
+def third_kernel(info_ref, ka_ref, kb_ref, p4_ref, p5_ref, msg_ref, keep_ref, sa_ref, sb_ref, *, bound):
     eye, low = square_masks()
-    add_message(sa_ref, k_ref.at[0], p4_ref, bound, eye, low)
-    add_message(sb_ref, k_ref.at[1], p5_ref, bound, eye, low)
+    add_message(sa_ref, ka_ref, p4_ref, bound, eye, low)
+    add_message(sb_ref, kb_ref, p5_ref, bound, eye, low)
     upper = info_ref[6] == 1
     encode(lambda r, c: jnp.where(upper, sa_ref[r, c], sb_ref[r, c]), msg_ref, bound, eye, low)
     keep_ref[...] = jnp.where(upper, sb_ref[...], sa_ref[...])
@@ -209,7 +207,6 @@
     col = lane % HALF
     half = lane - col
     here = [sub == p for p in range(TILE)]
-    tiles = list(tiles)
     count = len(tiles)
     for g in range(count):
         inside = (col >= g * TILE) & (col < (g + 1) * TILE)
@@ -238,12 +235,109 @@
             t = tiles[i]
             tiles[i] = jnp.where(inside, 0.0, t) - tree([spread(t, p) * rows[p] for p in range(TILE)])
         tiles[g] = r
-    return tiles
+        yield
 
 
 def block_diagonal(t):
     left = iota(t.shape, 1) < HALF
-    return jnp.concatenate([jnp.where(left, t, 0.0), jnp.where(left, 0.0, t)], axis=0)
+    zero = jnp.zeros_like(t)
+    return jnp.concatenate([jnp.where(left, t, zero), jnp.where(left, zero, t)], axis=0)
+
+
+def parts(x):
+    high = x.astype(bf16)
+    return high, (x - high.astype(f32)).astype(bf16)
+
+
+def left4(p):
+    return jnp.concatenate(p, axis=1)
+
+
+def rows4(p):
+    return jnp.concatenate([jnp.concatenate([q, q], axis=1) for q in p], axis=0)
+
+
+def cols4(p):
+    return jnp.concatenate([jnp.concatenate([q, q], axis=0) for q in p], axis=1)
+
+
+def fold_halves(r):
+    half = r.shape[1] // 2
+    return r[:, :half] + r[:, half:]
+
+
+def mm4(a, b):
+    return fold_halves(lax.dot_general(a, b, (((1,), (0,)), ((), ())), preferred_element_type=f32))
+
+
+def nt4(a, b):
+    return fold_halves(nt(a, b))
+
+
+def factor_solve(n, shift, m_ref, w_ref, x_ref):
+    blocks, groups = n // HALF, HALF // TILE
+
+    def begin(b):
+        top = m_ref[b * HALF : (b + 1) * HALF, b * LANES : (b + 1) * LANES] + shift
+        tiles = [top[i * TILE : (i + 1) * TILE] for i in range(groups)]
+        return tiles, invert_pair(tiles)
+
+    def run(steps, work):
+        done = 0
+        for g in range(groups):
+            next(steps)
+            todo = len(work) * (g + 1) // groups
+            for k in range(done, todo):
+                work[k]()
+            done = todo
+        for _ in steps:
+            pass
+
+    tiles, steps = begin(0)
+    run(steps, [])
+    for b in range(blocks):
+        cs, nx = slice(b * LANES, (b + 1) * LANES), (b + 1) * HALF
+        inverse = cols4(parts(block_diagonal(jnp.concatenate(tiles, axis=0))))
+        panel = parts(m_ref[nx:, cs])
+        left = left4(panel)
+        first = HALF if nx < n else 8
+        w0 = mm4(left[:first], inverse)
+        w_ref[nx : nx + first, cs] = w0
+        if nx >= n:
+            break
+
+        def right(j):
+            lo = (j - b - 1) * HALF
+            return rows4([block_diagonal(p[lo : lo + HALF]) for p in panel])
+
+        js = slice((b + 1) * LANES, (b + 2) * LANES)
+        m_ref[nx : nx + HALF, js] = m_ref[nx : nx + HALF, js] - nt4(left4(parts(w0)), right(b + 1))
+        tiles, steps = begin(b + 1)
+        kept = {}
+
+        def rest():
+            w = mm4(left[HALF:], inverse)
+            w_ref[nx + HALF :, cs] = w
+            kept["w"] = left4(parts(w))
+
+        def trail(j):
+            def go():
+                jc, r0 = slice(j * LANES, (j + 1) * LANES), max(j * HALF, nx + HALF)
+                m_ref[r0:, jc] = m_ref[r0:, jc] - nt4(kept["w"][r0 - nx - HALF :], right(j))
+
+            return go
+
+        run(steps, [rest] + [trail(j) for j in range(b + 1, blocks)])
+    for b in reversed(range(blocks)):
+        cs = slice(b * LANES, (b + 1) * LANES)
+        x = w_ref[n:, cs]
+        if b + 1 < blocks:
+            below = [
+                jnp.concatenate([block_diagonal(p[i * HALF : (i + 1) * HALF]) for i in range(blocks - b - 1)], axis=0)
+                for p in parts(w_ref[(b + 1) * HALF : n, cs])
+            ]
+            x = x - mm4(left4(parts(x_ref[:, (b + 1) * LANES :])), cols4(below))
+        x_ref[:, cs] = x
 
 
 def solve_kernel(shift_ref, k_ref, p_ref, o_ref, m_ref, w_ref, x_ref, *, bound):
@@ -263,38 +357,19 @@
         for c in range(4):
             i, j = LAYOUT[r][c]
             t = k_ref[place(r, c)] + matrix(r, c)
-            u = t.T
             if (r, c) in ((0, 0), (0, 2)):
+                u = t.T
                 put(place(i, 0)[0], jnp.where(eye, diag[i], jnp.where(low, t, u)), i)
                 put(place(j, 0)[0], jnp.where(eye, diag[j], jnp.where(low, u, t)), j)
             else:
                 put(place(i, 0)[0], t, j)
-                put(place(j, 0)[0], u, i)
     right = k_ref[256:264, :] + xy
     for c in range(4):
         put(slice(n, n + 8), right[:, c * LANES : (c + 1) * LANES], c)
 
     lane, sub = iota((HALF, LANES), 1), iota((HALF, LANES), 0)
     shift = jnp.where(lane % HALF == sub, jnp.where(lane < HALF, shift_ref[0], shift_ref[1]), 0.0)
-    blocks = n // HALF
-    for b in range(blocks):
-        rs, cs = slice(b * HALF, (b + 1) * HALF), slice(b * LANES, (b + 1) * LANES)
-        top = m_ref[rs, cs] + shift
-        tiles = invert_pair([top[i * TILE : (i + 1) * TILE] for i in range(HALF // TILE)])
-        inverse = block_diagonal(jnp.concatenate(tiles, axis=0))
-        nx = (b + 1) * HALF
-        w = mm(m_ref[nx:, cs], inverse)
-        w_ref[nx:, cs] = w
-        for j in range(b + 1, blocks):
-            js = slice(j * LANES, (j + 1) * LANES)
-            m_ref[nx:, js] = m_ref[nx:, js] - mm(w, block_diagonal(m_ref[rs, js]))
-    for b in reversed(range(blocks)):
-        cs = slice(b * LANES, (b + 1) * LANES)
-        x = w_ref[n:, cs]
-        if b + 1 < blocks:
-            below = [block_diagonal(w_ref[i * HALF : (i + 1) * HALF, cs]) for i in range(b + 1, blocks)]
-            x = x - mm(x_ref[:, (b + 1) * LANES :], jnp.concatenate(below, axis=0))
-        x_ref[:, cs] = x
+    factor_solve(n, shift, m_ref, w_ref, x_ref)
     left = iota((8, LANES), 1) < HALF
     for c in range(4):
         even, odd = x_ref[:, 2 * c * LANES : (2 * c + 1) * LANES], x_ref[:, (2 * c + 1) * LANES : (2 * c + 2) * LANES]
@@ -394,20 +469,39 @@
 
         xt = pltpu.VMEM((BLOCK + 16, rows), bf16)
         work = pltpu.VMEM((PACKED, BLOCK), f32)
-        msg, k1 = call(
-            gram_send_kernel, (wire(3), packed()), [SMEM, VMEM, VMEM, VMEM], [xt, work], info, x, yt, f_row, bound=bound
-        )
-        p1 = move(msg[0], 1, lambda u, v, w: True)
-        p2 = move(msg[1], 1, lambda u, v, w: u == 1)
-        p3 = move(msg[2], 2, lambda u, v, w: True)
-        k24 = call(gram_keep_kernel, packed(2), [SMEM, VMEM, VMEM, VMEM], [xt], info, x, yt, f_row)
+        m0, m1, m3, k1 = call(
+            gram_send_kernel,
+            (wire(), wire(), wire(), packed()),
+            [SMEM, VMEM, VMEM, VMEM],
+            [xt, work],
+            info,
+            x,
+            yt,
+            f_row,
+            bound=bound,
+        )
+        p1 = move(m0, 1, lambda u, v, w: True)
+        p2 = move(m1, 1, lambda u, v, w: u == 1)
+        p3 = move(m3, 2, lambda u, v, w: True)
+        k2, k4 = call(gram_keep_kernel, (packed(), packed()), [SMEM, VMEM, VMEM, VMEM], [xt], info, x, yt, f_row)
+        ma, mb, ka, kb = call(
+            second_kernel,
+            (wire(), wire(), packed(), packed()),
+            [SMEM] + [VMEM] * 6,
+            [work, work],
+            info,
+            k1,
+            k2,
+            k4,
+            p1,
+            p2,
+            p3,
+            bound=bound,
+        )
+        p4 = move(ma, 2, lambda u, v, w: (u, v) != (1, 1))
+        p5 = move(mb, 1, lambda u, v, w: u == 1)
         msg, keep = call(
-            second_kernel, (wire(2), packed(2)), [SMEM] + [VMEM] * 5, [work, work], info, k1, k24, p1, p2, p3, bound=bound
-        )
-        p4 = move(msg[0], 2, lambda u, v, w: (u, v) != (1, 1))
-        p5 = move(msg[1], 1, lambda u, v, w: u == 1)
-        msg, keep = call(
-            third_kernel, (wire(), packed()), [SMEM] + [VMEM] * 3, [work, work], info, keep, p4, p5, bound=bound
+            third_kernel, (wire(), packed()), [SMEM] + [VMEM] * 4, [work, work], info, ka, kb, p4, p5, bound=bound
         )
         p6 = move(msg, 4, lambda u, v, w: u == 0 or (u, v, w) == (1, 1, 1))
         beta = call(

time: 120 us -> 112 us (0.933)
  Pallas kernels: 45.4 us -> 39.6 us
  local copies, waits for them, and re-layouts: 9.27 us -> 7.05 us
    pallas_call x7, Pallas kernels: 45.4 us -> 39.6 us  [call(): pl.pallas_call(functools.partial(kernel, **static), out_shape=outs, in_sp...]
    squeeze x2 -> x0, local copies, waits for them, and re-layouts: 2.29 us -> none  [the longest x1 1.2 us: local(): p3 = move(msg[2], 2, lambda u, v, w: True)]
  transfers between devices with their start and end apart: 8 -> 8, of which waited for: 7 -> 8; matrix products, arithmetic and copies ran while one was open for 2% -> 2% of each run, Pallas kernels for 4% -> 4%
where the time goes in v2:
time: 112 us
  Pallas kernels  39.6 us (35%)
  starting transfers between devices  25.8 us (23%)
  waiting for transfers between devices  24.4 us (22%)
  blocking collectives  13.6 us (12%)
  local copies, waits for them, and re-layouts  7.05 us (6%)
    pallas_call x7, Pallas kernels, call(): pl.pallas_call(functools.partial(kernel, **static), out_shape=outs, in_sp...  39.6 us
    ppermute x6, waiting for transfers between devices, move(): return lax.ppermute(x, ('blk', 'smp'), pairs(bit, sends))  18.4 us
    ppermute x6, starting transfers between devices, move(): return lax.ppermute(x, ('blk', 'smp'), pairs(bit, sends))  15.7 us
    all_gather x1, blocking collectives, local(): oof_all = lax.all_gather(oof, 'blk', axis=0, tiled=True)  7.34 us
    all_gather x1, blocking collectives, local(): prior_all = lax.all_gather(prior, 'blk', axis=0)  6.23 us
    all_to_all x1, starting transfers between devices, local(): lax.all_to_all(part.reshape(n_smp, n_cross // n_smp, 16), 'smp', 0, 0)  5.24 us
    all_to_all x1, waiting for transfers between devices, local(): lax.all_to_all(part.reshape(n_smp, n_cross // n_smp, 16), 'smp', 0, 0)  4.98 us
    all_to_all x1, starting transfers between devices, local(): lax.all_to_all(jnp.broadcast_to(beta[None], (n_smp, 16, BLOCK)), 'smp', 0...  4.91 us
  transfers between devices with their start and end apart: 8, of which 8 were waited for; matrix products, arithmetic and copies ran while one was open for 2% of the time, Pallas kernels for 4%

profile of v2, /device:TPU:0, one launch (start us, length us, event | category | flops | bytes accessed | tf_op | source)
XLA Modules:
  0.0 111.7 jit_solution(14087428155465511400)
XLA Ops:
  1.3 5.7 %shard_map.68 = (s16[288,512]{1,0:T(8,128)(2,1)}, s16[288,512]{1,0:T(8,128)(2,1)}, s16[288,512]{1,0:T(8,128)(2,1)}, f32[272,512]{1,0:T(8,128)}) custom-call(s32[16]{0:T(128)} %stack.51.info_ref, bf16[2048,512]{1,0:T(8,128)(2,1)} %x_ref.5, bf16[8,2048]{1,0:T(8,128)(2,1)} %bitcast.25, s32[1,2048]{1,0:T(1,128)} %bitcast.27), custom_call_target="tpu_custom_call" | custom-call | tf_op jit(solution)/shard_map/pallas_call | solution.py:455
  7.0 3.0 %collective-permute-start = (s16[288,512]{1,0:T(8,128)(2,1)}, s16[288,512]{1,0:T(8,128)(2,1)S(1)}, u32[]{:S(2)}, u32[]{:S(2)}) collective-permute-start(s16[288,512]{1,0:T(8,128)(2,1)} %get-tuple-element.17), channel_id=1, source_target_pairs={{0,1},{1,0},{2,3},{3,2},{4,5},{5,4},{6,7},{7,6},{8,9},{9,8},{10,11... | collective-permute-start | bytes 884744 | tf_op jit(solution)/shard_map/ppermute | solution.py:424
  10.0 1.3 %collective-permute-start.1 = (s16[288,512]{1,0:T(8,128)(2,1)}, s16[288,512]{1,0:T(8,128)(2,1)S(1)}, u32[]{:S(2)}, u32[]{:S(2)}) collective-permute-start(s16[288,512]{1,0:T(8,128)(2,1)} %get-tuple-element.18), channel_id=1, source_target_pairs={{1,0},{3,2},{5,4},{7,6},{8,9},{10,11},{12,13},{14,15},{17,16},{19,... | collective-permute-start | bytes 884744 | tf_op jit(solution)/shard_map/ppermute | solution.py:424
  11.3 1.6 %collective-permute-start.2 = (s16[288,512]{1,0:T(8,128)(2,1)}, s16[288,512]{1,0:T(8,128)(2,1)S(1)}, u32[]{:S(2)}, u32[]{:S(2)}) collective-permute-start(s16[288,512]{1,0:T(8,128)(2,1)} %get-tuple-element.19), channel_id=1, source_target_pairs={{0,2},{1,3},{2,0},{3,1},{4,6},{5,7},{6,4},{7,5},{8,10},{9,11},{10,... | collective-permute-start | bytes 884744 | tf_op jit(solution)/shard_map/ppermute | solution.py:424
  12.9 4.4 %shard_map.69 = (f32[272,512]{1,0:T(8,128)}, f32[272,512]{1,0:T(8,128)}) custom-call(s32[16]{0:T(128)} %stack.51.info_ref, bf16[2048,512]{1,0:T(8,128)(2,1)} %x_ref.5, bf16[8,2048]{1,0:T(8,128)(2,1)} %bitcast.26, s32[1,2048]{1,0:T(1,128)} %bitcast.28), custom_call_target="tpu_custom_call" | custom-call | tf_op jit(solution)/shard_map/pallas_call | solution.py:455
  17.7 2.7 %collective-permute-done.1.p2_ref = s16[288,512]{1,0:T(8,128)(2,1)S(1)} collective-permute-done((s16[288,512]{1,0:T(8,128)(2,1)}, s16[288,512]{1,0:T(8,128)(2,1)S(1)}, u32[]{:S(2)}, u32[]{:S(2)}) %collective-permute-start.1) | collective-permute-done | bytes 294944 | tf_op jit(solution)/shard_map/ppermute | solution.py:424
  21.4 3.7 %shard_map.70 = (s16[288,512]{1,0:T(8,128)(2,1)}, s16[288,512]{1,0:T(8,128)(2,1)}, f32[272,512]{1,0:T(8,128)}, f32[272,512]{1,0:T(8,128)}) custom-call(s32[16]{0:T(128)} %stack.51.info_ref, f32[272,512]{1,0:T(8,128)} %get-tuple-element.14.k1_ref, f32[272,512]{1,0:T(8,128)} %get-tuple-element.15.k2_ref, f32[272,512]{1,0:T(8,128)} %get-tuple-element.16.k4_ref, ...), custom_call_target="tpu_custom_call" | custom-call | tf_op jit(solution)/shard_map/pallas_call | solution.py:455
  25.1 3.8 %collective-permute-start.3 = (s16[288,512]{1,0:T(8,128)(2,1)}, s16[288,512]{1,0:T(8,128)(2,1)S(1)}, u32[]{:S(2)}, u32[]{:S(2)}) collective-permute-start(s16[288,512]{1,0:T(8,128)(2,1)} %get-tuple-element.22), channel_id=1, source_target_pairs={{0,2},{1,3},{2,0},{4,6},{5,7},{6,4},{9,11},{10,8},{11,9},{13,15},{... | collective-permute-start | bytes 884744 | tf_op jit(solution)/shard_map/ppermute | solution.py:424
  28.9 1.3 %collective-permute-start.4 = (s16[288,512]{1,0:T(8,128)(2,1)}, s16[288,512]{1,0:T(8,128)(2,1)S(1)}, u32[]{:S(2)}, u32[]{:S(2)}) collective-permute-start(s16[288,512]{1,0:T(8,128)(2,1)} %get-tuple-element.23), channel_id=1, source_target_pairs={{1,0},{3,2},{5,4},{7,6},{8,9},{10,11},{12,13},{14,15},{17,16},{19,... | collective-permute-start | bytes 884744 | tf_op jit(solution)/shard_map/ppermute | solution.py:424
  30.2 5.4 %collective-permute-done.3.p4_ref = s16[288,512]{1,0:T(8,128)(2,1)S(1)} collective-permute-done((s16[288,512]{1,0:T(8,128)(2,1)}, s16[288,512]{1,0:T(8,128)(2,1)S(1)}, u32[]{:S(2)}, u32[]{:S(2)}) %collective-permute-start.3) | collective-permute-done | bytes 294944 | tf_op jit(solution)/shard_map/ppermute | solution.py:424
  35.6 2.1 %collective-permute-done.4.p5_ref = s16[288,512]{1,0:T(8,128)(2,1)S(1)} collective-permute-done((s16[288,512]{1,0:T(8,128)(2,1)}, s16[288,512]{1,0:T(8,128)(2,1)S(1)}, u32[]{:S(2)}, u32[]{:S(2)}) %collective-permute-start.4) | collective-permute-done | bytes 294944 | tf_op jit(solution)/shard_map/ppermute | solution.py:424
  38.4 2.8 %shard_map.71 = (s16[288,512]{1,0:T(8,128)(2,1)}, f32[272,512]{1,0:T(8,128)}) custom-call(s32[16]{0:T(128)} %stack.51.info_ref, f32[272,512]{1,0:T(8,128)} %get-tuple-element.20.ka_ref, f32[272,512]{1,0:T(8,128)} %get-tuple-element.21.kb_ref, s16[288,512]{1,0:T(8,128)(2,1)} %copy-done.5, s16[288,512]{1,0:T(8,128)(2,1)} %copy-done.6), custom_call_target="tpu_custom_call" | custom-call | tf_op jit(solution)/shard_map/pallas_call | solution.py:455
  41.3 4.7 %collective-permute-start.5 = (s16[288,512]{1,0:T(8,128)(2,1)}, s16[288,512]{1,0:T(8,128)(2,1)S(1)}, u32[]{:S(2)}, u32[]{:S(2)}) collective-permute-start(s16[288,512]{1,0:T(8,128)(2,1)} %get-tuple-element.25), channel_id=1, source_target_pairs={{0,4},{2,6},{4,0},{6,2},{7,3},{8,12},{9,13},{11,15},{13,9},{15,11}... | collective-permute-start | bytes 884744 | tf_op jit(solution)/shard_map/ppermute | solution.py:424
  46.5 7.4 %collective-permute-done.5.p_ref = s16[288,512]{1,0:T(8,128)(2,1)S(1)} collective-permute-done((s16[288,512]{1,0:T(8,128)(2,1)}, s16[288,512]{1,0:T(8,128)(2,1)S(1)}, u32[]{:S(2)}, u32[]{:S(2)}) %collective-permute-start.5) | collective-permute-done | bytes 294944 | tf_op jit(solution)/shard_map/ppermute | solution.py:424
  54.6 18.0 %shard_map.72 = bf16[16,512]{1,0:T(8,128)(2,1)} custom-call(f32[2]{0:T(128)} %broadcast_multiply_fusion.shift_ref, f32[272,512]{1,0:T(8,128)} %get-tuple-element.24.k_ref, s16[288,512]{1,0:T(8,128)(2,1)} %copy-done.1), custom_call_target="tpu_custom_call" | custom-call | tf_op jit(solution)/shard_map/pallas_call | solution.py:455
  72.5 1.4 %broadcast_in_dim.2 = bf16[8,16,512]{2,1,0:T(8,128)(2,1)} broadcast(bf16[16,512]{1,0:T(8,128)(2,1)} %shard_map.72), dimensions={1,2} | broadcast | bytes 147456 | tf_op jit(solution)/shard_map/broadcast_in_dim | solution.py:517
  73.9 4.9 %all-to-all-start = ((bf16[8,16,512]{2,1,0:T(8,128)(2,1)}), bf16[8,16,512]{2,1,0:T(8,128)(2,1)S(1)}, u32[]{:S(2)}, u32[]{:S(2)}) async-start(bf16[8,16,512]{2,1,0:T(8,128)(2,1)} %broadcast_in_dim.2), calls=%async_computation | async-start | bytes 262144 | tf_op jit(solution)/shard_map/all_to_all | solution.py:517
  78.8 6.2 %all_gather.7.g_ref = bf16[4,64,512]{2,1,0:T(8,128)(2,1)} all-gather(bf16[1,64,512]{2,1,0:T(8,128)(2,1)S(1)} %bitcast.30), channel_id=1, replica_groups=mesh['blk'=4,'smp'=8] {'blk'}, dimensions={0}, use_global_device_ids=true | all-gather | bytes 327680 | tf_op jit(solution)/shard_map/all_gather | solution.py:529
  86.8 3.1 %shard_map.73.o_ref = bf16[16,2048]{1,0:T(8,128)(2,1)} custom-call(s32[16]{0:T(128)} %stack.51.info_ref, bf16[2048,512]{1,0:T(8,128)(2,1)} %x_ref.5, bf16[8,16,512]{2,1,0:T(8,128)(2,1)} %copy-done, s32[1,2048]{1,0:T(1,128)} %bitcast.29), custom_call_target="tpu_custom_call" | custom-call | tf_op jit(solution)/shard_map/pallas_call | solution.py:455
  89.9 7.3 %all_gather.6.j_ref = bf16[64,2048]{1,0:T(8,128)(2,1)} all-gather(bf16[16,2048]{1,0:T(8,128)(2,1)} %shard_map.73.o_ref), channel_id=1, replica_groups=mesh['blk'=4,'smp'=8] {'blk'}, dimensions={0}, use_global_device_ids=true | all-gather | bytes 327680 | tf_op jit(solution)/shard_map/all_gather | solution.py:530
  97.2 2.1 %shard_map.74 = f32[16,16]{1,0:T(8,128)} custom-call(bf16[16,2048]{1,0:T(8,128)(2,1)} %shard_map.73.o_ref, bf16[64,2048]{1,0:T(8,128)(2,1)} %all_gather.6.j_ref, bf16[4,64,512]{2,1,0:T(8,128)(2,1)} %all_gather.7.g_ref), custom_call_target="tpu_custom_call" | custom-call | tf_op jit(solution)/shard_map/pallas_call | solution.py:455
  99.3 5.2 %all-to-all-start.1 = ((f32[8,2,16]{2,1,0:T(2,128)}), f32[8,2,16]{2,1,0:T(2,128)S(1)}, u32[]{:S(2)}, u32[]{:S(2)}) async-start(f32[8,2,16]{2,1,0:T(2,128)} %bitcast.32), calls=%async_computation.1 | async-start | bytes 16384 | tf_op jit(solution)/shard_map/all_to_all | solution.py:542
  104.5 1.5 %copy.12 = bf16[2,8,2048]{2,0,1:T(2,128)(2,1)} copy(bf16[2,8,2048]{2,1,0:T(8,128)(2,1)} %bitcast.24) | data formatting | bytes 131072 | tf_op jit(solution)/shard_map/reshape | solution.py:545
  106.1 5.0 %all-to-all-done.1 = f32[8,2,16]{2,1,0:T(2,128)S(1)} async-done(((f32[8,2,16]{2,1,0:T(2,128)}), f32[8,2,16]{2,1,0:T(2,128)S(1)}, u32[]{:S(2)}, u32[]{:S(2)}) %all-to-all-start.1) | async-done | bytes 1056 | tf_op jit(solution)/shard_map/all_to_all | solution.py:542
  (26 shorter events, 6.5 us)
Async XLA Ops:
  7.0 10.7 %collective-permute-start = (s16[288,512]{1,0:T(8,128)(2,1)}, s16[288,512]{1,0:T(8,128)(2,1)S(1)}, u32[]{:S(2)}, u32[]{:S(2)}) collective-permute-start(s16[288,512]{1,0:T(8,128)(2,1)} %get-tuple-element.17), channel_id=1, source_target_pairs={{0,1},{1,0},{2,3},{3,2},{4,5},{5,4},{6,7},{7,6},{8,9},{9,8},{10,11... | collective-permute-start | bytes 884744 | tf_op jit(solution)/shard_map/ppermute | solution.py:424
  10.0 10.4 %collective-permute-start.1 = (s16[288,512]{1,0:T(8,128)(2,1)}, s16[288,512]{1,0:T(8,128)(2,1)S(1)}, u32[]{:S(2)}, u32[]{:S(2)}) collective-permute-start(s16[288,512]{1,0:T(8,128)(2,1)} %get-tuple-element.18), channel_id=1, source_target_pairs={{1,0},{3,2},{5,4},{7,6},{8,9},{10,11},{12,13},{14,15},{17,16},{19,... | collective-permute-start | bytes 884744 | tf_op jit(solution)/shard_map/ppermute | solution.py:424
  11.3 9.4 %collective-permute-start.2 = (s16[288,512]{1,0:T(8,128)(2,1)}, s16[288,512]{1,0:T(8,128)(2,1)S(1)}, u32[]{:S(2)}, u32[]{:S(2)}) collective-permute-start(s16[288,512]{1,0:T(8,128)(2,1)} %get-tuple-element.19), channel_id=1, source_target_pairs={{0,2},{1,3},{2,0},{3,1},{4,6},{5,7},{6,4},{7,5},{8,10},{9,11},{10,... | collective-permute-start | bytes 884744 | tf_op jit(solution)/shard_map/ppermute | solution.py:424
  17.7 3.0 %copy-start.2 = (s16[288,512]{1,0:T(8,128)(2,1)}, s16[288,512]{1,0:T(8,128)(2,1)S(1)}, u32[]{:S(2)}) copy-start(s16[288,512]{1,0:T(8,128)(2,1)S(1)} %collective-permute-done.p1_ref) | copy-start | bytes 884740
  20.4 0.7 copy-start.3
  20.7 0.7 copy-start.4
  21.4 24.5 %copy-start.8 = (f32[2]{0:T(128)S(1)}, f32[2]{0:T(128)}, u32[]{:S(2)}) copy-start(f32[2]{0:T(128)} %param.8) | copy-start | bytes 28
  25.1 53.7 %copy-start.7 = (bf16[1,512,8,8]{1,3,2,0:T(8,128)(2,1)S(1)}, bf16[1,512,8,8]{1,3,2,0:T(8,128)(2,1)}, u32[]{:S(2)}) copy-start(bf16[1,512,8,8]{1,3,2,0:T(8,128)(2,1)} %param.9) | copy-start | bytes 196612
  25.1 10.5 %collective-permute-start.3 = (s16[288,512]{1,0:T(8,128)(2,1)}, s16[288,512]{1,0:T(8,128)(2,1)S(1)}, u32[]{:S(2)}, u32[]{:S(2)}) collective-permute-start(s16[288,512]{1,0:T(8,128)(2,1)} %get-tuple-element.22), channel_id=1, source_target_pairs={{0,2},{1,3},{2,0},{4,6},{5,7},{6,4},{9,11},{10,8},{11,9},{13,15},{... | collective-permute-start | bytes 884744 | tf_op jit(solution)/shard_map/ppermute | solution.py:424
  28.9 8.8 %collective-permute-start.4 = (s16[288,512]{1,0:T(8,128)(2,1)}, s16[288,512]{1,0:T(8,128)(2,1)S(1)}, u32[]{:S(2)}, u32[]{:S(2)}) collective-permute-start(s16[288,512]{1,0:T(8,128)(2,1)} %get-tuple-element.23), channel_id=1, source_target_pairs={{1,0},{3,2},{5,4},{7,6},{8,9},{10,11},{12,13},{14,15},{17,16},{19,... | collective-permute-start | bytes 884744 | tf_op jit(solution)/shard_map/ppermute | solution.py:424
  35.6 2.1 %copy-start.5 = (s16[288,512]{1,0:T(8,128)(2,1)}, s16[288,512]{1,0:T(8,128)(2,1)S(1)}, u32[]{:S(2)}) copy-start(s16[288,512]{1,0:T(8,128)(2,1)S(1)} %collective-permute-done.3.p4_ref) | copy-start | bytes 884740
  37.7 0.7 copy-start.6
  41.3 12.6 %collective-permute-start.5 = (s16[288,512]{1,0:T(8,128)(2,1)}, s16[288,512]{1,0:T(8,128)(2,1)S(1)}, u32[]{:S(2)}, u32[]{:S(2)}) collective-permute-start(s16[288,512]{1,0:T(8,128)(2,1)} %get-tuple-element.25), channel_id=1, source_target_pairs={{0,4},{2,6},{4,0},{6,2},{7,3},{8,12},{9,13},{11,15},{13,9},{15,11}... | collective-permute-start | bytes 884744 | tf_op jit(solution)/shard_map/ppermute | solution.py:424
  53.9 0.7 copy-start.1
  73.9 12.3 %all-to-all-start = ((bf16[8,16,512]{2,1,0:T(8,128)(2,1)}), bf16[8,16,512]{2,1,0:T(8,128)(2,1)S(1)}, u32[]{:S(2)}, u32[]{:S(2)}) async-start(bf16[8,16,512]{2,1,0:T(8,128)(2,1)} %broadcast_in_dim.2), calls=%async_computation | async-start | bytes 262144 | tf_op jit(solution)/shard_map/all_to_all | solution.py:517
  86.2 0.6 copy-start
  99.3 11.8 %all-to-all-start.1 = ((f32[8,2,16]{2,1,0:T(2,128)}), f32[8,2,16]{2,1,0:T(2,128)S(1)}, u32[]{:S(2)}, u32[]{:S(2)}) async-start(f32[8,2,16]{2,1,0:T(2,128)} %bitcast.32), calls=%async_computation.1 | async-start | bytes 16384 | tf_op jit(solution)/shard_map/all_to_all | solution.py:542

commit v3 on v2

--- a/solution.py
+++ b/solution.py
@@ -25,7 +25,7 @@
 bf16 = jnp.bfloat16
 VMEM = pl.BlockSpec(memory_space=pltpu.VMEM)
 SMEM = pl.BlockSpec(memory_space=pltpu.SMEM)
-PARAMS = pltpu.CompilerParams(vmem_limit_bytes=60 * 1024 * 1024)
+MIB = 1024 * 1024
 
 
 def nt(a, b, precision=None):
@@ -375,7 +375,9 @@
         even, odd = x_ref[:, 2 * c * LANES : (2 * c + 1) * LANES], x_ref[:, (2 * c + 1) * LANES : (2 * c + 2) * LANES]
         first = jnp.where(left, even, pltpu.roll(odd, HALF, 1))
         second = jnp.where(left, pltpu.roll(even, HALF, 1), odd)
-        o_ref[:, c * LANES : (c + 1) * LANES] = jnp.concatenate([first, second], axis=0).astype(bf16)
+        both = jnp.concatenate([first, second], axis=0).astype(bf16)
+        for d in range(o_ref.shape[0]):
+            o_ref[d, :, c * LANES : (c + 1) * LANES] = both
 
 
 def predict_kernel(info_ref, x_ref, b_ref, f_ref, o_ref, *, scale):
@@ -449,7 +451,7 @@
         f_row = folds.reshape(1, rows)
         prior = jnp.transpose(guesses[0], (1, 2, 0)).reshape(-1, guesses.shape[1])
 
-        def call(kernel, outs, specs, scratch, *args, **static):
+        def call(kernel, outs, specs, scratch, *args, mib=12, **static):
             import functools
 
             return pl.pallas_call(
@@ -458,7 +460,7 @@
                 in_specs=specs,
                 out_specs=jax.tree.map(lambda _: VMEM, outs),
                 scratch_shapes=scratch,
-                compiler_params=PARAMS,
+                compiler_params=pltpu.CompilerParams(vmem_limit_bytes=mib * MIB),
             )(*args)
 
         def packed(*lead):
@@ -479,11 +481,12 @@
             yt,
             f_row,
             bound=bound,
+            mib=16,
         )
         p1 = move(m0, 1, lambda u, v, w: True)
         p2 = move(m1, 1, lambda u, v, w: u == 1)
         p3 = move(m3, 2, lambda u, v, w: True)
-        k2, k4 = call(gram_keep_kernel, (packed(), packed()), [SMEM, VMEM, VMEM, VMEM], [xt], info, x, yt, f_row)
+        k2, k4 = call(gram_keep_kernel, (packed(), packed()), [SMEM, VMEM, VMEM, VMEM], [xt], info, x, yt, f_row, mib=16)
         ma, mb, ka, kb = call(
             second_kernel,
             (wire(), wire(), packed(), packed()),
@@ -506,7 +509,7 @@
         p6 = move(msg, 4, lambda u, v, w: u == 0 or (u, v, w) == (1, 1, 1))
         beta = call(
             solve_kernel,
-            jax.ShapeDtypeStruct((16, BLOCK), bf16),
+            jax.ShapeDtypeStruct((n_smp, 16, BLOCK), bf16),
             [SMEM, VMEM, VMEM],
             [pltpu.VMEM((BLOCK + 8, 2 * BLOCK), f32), pltpu.VMEM((BLOCK + 8, 2 * BLOCK), f32), pltpu.VMEM((8, 2 * BLOCK), f32)],
             shift,
@@ -514,7 +517,7 @@
             p6,
             bound=bound,
         )
-        betas = lax.all_to_all(jnp.broadcast_to(beta[None], (n_smp, 16, BLOCK)), "smp", 0, 0)
+        betas = lax.all_to_all(beta, "smp", 0, 0)
         oof = call(
             predict_kernel,
             jax.ShapeDtypeStruct((16, rows), bf16),

time: 112 us -> 98.4 us (0.88)
  Pallas kernels: 39.6 us -> 28.6 us
  waiting for transfers between devices: 24.4 us -> 27.5 us
  local copies, waits for them, and re-layouts: 7.05 us -> 4.52 us
  blocking collectives: 13.6 us -> 11.6 us
    pallas_call x7, Pallas kernels: 39.6 us -> 28.6 us  [call(): pl.pallas_call(functools.partial(kernel, **static), out_shape=outs, in_sp...]
    ppermute x6, waiting for transfers between devices: 18.4 us -> 20.1 us  [move(): return lax.ppermute(x, ('blk', 'smp'), pairs(bit, sends))]
    all_gather x1, blocking collectives: 7.34 us -> 5.78 us  [local(): oof_all = lax.all_gather(oof, 'blk', axis=0, tiled=True)]
    broadcast_in_dim x1 -> x0, local copies, waits for them, and re-layouts: 1.37 us -> none  [local(): jnp.broadcast_to(beta[None], (n_smp, 16, BLOCK))]
    unnamed x19 -> x15, local copies, waits for them, and re-layouts: 3.37 us -> 3.65 us
  transfers between devices with their start and end apart: 8 -> 8, of which waited for: 8 -> 8; matrix products, arithmetic and copies ran while one was open for 2% -> 1% of each run, Pallas kernels for 4% -> 3%
where the time goes in v3:
time: 98.4 us; the launch traced here: 97.8 us
  Pallas kernels  28.6 us (29%)
  waiting for transfers between devices  27.5 us (28%)
  starting transfers between devices  24.9 us (25%)
  blocking collectives  11.6 us (12%)
  local copies, waits for them, and re-layouts  4.52 us (5%)
    pallas_call x7, Pallas kernels, call(): pl.pallas_call(functools.partial(kernel, **static), out_shape=outs, in_sp...  28.6 us
    ppermute x6, waiting for transfers between devices, move(): return lax.ppermute(x, ('blk', 'smp'), pairs(bit, sends))  20.1 us
    ppermute x6, starting transfers between devices, move(): return lax.ppermute(x, ('blk', 'smp'), pairs(bit, sends))  15.7 us
    all_to_all x1, waiting for transfers between devices, local(): lax.all_to_all(part.reshape(n_smp, n_cross // n_smp, 16), 'smp', 0, 0)  5.82 us
    all_gather x1, blocking collectives, local(): prior_all = lax.all_gather(prior, 'blk', axis=0)  5.78 us
    all_gather x1, blocking collectives, local(): oof_all = lax.all_gather(oof, 'blk', axis=0, tiled=True)  5.78 us
    all_to_all x1, starting transfers between devices, local(): betas = lax.all_to_all(beta, 'smp', 0, 0)  4.67 us
    all_to_all x1, starting transfers between devices, local(): lax.all_to_all(part.reshape(n_smp, n_cross // n_smp, 16), 'smp', 0, 0)  4.5 us
  transfers between devices with their start and end apart: 8, of which 8 were waited for; matrix products, arithmetic and copies ran while one was open for 1% of the time, Pallas kernels for 3%

profile of v3, /device:TPU:0, one launch (start us, length us, event | category | flops | bytes accessed | tf_op | source)
XLA Modules:
  0.0 97.8 jit_solution(15162812675420709772)
XLA Ops:
  0.8 1.6 %copy-done = bf16[2048,512]{1,0:T(8,128)(2,1)S(1)} copy-done((bf16[2048,512]{1,0:T(8,128)(2,1)S(1)}, bf16[2048,512]{1,0:T(8,128)(2,1)}, u32[]{:S(2)}) %copy-start) | copy-done | bytes 2097176
  3.8 3.8 %shard_map.68 = (s16[288,512]{1,0:T(8,128)(2,1)S(1)}, s16[288,512]{1,0:T(8,128)(2,1)S(1)}, s16[288,512]{1,0:T(8,128)(2,1)S(1)}, f32[272,512]{1,0:T(8,128)S(1)}) custom-call(s32[16]{0:T(128)S(1)} %stack.51.info_ref, bf16[2048,512]{1,0:T(8,128)(2,1)S(1)} %copy-done, bf16[8,2048]{1,0:T(8,128)(2,1)S(1)} %bitcast.25, s32[1,2048]{1,0:T(1,128)S(1)} %bitcast.27), custom_call_target="tpu_custom_call" | custom-call | tf_op jit(solution)/shard_map/pallas_call | solution.py:457
  7.7 3.1 %collective-permute-start = (s16[288,512]{1,0:T(8,128)(2,1)S(1)}, s16[288,512]{1,0:T(8,128)(2,1)S(1)}, u32[]{:S(2)}, u32[]{:S(2)}) collective-permute-start(s16[288,512]{1,0:T(8,128)(2,1)S(1)} %get-tuple-element.17), channel_id=1, source_target_pairs={{0,1},{1,0},{2,3},{3,2},{4,5},{5,4},{6,7},{7,6},{8,9},{9,8},{10,11... | collective-permute-start | bytes 884744 | tf_op jit(solution)/shard_map/ppermute | solution.py:426
  10.7 1.3 %collective-permute-start.1 = (s16[288,512]{1,0:T(8,128)(2,1)S(1)}, s16[288,512]{1,0:T(8,128)(2,1)S(1)}, u32[]{:S(2)}, u32[]{:S(2)}) collective-permute-start(s16[288,512]{1,0:T(8,128)(2,1)S(1)} %get-tuple-element.18), channel_id=1, source_target_pairs={{1,0},{3,2},{5,4},{7,6},{8,9},{10,11},{12,13},{14,15},{17,16},{19,... | collective-permute-start | bytes 884744 | tf_op jit(solution)/shard_map/ppermute | solution.py:426
  12.0 1.6 %collective-permute-start.2 = (s16[288,512]{1,0:T(8,128)(2,1)S(1)}, s16[288,512]{1,0:T(8,128)(2,1)S(1)}, u32[]{:S(2)}, u32[]{:S(2)}) collective-permute-start(s16[288,512]{1,0:T(8,128)(2,1)S(1)} %get-tuple-element.19), channel_id=1, source_target_pairs={{0,2},{1,3},{2,0},{3,1},{4,6},{5,7},{6,4},{7,5},{8,10},{9,11},{10,... | collective-permute-start | bytes 884744 | tf_op jit(solution)/shard_map/ppermute | solution.py:426
  13.7 2.5 %shard_map.69 = (f32[272,512]{1,0:T(8,128)S(1)}, f32[272,512]{1,0:T(8,128)S(1)}) custom-call(s32[16]{0:T(128)S(1)} %stack.51.info_ref, bf16[2048,512]{1,0:T(8,128)(2,1)S(1)} %copy-done, bf16[8,2048]{1,0:T(8,128)(2,1)S(1)} %bitcast.26, s32[1,2048]{1,0:T(1,128)S(1)} %bitcast.28), custom_call_target="tpu_custom_call" | custom-call | tf_op jit(solution)/shard_map/pallas_call | solution.py:457
  16.2 2.0 %collective-permute-done.p1_ref = s16[288,512]{1,0:T(8,128)(2,1)S(1)} collective-permute-done((s16[288,512]{1,0:T(8,128)(2,1)S(1)}, s16[288,512]{1,0:T(8,128)(2,1)S(1)}, u32[]{:S(2)}, u32[]{:S(2)}) %collective-permute-start) | collective-permute-done | bytes 294944 | tf_op jit(solution)/shard_map/ppermute | solution.py:426
  18.1 2.8 %collective-permute-done.1.p2_ref = s16[288,512]{1,0:T(8,128)(2,1)S(1)} collective-permute-done((s16[288,512]{1,0:T(8,128)(2,1)S(1)}, s16[288,512]{1,0:T(8,128)(2,1)S(1)}, u32[]{:S(2)}, u32[]{:S(2)}) %collective-permute-start.1) | collective-permute-done | bytes 294944 | tf_op jit(solution)/shard_map/ppermute | solution.py:426
  21.2 1.4 %shard_map.70 = (s16[288,512]{1,0:T(8,128)(2,1)S(1)}, s16[288,512]{1,0:T(8,128)(2,1)S(1)}, f32[272,512]{1,0:T(8,128)S(1)}, f32[272,512]{1,0:T(8,128)S(1)}) custom-call(s32[16]{0:T(128)S(1)} %stack.51.info_ref, f32[272,512]{1,0:T(8,128)S(1)} %get-tuple-element.14.k1_ref, f32[272,512]{1,0:T(8,128)S(1)} %get-tuple-element.15.k2_ref, ...), custom_call_target="tpu_custom_call" | custom-call | tf_op jit(solution)/shard_map/pallas_call | solution.py:457
  22.7 3.8 %collective-permute-start.3 = (s16[288,512]{1,0:T(8,128)(2,1)S(1)}, s16[288,512]{1,0:T(8,128)(2,1)S(1)}, u32[]{:S(2)}, u32[]{:S(2)}) collective-permute-start(s16[288,512]{1,0:T(8,128)(2,1)S(1)} %get-tuple-element.22), channel_id=1, source_target_pairs={{0,2},{1,3},{2,0},{4,6},{5,7},{6,4},{9,11},{10,8},{11,9},{13,15},{... | collective-permute-start | bytes 884744 | tf_op jit(solution)/shard_map/ppermute | solution.py:426
  26.5 1.3 %collective-permute-start.4 = (s16[288,512]{1,0:T(8,128)(2,1)S(1)}, s16[288,512]{1,0:T(8,128)(2,1)S(1)}, u32[]{:S(2)}, u32[]{:S(2)}) collective-permute-start(s16[288,512]{1,0:T(8,128)(2,1)S(1)} %get-tuple-element.23), channel_id=1, source_target_pairs={{1,0},{3,2},{5,4},{7,6},{8,9},{10,11},{12,13},{14,15},{17,16},{19,... | collective-permute-start | bytes 884744 | tf_op jit(solution)/shard_map/ppermute | solution.py:426
  27.8 5.2 %collective-permute-done.3.p4_ref = s16[288,512]{1,0:T(8,128)(2,1)S(1)} collective-permute-done((s16[288,512]{1,0:T(8,128)(2,1)S(1)}, s16[288,512]{1,0:T(8,128)(2,1)S(1)}, u32[]{:S(2)}, u32[]{:S(2)}) %collective-permute-start.3) | collective-permute-done | bytes 294944 | tf_op jit(solution)/shard_map/ppermute | solution.py:426
  33.0 2.1 %collective-permute-done.4.p5_ref = s16[288,512]{1,0:T(8,128)(2,1)S(1)} collective-permute-done((s16[288,512]{1,0:T(8,128)(2,1)S(1)}, s16[288,512]{1,0:T(8,128)(2,1)S(1)}, u32[]{:S(2)}, u32[]{:S(2)}) %collective-permute-start.4) | collective-permute-done | bytes 294944 | tf_op jit(solution)/shard_map/ppermute | solution.py:426
  35.1 1.1 %shard_map.71 = (s16[288,512]{1,0:T(8,128)(2,1)S(1)}, f32[272,512]{1,0:T(8,128)S(1)}) custom-call(s32[16]{0:T(128)S(1)} %stack.51.info_ref, f32[272,512]{1,0:T(8,128)S(1)} %get-tuple-element.20.ka_ref, f32[272,512]{1,0:T(8,128)S(1)} %get-tuple-element.21.kb_ref, s16[288,512]{1,0:T(8,128)(2,1)S(1)} %collective-permute-done.3.p4_ref, ...), custom_call_target="tpu_custom_call" | custom-call | tf_op jit(solution)/shard_map/pallas_call | solution.py:457
  36.2 4.7 %collective-permute-start.5 = (s16[288,512]{1,0:T(8,128)(2,1)S(1)}, s16[288,512]{1,0:T(8,128)(2,1)S(1)}, u32[]{:S(2)}, u32[]{:S(2)}) collective-permute-start(s16[288,512]{1,0:T(8,128)(2,1)S(1)} %get-tuple-element.25), channel_id=1, source_target_pairs={{0,4},{2,6},{4,0},{6,2},{7,3},{8,12},{9,13},{11,15},{13,9},{15,11}... | collective-permute-start | bytes 884744 | tf_op jit(solution)/shard_map/ppermute | solution.py:426
  40.9 7.7 %collective-permute-done.5.p_ref = s16[288,512]{1,0:T(8,128)(2,1)S(1)} collective-permute-done((s16[288,512]{1,0:T(8,128)(2,1)S(1)}, s16[288,512]{1,0:T(8,128)(2,1)S(1)}, u32[]{:S(2)}, u32[]{:S(2)}) %collective-permute-start.5) | collective-permute-done | bytes 294944 | tf_op jit(solution)/shard_map/ppermute | solution.py:426
  48.6 17.4 %shard_map.72 = bf16[8,16,512]{2,1,0:T(8,128)(2,1)} custom-call(f32[2]{0:T(128)S(1)} %broadcast_multiply_fusion.shift_ref, f32[272,512]{1,0:T(8,128)S(1)} %get-tuple-element.24.k_ref, s16[288,512]{1,0:T(8,128)(2,1)S(1)} %collective-permute-done.5.p_ref), custom_call_target="tpu_custom_call" | custom-call | tf_op jit(solution)/shard_map/pallas_call | solution.py:457
  66.0 4.7 %all-to-all-start = ((bf16[8,16,512]{2,1,0:T(8,128)(2,1)}), bf16[8,16,512]{2,1,0:T(8,128)(2,1)S(1)}, u32[]{:S(2)}, u32[]{:S(2)}) async-start(bf16[8,16,512]{2,1,0:T(8,128)(2,1)} %shard_map.72), calls=%async_computation | async-start | bytes 262144 | tf_op jit(solution)/shard_map/all_to_all | solution.py:520
  70.7 5.8 %all_gather.7.g_ref = bf16[4,64,512]{2,1,0:T(8,128)(2,1)S(1)} all-gather(bf16[1,64,512]{2,1,0:T(8,128)(2,1)S(1)} %bitcast.30), channel_id=1, replica_groups=mesh['blk'=4,'smp'=8] {'blk'}, dimensions={0}, use_global_device_ids=true | all-gather | bytes 327680 | tf_op jit(solution)/shard_map/all_gather | solution.py:532
  76.5 1.6 %all-to-all-done.b_ref = bf16[8,16,512]{2,1,0:T(8,128)(2,1)S(1)} async-done(((bf16[8,16,512]{2,1,0:T(8,128)(2,1)}), bf16[8,16,512]{2,1,0:T(8,128)(2,1)S(1)}, u32[]{:S(2)}, u32[]{:S(2)}) %all-to-all-start) | async-done | bytes 131104 | tf_op jit(solution)/shard_map/all_to_all | solution.py:520
  78.1 1.3 %shard_map.73.o_ref = bf16[16,2048]{1,0:T(8,128)(2,1)S(1)} custom-call(s32[16]{0:T(128)S(1)} %stack.51.info_ref, bf16[2048,512]{1,0:T(8,128)(2,1)S(1)} %copy-done.1, bf16[8,16,512]{2,1,0:T(8,128)(2,1)S(1)} %all-to-all-done.b_ref, s32[1,2048]{1,0:T(1,128)S(1)} %bitcast.29), custom_call_target="tpu_custom_call" | custom-call | tf_op jit(solution)/shard_map/pallas_call | solution.py:457
  79.4 5.8 %all_gather.6.j_ref = bf16[64,2048]{1,0:T(8,128)(2,1)S(1)} all-gather(bf16[16,2048]{1,0:T(8,128)(2,1)S(1)} %shard_map.73.o_ref), channel_id=1, replica_groups=mesh['blk'=4,'smp'=8] {'blk'}, dimensions={0}, use_global_device_ids=true | all-gather | bytes 327680 | tf_op jit(solution)/shard_map/all_gather | solution.py:533
  86.1 4.5 %all-to-all-start.1 = ((f32[8,2,16]{2,1,0:T(2,128)}), f32[8,2,16]{2,1,0:T(2,128)S(1)}, u32[]{:S(2)}, u32[]{:S(2)}) async-start(f32[8,2,16]{2,1,0:T(2,128)} %bitcast.18), calls=%async_computation.1 | async-start | bytes 16384 | tf_op jit(solution)/shard_map/all_to_all | solution.py:545
  91.3 5.8 %all-to-all-done.1 = f32[8,2,16]{2,1,0:T(2,128)S(1)} async-done(((f32[8,2,16]{2,1,0:T(2,128)}), f32[8,2,16]{2,1,0:T(2,128)S(1)}, u32[]{:S(2)}, u32[]{:S(2)}) %all-to-all-start.1) | async-done | bytes 1056 | tf_op jit(solution)/shard_map/all_to_all | solution.py:545
  (21 shorter events, 4.3 us)
Async XLA Ops:
  0.8 1.6 %copy-start = (bf16[2048,512]{1,0:T(8,128)(2,1)S(1)}, bf16[2048,512]{1,0:T(8,128)(2,1)}, u32[]{:S(2)}) copy-start(bf16[2048,512]{1,0:T(8,128)(2,1)} %x_ref.5) | copy-start | bytes 6291460
  2.3 0.8 copy-start.2
  3.1 0.7 copy-start.3
  7.7 10.5 %collective-permute-start = (s16[288,512]{1,0:T(8,128)(2,1)S(1)}, s16[288,512]{1,0:T(8,128)(2,1)S(1)}, u32[]{:S(2)}, u32[]{:S(2)}) collective-permute-start(s16[288,512]{1,0:T(8,128)(2,1)S(1)} %get-tuple-element.17), channel_id=1, source_target_pairs={{0,1},{1,0},{2,3},{3,2},{4,5},{5,4},{6,7},{7,6},{8,9},{9,8},{10,11... | collective-permute-start | bytes 884744 | tf_op jit(solution)/shard_map/ppermute | solution.py:426
  10.7 10.2 %collective-permute-start.1 = (s16[288,512]{1,0:T(8,128)(2,1)S(1)}, s16[288,512]{1,0:T(8,128)(2,1)S(1)}, u32[]{:S(2)}, u32[]{:S(2)}) collective-permute-start(s16[288,512]{1,0:T(8,128)(2,1)S(1)} %get-tuple-element.18), channel_id=1, source_target_pairs={{1,0},{3,2},{5,4},{7,6},{8,9},{10,11},{12,13},{14,15},{17,16},{19,... | collective-permute-start | bytes 884744 | tf_op jit(solution)/shard_map/ppermute | solution.py:426
  12.0 9.2 %collective-permute-start.2 = (s16[288,512]{1,0:T(8,128)(2,1)S(1)}, s16[288,512]{1,0:T(8,128)(2,1)S(1)}, u32[]{:S(2)}, u32[]{:S(2)}) collective-permute-start(s16[288,512]{1,0:T(8,128)(2,1)S(1)} %get-tuple-element.19), channel_id=1, source_target_pairs={{0,2},{1,3},{2,0},{3,1},{4,6},{5,7},{6,4},{7,5},{8,10},{9,11},{10,... | collective-permute-start | bytes 884744 | tf_op jit(solution)/shard_map/ppermute | solution.py:426
  21.2 19.7 %copy-start.6 = (f32[2]{0:T(128)S(1)}, f32[2]{0:T(128)}, u32[]{:S(2)}) copy-start(f32[2]{0:T(128)} %param.8) | copy-start | bytes 28
  22.7 48.1 %copy-start.5 = (bf16[1,512,8,8]{1,3,2,0:T(8,128)(2,1)S(1)}, bf16[1,512,8,8]{1,3,2,0:T(8,128)(2,1)}, u32[]{:S(2)}) copy-start(bf16[1,512,8,8]{1,3,2,0:T(8,128)(2,1)} %param.9) | copy-start | bytes 196612
  22.7 55.4 %copy-start.1 = (bf16[2048,512]{1,0:T(8,128)(2,1)S(1)}, bf16[2048,512]{1,0:T(8,128)(2,1)}, u32[]{:S(2)}) copy-start(bf16[2048,512]{1,0:T(8,128)(2,1)} %x_ref.5) | copy-start | bytes 6291460
  22.7 55.4 %copy-start.4 = (s32[2048]{0:T(1024)S(1)}, s32[2048]{0:T(1024)}, u32[]{:S(2)}) copy-start(s32[2048]{0:T(1024)} %param.7) | copy-start | bytes 24580
  22.7 10.3 %collective-permute-start.3 = (s16[288,512]{1,0:T(8,128)(2,1)S(1)}, s16[288,512]{1,0:T(8,128)(2,1)S(1)}, u32[]{:S(2)}, u32[]{:S(2)}) collective-permute-start(s16[288,512]{1,0:T(8,128)(2,1)S(1)} %get-tuple-element.22), channel_id=1, source_target_pairs={{0,2},{1,3},{2,0},{4,6},{5,7},{6,4},{9,11},{10,8},{11,9},{13,15},{... | collective-permute-start | bytes 884744 | tf_op jit(solution)/shard_map/ppermute | solution.py:426
  26.5 8.6 %collective-permute-start.4 = (s16[288,512]{1,0:T(8,128)(2,1)S(1)}, s16[288,512]{1,0:T(8,128)(2,1)S(1)}, u32[]{:S(2)}, u32[]{:S(2)}) collective-permute-start(s16[288,512]{1,0:T(8,128)(2,1)S(1)} %get-tuple-element.23), channel_id=1, source_target_pairs={{1,0},{3,2},{5,4},{7,6},{8,9},{10,11},{12,13},{14,15},{17,16},{19,... | collective-permute-start | bytes 884744 | tf_op jit(solution)/shard_map/ppermute | solution.py:426
  36.2 12.4 %collective-permute-start.5 = (s16[288,512]{1,0:T(8,128)(2,1)S(1)}, s16[288,512]{1,0:T(8,128)(2,1)S(1)}, u32[]{:S(2)}, u32[]{:S(2)}) collective-permute-start(s16[288,512]{1,0:T(8,128)(2,1)S(1)} %get-tuple-element.25), channel_id=1, source_target_pairs={{0,4},{2,6},{4,0},{6,2},{7,3},{8,12},{9,13},{11,15},{13,9},{15,11}... | collective-permute-start | bytes 884744 | tf_op jit(solution)/shard_map/ppermute | solution.py:426
  66.0 12.0 %all-to-all-start = ((bf16[8,16,512]{2,1,0:T(8,128)(2,1)}), bf16[8,16,512]{2,1,0:T(8,128)(2,1)S(1)}, u32[]{:S(2)}, u32[]{:S(2)}) async-start(bf16[8,16,512]{2,1,0:T(8,128)(2,1)} %shard_map.72), calls=%async_computation | async-start | bytes 262144 | tf_op jit(solution)/shard_map/all_to_all | solution.py:520
  86.1 11.0 %all-to-all-start.1 = ((f32[8,2,16]{2,1,0:T(2,128)}), f32[8,2,16]{2,1,0:T(2,128)S(1)}, u32[]{:S(2)}, u32[]{:S(2)}) async-start(f32[8,2,16]{2,1,0:T(2,128)} %bitcast.18), calls=%async_computation.1 | async-start | bytes 16384 | tf_op jit(solution)/shard_map/all_to_all | solution.py:545

commit v4 on v3

--- a/solution.py
+++ b/solution.py
@@ -8,9 +8,7 @@
 from jax.sharding import PartitionSpec as P
 
 BLOCK = 512
-PHENOTYPIC_MEASURES = 8
 FOLDS = 5
-SHRINK_STRENGTH = 2
 
 LANES = 128
 TILE = 8
@@ -25,6 +23,7 @@
 bf16 = jnp.bfloat16
 VMEM = pl.BlockSpec(memory_space=pltpu.VMEM)
 SMEM = pl.BlockSpec(memory_space=pltpu.SMEM)
+HBM = pl.BlockSpec(memory_space=pltpu.HBM)
 MIB = 1024 * 1024
 
 
@@ -127,10 +126,11 @@
     return lambda rows, cols: ref[rows, cols]
 
 
-def gram_one(fold, x_ref, xt_ref, f_ref, out_ref, eye, low):
+def gram_one(fold, x_ref, xt_ref, yt_ref, f_ref, out_ref, eye, low):
     mask = jnp.where(f_ref[...] != fold, 1.0, 0.0).astype(bf16)
     g0 = jnp.dot(xt_ref[0:256, :] * mask, x_ref[:, 0:256], preferred_element_type=f32)
-    g1 = jnp.dot(xt_ref[256:528, :] * mask, x_ref[...], preferred_element_type=f32)
+    lower = jnp.concatenate([xt_ref[256:BLOCK, :], yt_ref[...]], axis=0)
+    g1 = jnp.dot(lower * mask, x_ref[...], preferred_element_type=f32)
 
     def block(i, j):
         rs, cs = place(i, j)
@@ -149,24 +149,42 @@
     out_ref[264:272, :] = jnp.concatenate([jnp.concatenate(diag, axis=1), jnp.zeros((7, BLOCK), f32)], axis=0)
 
 
-def load_transposed(x_ref, yt_ref, xt_ref):
-    xt_ref[0:BLOCK, :] = x_ref[...].T
-    xt_ref[BLOCK : BLOCK + 16, :] = jnp.concatenate([yt_ref[...], jnp.zeros_like(yt_ref[...])], axis=0)
-
-
-def gram_send_kernel(info_ref, x_ref, yt_ref, f_ref, m0_ref, m1_ref, m3_ref, keep_ref, xt_ref, work_ref, *, bound):
+def gram_first_kernel(
+    x_hbm, yt_hbm, f_hbm, msg_ref, x_ref, yt_ref, f_ref, work_ref, xt_ref, in_ref, sems, *, bound, fold_of, chunks
+):
+    rows = x_ref.shape[0] // chunks
+    small = [pltpu.make_async_copy(yt_hbm, in_ref, sems.at[chunks]), pltpu.make_async_copy(f_hbm, f_ref, sems.at[chunks + 1])]
+    loads = []
+    for c in range(chunks):
+        part = pl.ds(c * rows, rows)
+        loads.append(pltpu.make_async_copy(x_hbm.at[part], x_ref.at[part], sems.at[c]))
+    for copy in loads + small:
+        copy.start()
     eye, low = square_masks()
-    load_transposed(x_ref, yt_ref, xt_ref)
-    for slot, dst, msg_ref in ((0, work_ref, m0_ref), (1, keep_ref, m1_ref), (3, work_ref, m3_ref)):
-        gram_one(info_ref[slot], x_ref, xt_ref, f_ref, dst, eye, low)
+    for c, copy in enumerate(loads):
+        copy.wait()
+        part = slice(c * rows, (c + 1) * rows)
+        xt_ref[:, part] = x_ref[part, :].T
+    for copy in small:
+        copy.wait()
+    yt_ref[...] = jnp.concatenate([in_ref[...], jnp.zeros_like(in_ref[...])], axis=0)
+    gram_one(fold_of(), x_ref, xt_ref, yt_ref, f_ref, work_ref, eye, low)
+    encode(reader(work_ref), msg_ref, bound, eye, low)
+
+
+def gram_send_kernel(info_ref, x_ref, yt_ref, f_ref, m1_ref, m3_ref, keep_ref, work_ref, xt_ref, *, bound):
+    eye, low = square_masks()
+    xt_ref[...] = x_ref[...].T
+    for slot, dst, msg_ref in ((1, keep_ref, m1_ref), (3, work_ref, m3_ref)):
+        gram_one(info_ref[slot], x_ref, xt_ref, yt_ref, f_ref, dst, eye, low)
         encode(reader(dst), msg_ref, bound, eye, low)
 
 
 def gram_keep_kernel(info_ref, x_ref, yt_ref, f_ref, k2_ref, k4_ref, xt_ref):
     eye, low = square_masks()
-    load_transposed(x_ref, yt_ref, xt_ref)
+    xt_ref[...] = x_ref[...].T
     for slot, dst in ((2, k2_ref), (4, k4_ref)):
-        gram_one(info_ref[slot], x_ref, xt_ref, f_ref, dst, eye, low)
+        gram_one(info_ref[slot], x_ref, xt_ref, yt_ref, f_ref, dst, eye, low)
 
 
 def second_kernel(
@@ -451,7 +469,7 @@
         f_row = folds.reshape(1, rows)
         prior = jnp.transpose(guesses[0], (1, 2, 0)).reshape(-1, guesses.shape[1])
 
-        def call(kernel, outs, specs, scratch, *args, mib=12, **static):
+        def call(kernel, outs, specs, scratch, *args, mib=12, flops=0, **static):
             import functools
 
             return pl.pallas_call(
@@ -461,6 +479,7 @@
                 out_specs=jax.tree.map(lambda _: VMEM, outs),
                 scratch_shapes=scratch,
                 compiler_params=pltpu.CompilerParams(vmem_limit_bytes=mib * MIB),
+                cost_estimate=pl.CostEstimate(flops=flops, bytes_accessed=4 * MIB, transcendentals=0),
             )(*args)
 
         def packed(*lead):
@@ -469,24 +488,50 @@
         def wire(*lead):
             return jax.ShapeDtypeStruct((*lead, WIRE, BLOCK), jnp.int16)
 
-        xt = pltpu.VMEM((BLOCK + 16, rows), bf16)
+        def first_fold():
+            s = lax.axis_index("smp") ^ (lax.axis_index("blk") & 1)
+            return jnp.where(s & 1 == 0, 2, 0)
+
         work = pltpu.VMEM((PACKED, BLOCK), f32)
-        m0, m1, m3, k1 = call(
+        xt = pltpu.VMEM((BLOCK, rows), bf16)
+        chunks = 4
+        gram_flops = 2 * rows * BLOCK * BLOCK
+        m0, x_near, yt_near, f_near = call(
+            gram_first_kernel,
+            (
+                wire(),
+                jax.ShapeDtypeStruct(x.shape, bf16),
+                jax.ShapeDtypeStruct((16, rows), bf16),
+                jax.ShapeDtypeStruct((1, rows), jnp.int32),
+            ),
+            [HBM] * 3,
+            [work, xt, pltpu.VMEM(yt.shape, bf16), pltpu.SemaphoreType.DMA((chunks + 2,))],
+            *(pltpu.with_memory_space_constraint(v, pltpu.HBM) for v in (x, yt, f_row)),
+            bound=bound,
+            fold_of=first_fold,
+            chunks=chunks,
+            mib=14,
+            flops=gram_flops,
+        )
+        p1 = move(m0, 1, lambda u, v, w: True)
+        m1, m3, k1 = call(
             gram_send_kernel,
-            (wire(), wire(), wire(), packed()),
+            (wire(), wire(), packed()),
             [SMEM, VMEM, VMEM, VMEM],
-            [xt, work],
+            [work, xt],
             info,
-            x,
-            yt,
-            f_row,
+            x_near,
+            yt_near,
+            f_near,
             bound=bound,
-            mib=16,
-        )
-        p1 = move(m0, 1, lambda u, v, w: True)
+            mib=14,
+            flops=2 * gram_flops,
+        )
         p2 = move(m1, 1, lambda u, v, w: u == 1)
         p3 = move(m3, 2, lambda u, v, w: True)
-        k2, k4 = call(gram_keep_kernel, (packed(), packed()), [SMEM, VMEM, VMEM, VMEM], [xt], info, x, yt, f_row, mib=16)
+        k2, k4 = call(
+            gram_keep_kernel, (packed(), packed()), [SMEM] + [VMEM] * 3, [xt], info, x_near, yt_near, f_near, mib=14, flops=2 * gram_flops
+        )
         ma, mb, ka, kb = call(
             second_kernel,
             (wire(), wire(), packed(), packed()),
@@ -524,9 +569,9 @@
             [SMEM, VMEM, VMEM, VMEM],
             [],
             info,
-            x,
+            x_near,
             betas,
-            f_row,
+            f_near,
             scale=math.sqrt(total / BLOCK),
         )
         prior_all = lax.all_gather(prior, "blk", axis=0)

time: 98.4 us -> 99.3 us (level)
  local copies, waits for them, and re-layouts: 4.52 us -> 1.47 us
  Pallas kernels: 28.6 us -> 30.5 us
  starting transfers between devices: 24.9 us -> 26.5 us
    unnamed x15 -> x5, local copies, waits for them, and re-layouts: 3.65 us -> 0.59 us
    ppermute x6, starting transfers between devices: 15.7 us -> 17.8 us  [move(): return lax.ppermute(x, ('blk', 'smp'), pairs(bit, sends))]
    pallas_call x7 -> x8, Pallas kernels: 28.6 us -> 30.5 us  [call(): pl.pallas_call(functools.partial(kernel, **static), out_shape=outs, in_sp...]
  transfers between devices with their start and end apart: 8 -> 8, of which waited for: 8 -> 7; matrix products, arithmetic and copies ran while one was open for 1% -> 1% of each run, Pallas kernels for 3% -> 2%
where the time goes in v4:
time: 99.3 us; the launch traced here: 98.8 us
  Pallas kernels  30.5 us (31%)
  waiting for transfers between devices  28 us (28%)
  starting transfers between devices  26.5 us (27%)
  blocking collectives  11.6 us (12%)
  local copies, waits for them, and re-layouts  1.47 us (1%)
    pallas_call x8, Pallas kernels, call(): pl.pallas_call(functools.partial(kernel, **static), out_shape=outs, in_sp...  30.5 us
    ppermute x6, waiting for transfers between devices, move(): return lax.ppermute(x, ('blk', 'smp'), pairs(bit, sends))  20.6 us
    ppermute x6, starting transfers between devices, move(): return lax.ppermute(x, ('blk', 'smp'), pairs(bit, sends))  17.8 us
    all_to_all x1, waiting for transfers between devices, local(): lax.all_to_all(part.reshape(n_smp, n_cross // n_smp, 16), 'smp', 0, 0)  5.82 us
    all_gather x1, blocking collectives, local(): prior_all = lax.all_gather(prior, 'blk', axis=0)  5.78 us
    all_gather x1, blocking collectives, local(): oof_all = lax.all_gather(oof, 'blk', axis=0, tiled=True)  5.78 us
    all_to_all x1, starting transfers between devices, local(): lax.all_to_all(part.reshape(n_smp, n_cross // n_smp, 16), 'smp', 0, 0)  4.5 us
    all_to_all x1, starting transfers between devices, local(): betas = lax.all_to_all(beta, 'smp', 0, 0)  4.19 us
  transfers between devices with their start and end apart: 8, of which 7 were waited for; matrix products, arithmetic and copies ran while one was open for 1% of the time, Pallas kernels for 2%

profile of v4, /device:TPU:0, one launch (start us, length us, event | category | flops | bytes accessed | tf_op | source)
XLA Modules:
  0.0 98.8 jit_solution(10836931228777984924)
XLA Ops:
  0.7 3.1 %shard_map.68 = (s16[288,512]{1,0:T(8,128)(2,1)S(1)}, bf16[2048,512]{1,0:T(8,128)(2,1)S(1)}, bf16[16,2048]{1,0:T(8,128)(2,1)S(1)}, s32[1,2048]{1,0:T(1,128)S(1)}) custom-call(bf16[2048,512]{1,0:T(8,128)(2,1)} %x_hbm.1, bf16[8,2048]{1,0:T(8,128)(2,1)} %bitcast.28, s32[1,2048]{1,0:T(1,128)} %bitcast.29), custom_call_target="tpu_custom_call" | custom-call | flops 1073741824 | bytes 4194304 | tf_op jit(solution)/shard_map/pallas_call | solution.py:475
  3.9 2.8 %shard_map.69 = (s16[288,512]{1,0:T(8,128)(2,1)S(1)}, s16[288,512]{1,0:T(8,128)(2,1)S(1)}, f32[272,512]{1,0:T(8,128)S(1)}) custom-call(s32[16]{0:T(128)S(1)} %stack.51.info_ref, bf16[2048,512]{1,0:T(8,128)(2,1)S(1)} %get-tuple-element.17.x_ref, bf16[16,2048]{1,0:T(8,128)(2,1)S(1)} %get-tuple-element.18.yt_ref, s32[1,2048]{1,0:T(1,128)S(1)} %get-tuple-element.19.f_ref), custom_call_target="tpu_custom_call" | custom-call | flops 2147483648 | bytes 4194304 | tf_op jit(solution)/shard_map/pallas_call | solution.py:475
  6.7 1.3 %collective-permute-start.1 = (s16[288,512]{1,0:T(8,128)(2,1)S(1)}, s16[288,512]{1,0:T(8,128)(2,1)S(1)}, u32[]{:S(2)}, u32[]{:S(2)}) collective-permute-start(s16[288,512]{1,0:T(8,128)(2,1)S(1)} %get-tuple-element.24), channel_id=1, source_target_pairs={{1,0},{3,2},{5,4},{7,6},{8,9},{10,11},{12,13},{14,15},{17,16},{19,... | collective-permute-start | bytes 884744 | tf_op jit(solution)/shard_map/ppermute | solution.py:444
  8.0 3.1 %collective-permute-start.2 = (s16[288,512]{1,0:T(8,128)(2,1)S(1)}, s16[288,512]{1,0:T(8,128)(2,1)S(1)}, u32[]{:S(2)}, u32[]{:S(2)}) collective-permute-start(s16[288,512]{1,0:T(8,128)(2,1)S(1)} %get-tuple-element.25), channel_id=1, source_target_pairs={{0,2},{1,3},{2,0},{3,1},{4,6},{5,7},{6,4},{7,5},{8,10},{9,11},{10,... | collective-permute-start | bytes 884744 | tf_op jit(solution)/shard_map/ppermute | solution.py:444
  11.1 2.7 %collective-permute-start = (s16[288,512]{1,0:T(8,128)(2,1)S(1)}, s16[288,512]{1,0:T(8,128)(2,1)S(1)}, u32[]{:S(2)}, u32[]{:S(2)}) collective-permute-start(s16[288,512]{1,0:T(8,128)(2,1)S(1)} %get-tuple-element.23), channel_id=1, source_target_pairs={{0,1},{1,0},{2,3},{3,2},{4,5},{5,4},{6,7},{7,6},{8,9},{9,8},{10,11... | collective-permute-start | bytes 884744 | tf_op jit(solution)/shard_map/ppermute | solution.py:444
  13.7 2.4 %shard_map.70 = (f32[272,512]{1,0:T(8,128)S(1)}, f32[272,512]{1,0:T(8,128)S(1)}) custom-call(s32[16]{0:T(128)S(1)} %stack.51.info_ref, bf16[2048,512]{1,0:T(8,128)(2,1)S(1)} %get-tuple-element.17.x_ref, bf16[16,2048]{1,0:T(8,128)(2,1)S(1)} %get-tuple-element.18.yt_ref, s32[1,2048]{1,0:T(1,128)S(1)} %get-tuple-element.19.f_ref), custom_call_target="tpu_custom_call" | custom-call | flops 2147483648 | bytes 4194304 | tf_op jit(solution)/shard_map/pallas_call | solution.py:475
  16.2 1.6 %collective-permute-done.2.p3_ref = s16[288,512]{1,0:T(8,128)(2,1)S(1)} collective-permute-done((s16[288,512]{1,0:T(8,128)(2,1)S(1)}, s16[288,512]{1,0:T(8,128)(2,1)S(1)}, u32[]{:S(2)}, u32[]{:S(2)}) %collective-permute-start.2) | collective-permute-done | bytes 294944 | tf_op jit(solution)/shard_map/ppermute | solution.py:444
  17.8 4.2 %collective-permute-done.p1_ref = s16[288,512]{1,0:T(8,128)(2,1)S(1)} collective-permute-done((s16[288,512]{1,0:T(8,128)(2,1)S(1)}, s16[288,512]{1,0:T(8,128)(2,1)S(1)}, u32[]{:S(2)}, u32[]{:S(2)}) %collective-permute-start) | collective-permute-done | bytes 294944 | tf_op jit(solution)/shard_map/ppermute | solution.py:444
  22.0 1.4 %shard_map.71 = (s16[288,512]{1,0:T(8,128)(2,1)S(1)}, s16[288,512]{1,0:T(8,128)(2,1)S(1)}, f32[272,512]{1,0:T(8,128)S(1)}, f32[272,512]{1,0:T(8,128)S(1)}) custom-call(s32[16]{0:T(128)S(1)} %stack.51.info_ref, f32[272,512]{1,0:T(8,128)S(1)} %get-tuple-element.20.k1_ref, f32[272,512]{1,0:T(8,128)S(1)} %get-tuple-element.21.k2_ref, ...), custom_call_target="tpu_custom_call" | custom-call | bytes 4194304 | tf_op jit(solution)/shard_map/pallas_call | solution.py:475
  23.4 4.7 %collective-permute-start.3 = (s16[288,512]{1,0:T(8,128)(2,1)S(1)}, s16[288,512]{1,0:T(8,128)(2,1)S(1)}, u32[]{:S(2)}, u32[]{:S(2)}) collective-permute-start(s16[288,512]{1,0:T(8,128)(2,1)S(1)} %get-tuple-element.28), channel_id=1, source_target_pairs={{0,2},{1,3},{2,0},{4,6},{5,7},{6,4},{9,11},{10,8},{11,9},{13,15},{... | collective-permute-start | bytes 884744 | tf_op jit(solution)/shard_map/ppermute | solution.py:444
  28.1 1.3 %collective-permute-start.4 = (s16[288,512]{1,0:T(8,128)(2,1)S(1)}, s16[288,512]{1,0:T(8,128)(2,1)S(1)}, u32[]{:S(2)}, u32[]{:S(2)}) collective-permute-start(s16[288,512]{1,0:T(8,128)(2,1)S(1)} %get-tuple-element.29), channel_id=1, source_target_pairs={{1,0},{3,2},{5,4},{7,6},{8,9},{10,11},{12,13},{14,15},{17,16},{19,... | collective-permute-start | bytes 884744 | tf_op jit(solution)/shard_map/ppermute | solution.py:444
  29.4 4.5 %collective-permute-done.3.p4_ref = s16[288,512]{1,0:T(8,128)(2,1)S(1)} collective-permute-done((s16[288,512]{1,0:T(8,128)(2,1)S(1)}, s16[288,512]{1,0:T(8,128)(2,1)S(1)}, u32[]{:S(2)}, u32[]{:S(2)}) %collective-permute-start.3) | collective-permute-done | bytes 294944 | tf_op jit(solution)/shard_map/ppermute | solution.py:444
  33.9 2.8 %collective-permute-done.4.p5_ref = s16[288,512]{1,0:T(8,128)(2,1)S(1)} collective-permute-done((s16[288,512]{1,0:T(8,128)(2,1)S(1)}, s16[288,512]{1,0:T(8,128)(2,1)S(1)}, u32[]{:S(2)}, u32[]{:S(2)}) %collective-permute-start.4) | collective-permute-done | bytes 294944 | tf_op jit(solution)/shard_map/ppermute | solution.py:444
  36.8 1.1 %shard_map.72 = (s16[288,512]{1,0:T(8,128)(2,1)S(1)}, f32[272,512]{1,0:T(8,128)S(1)}) custom-call(s32[16]{0:T(128)S(1)} %stack.51.info_ref, f32[272,512]{1,0:T(8,128)S(1)} %get-tuple-element.26.ka_ref, f32[272,512]{1,0:T(8,128)S(1)} %get-tuple-element.27.kb_ref, s16[288,512]{1,0:T(8,128)(2,1)S(1)} %collective-permute-done.3.p4_ref, ...), custom_call_target="tpu_custom_call" | custom-call | bytes 4194304 | tf_op jit(solution)/shard_map/pallas_call | solution.py:475
  37.9 4.7 %collective-permute-start.5 = (s16[288,512]{1,0:T(8,128)(2,1)S(1)}, s16[288,512]{1,0:T(8,128)(2,1)S(1)}, u32[]{:S(2)}, u32[]{:S(2)}) collective-permute-start(s16[288,512]{1,0:T(8,128)(2,1)S(1)} %get-tuple-element.31), channel_id=1, source_target_pairs={{0,4},{2,6},{4,0},{6,2},{7,3},{8,12},{9,13},{11,15},{13,9},{15,11}... | collective-permute-start | bytes 884744 | tf_op jit(solution)/shard_map/ppermute | solution.py:444
  42.6 7.5 %collective-permute-done.5.p_ref = s16[288,512]{1,0:T(8,128)(2,1)S(1)} collective-permute-done((s16[288,512]{1,0:T(8,128)(2,1)S(1)}, s16[288,512]{1,0:T(8,128)(2,1)S(1)}, u32[]{:S(2)}, u32[]{:S(2)}) %collective-permute-start.5) | collective-permute-done | bytes 294944 | tf_op jit(solution)/shard_map/ppermute | solution.py:444
  50.1 17.4 %shard_map.73 = bf16[8,16,512]{2,1,0:T(8,128)(2,1)} custom-call(f32[2]{0:T(128)S(1)} %broadcast_multiply_fusion.shift_ref, f32[272,512]{1,0:T(8,128)S(1)} %get-tuple-element.30.k_ref, s16[288,512]{1,0:T(8,128)(2,1)S(1)} %collective-permute-done.5.p_ref), custom_call_target="tpu_custom_call" | custom-call | bytes 4194304 | tf_op jit(solution)/shard_map/pallas_call | solution.py:475
  67.5 4.2 %all-to-all-start = ((bf16[8,16,512]{2,1,0:T(8,128)(2,1)}), bf16[8,16,512]{2,1,0:T(8,128)(2,1)S(1)}, u32[]{:S(2)}, u32[]{:S(2)}) async-start(bf16[8,16,512]{2,1,0:T(8,128)(2,1)} %shard_map.73), calls=%async_computation | async-start | bytes 262144 | tf_op jit(solution)/shard_map/all_to_all | solution.py:565
  71.7 5.8 %all_gather.7.g_ref = bf16[4,64,512]{2,1,0:T(8,128)(2,1)S(1)} all-gather(bf16[1,64,512]{2,1,0:T(8,128)(2,1)S(1)} %bitcast.25), channel_id=1, replica_groups=mesh['blk'=4,'smp'=8] {'blk'}, dimensions={0}, use_global_device_ids=true | all-gather | bytes 327680 | tf_op jit(solution)/shard_map/all_gather | solution.py:577
  77.5 1.6 %all-to-all-done.b_ref = bf16[8,16,512]{2,1,0:T(8,128)(2,1)S(1)} async-done(((bf16[8,16,512]{2,1,0:T(8,128)(2,1)}), bf16[8,16,512]{2,1,0:T(8,128)(2,1)S(1)}, u32[]{:S(2)}, u32[]{:S(2)}) %all-to-all-start) | async-done | bytes 131104 | tf_op jit(solution)/shard_map/all_to_all | solution.py:565
  79.1 1.3 %shard_map.74.o_ref = bf16[16,2048]{1,0:T(8,128)(2,1)S(1)} custom-call(s32[16]{0:T(128)S(1)} %stack.51.info_ref, bf16[2048,512]{1,0:T(8,128)(2,1)S(1)} %get-tuple-element.17.x_ref, bf16[8,16,512]{2,1,0:T(8,128)(2,1)S(1)} %all-to-all-done.b_ref, s32[1,2048]{1,0:T(1,128)S(1)} %get-tuple-element.19.f_ref), custom_call_target="tpu_custom_call" | custom-call | bytes 4194304 | tf_op jit(solution)/shard_map/pallas_call | solution.py:475
  80.4 5.8 %all_gather.6.j_ref = bf16[64,2048]{1,0:T(8,128)(2,1)S(1)} all-gather(bf16[16,2048]{1,0:T(8,128)(2,1)S(1)} %shard_map.74.o_ref), channel_id=1, replica_groups=mesh['blk'=4,'smp'=8] {'blk'}, dimensions={0}, use_global_device_ids=true | all-gather | bytes 327680 | tf_op jit(solution)/shard_map/all_gather | solution.py:578
  87.1 4.5 %all-to-all-start.1 = ((f32[8,2,16]{2,1,0:T(2,128)}), f32[8,2,16]{2,1,0:T(2,128)S(1)}, u32[]{:S(2)}, u32[]{:S(2)}) async-start(f32[8,2,16]{2,1,0:T(2,128)} %bitcast.18), calls=%async_computation.1 | async-start | bytes 16384 | tf_op jit(solution)/shard_map/all_to_all | solution.py:590
  92.3 5.8 %all-to-all-done.1 = f32[8,2,16]{2,1,0:T(2,128)S(1)} async-done(((f32[8,2,16]{2,1,0:T(2,128)}), f32[8,2,16]{2,1,0:T(2,128)S(1)}, u32[]{:S(2)}, u32[]{:S(2)}) %all-to-all-start.1) | async-done | bytes 1056 | tf_op jit(solution)/shard_map/all_to_all | solution.py:590
  (12 shorter events, 2.5 us)
Async XLA Ops:
  6.7 9.5 %collective-permute-start.1 = (s16[288,512]{1,0:T(8,128)(2,1)S(1)}, s16[288,512]{1,0:T(8,128)(2,1)S(1)}, u32[]{:S(2)}, u32[]{:S(2)}) collective-permute-start(s16[288,512]{1,0:T(8,128)(2,1)S(1)} %get-tuple-element.24), channel_id=1, source_target_pairs={{1,0},{3,2},{5,4},{7,6},{8,9},{10,11},{12,13},{14,15},{17,16},{19,... | collective-permute-start | bytes 884744 | tf_op jit(solution)/shard_map/ppermute | solution.py:444
  8.0 9.8 %collective-permute-start.2 = (s16[288,512]{1,0:T(8,128)(2,1)S(1)}, s16[288,512]{1,0:T(8,128)(2,1)S(1)}, u32[]{:S(2)}, u32[]{:S(2)}) collective-permute-start(s16[288,512]{1,0:T(8,128)(2,1)S(1)} %get-tuple-element.25), channel_id=1, source_target_pairs={{0,2},{1,3},{2,0},{3,1},{4,6},{5,7},{6,4},{7,5},{8,10},{9,11},{10,... | collective-permute-start | bytes 884744 | tf_op jit(solution)/shard_map/ppermute | solution.py:444
  11.1 10.9 %collective-permute-start = (s16[288,512]{1,0:T(8,128)(2,1)S(1)}, s16[288,512]{1,0:T(8,128)(2,1)S(1)}, u32[]{:S(2)}, u32[]{:S(2)}) collective-permute-start(s16[288,512]{1,0:T(8,128)(2,1)S(1)} %get-tuple-element.23), channel_id=1, source_target_pairs={{0,1},{1,0},{2,3},{3,2},{4,5},{5,4},{6,7},{7,6},{8,9},{9,8},{10,11... | collective-permute-start | bytes 884744 | tf_op jit(solution)/shard_map/ppermute | solution.py:444
  22.0 20.6 %copy-start.1 = (f32[2]{0:T(128)S(1)}, f32[2]{0:T(128)}, u32[]{:S(2)}) copy-start(f32[2]{0:T(128)} %param.8) | copy-start | bytes 28
  23.4 48.3 %copy-start = (bf16[1,512,8,8]{1,3,2,0:T(8,128)(2,1)S(1)}, bf16[1,512,8,8]{1,3,2,0:T(8,128)(2,1)}, u32[]{:S(2)}) copy-start(bf16[1,512,8,8]{1,3,2,0:T(8,128)(2,1)} %param.9) | copy-start | bytes 196612
  23.4 10.5 %collective-permute-start.3 = (s16[288,512]{1,0:T(8,128)(2,1)S(1)}, s16[288,512]{1,0:T(8,128)(2,1)S(1)}, u32[]{:S(2)}, u32[]{:S(2)}) collective-permute-start(s16[288,512]{1,0:T(8,128)(2,1)S(1)} %get-tuple-element.28), channel_id=1, source_target_pairs={{0,2},{1,3},{2,0},{4,6},{5,7},{6,4},{9,11},{10,8},{11,9},{13,15},{... | collective-permute-start | bytes 884744 | tf_op jit(solution)/shard_map/ppermute | solution.py:444
  28.1 8.6 %collective-permute-start.4 = (s16[288,512]{1,0:T(8,128)(2,1)S(1)}, s16[288,512]{1,0:T(8,128)(2,1)S(1)}, u32[]{:S(2)}, u32[]{:S(2)}) collective-permute-start(s16[288,512]{1,0:T(8,128)(2,1)S(1)} %get-tuple-element.29), channel_id=1, source_target_pairs={{1,0},{3,2},{5,4},{7,6},{8,9},{10,11},{12,13},{14,15},{17,16},{19,... | collective-permute-start | bytes 884744 | tf_op jit(solution)/shard_map/ppermute | solution.py:444
  37.9 12.2 %collective-permute-start.5 = (s16[288,512]{1,0:T(8,128)(2,1)S(1)}, s16[288,512]{1,0:T(8,128)(2,1)S(1)}, u32[]{:S(2)}, u32[]{:S(2)}) collective-permute-start(s16[288,512]{1,0:T(8,128)(2,1)S(1)} %get-tuple-element.31), channel_id=1, source_target_pairs={{0,4},{2,6},{4,0},{6,2},{7,3},{8,12},{9,13},{11,15},{13,9},{15,11}... | collective-permute-start | bytes 884744 | tf_op jit(solution)/shard_map/ppermute | solution.py:444
  67.5 11.5 %all-to-all-start = ((bf16[8,16,512]{2,1,0:T(8,128)(2,1)}), bf16[8,16,512]{2,1,0:T(8,128)(2,1)S(1)}, u32[]{:S(2)}, u32[]{:S(2)}) async-start(bf16[8,16,512]{2,1,0:T(8,128)(2,1)} %shard_map.73), calls=%async_computation | async-start | bytes 262144 | tf_op jit(solution)/shard_map/all_to_all | solution.py:565
  87.1 11.0 %all-to-all-start.1 = ((f32[8,2,16]{2,1,0:T(2,128)}), f32[8,2,16]{2,1,0:T(2,128)S(1)}, u32[]{:S(2)}, u32[]{:S(2)}) async-start(f32[8,2,16]{2,1,0:T(2,128)} %bitcast.18), calls=%async_computation.1 | async-start | bytes 16384 | tf_op jit(solution)/shard_map/all_to_all | solution.py:590

commit v5 on v4

--- a/solution.py
+++ b/solution.py
@@ -175,7 +175,7 @@
 def gram_send_kernel(info_ref, x_ref, yt_ref, f_ref, m1_ref, m3_ref, keep_ref, work_ref, xt_ref, *, bound):
     eye, low = square_masks()
     xt_ref[...] = x_ref[...].T
-    for slot, dst, msg_ref in ((1, keep_ref, m1_ref), (3, work_ref, m3_ref)):
+    for slot, dst, msg_ref in ((3, work_ref, m3_ref), (1, keep_ref, m1_ref)):
         gram_one(info_ref[slot], x_ref, xt_ref, yt_ref, f_ref, dst, eye, low)
         encode(reader(dst), msg_ref, bound, eye, low)
 
@@ -422,8 +422,11 @@
     features = new.shape[1] // 8
     pick_new = jnp.where(iota((features, new.shape[1]), 1) // 8 == iota((features, new.shape[1]), 0), 1.0, 0.0)
     high = lax.Precision.HIGHEST
-    c_ref[0:prior, :] = nt(pick_old, old, high) * scale
-    c_ref[prior : prior + features, :] = nt(pick_new, new, high) * scale
+    both = jnp.concatenate([nt(pick_old, old, high), nt(pick_new, new, high)], axis=0) * scale
+    share = (prior + features) // c_ref.shape[0]
+    for j in range(2):
+        for d in range(c_ref.shape[0]):
+            c_ref[d, j] = both[d * share : (d + 1) * share, 8 * j : 8 * (j + 1)]
 
 
 def make_local(mesh):
@@ -527,8 +530,8 @@
             mib=14,
             flops=2 * gram_flops,
         )
+        p3 = move(m3, 2, lambda u, v, w: True)
         p2 = move(m1, 1, lambda u, v, w: u == 1)
-        p3 = move(m3, 2, lambda u, v, w: True)
         k2, k4 = call(
             gram_keep_kernel, (packed(), packed()), [SMEM] + [VMEM] * 3, [xt], info, x_near, yt_near, f_near, mib=14, flops=2 * gram_flops
         )
@@ -546,8 +549,11 @@
             p3,
             bound=bound,
         )
+        early, ma, mb = lax.optimization_barrier((prior, ma, mb))
         p4 = move(ma, 2, lambda u, v, w: (u, v) != (1, 1))
         p5 = move(mb, 1, lambda u, v, w: u == 1)
+        prior_all = lax.all_gather(early, "blk", axis=0)
+        prior_all, p4 = lax.optimization_barrier((prior_all, p4))
         msg, keep = call(
             third_kernel, (wire(), packed()), [SMEM] + [VMEM] * 4, [work, work], info, ka, kb, p4, p5, bound=bound
         )
@@ -574,12 +580,11 @@
             f_near,
             scale=math.sqrt(total / BLOCK),
         )
-        prior_all = lax.all_gather(prior, "blk", axis=0)
         oof_all = lax.all_gather(oof, "blk", axis=0, tiled=True)
         n_cross = prior.shape[0] // 8 + 2 * n_blk
         part = call(
             cross_kernel,
-            jax.ShapeDtypeStruct((n_cross, 16), f32),
+            jax.ShapeDtypeStruct((n_smp, 2, n_cross // n_smp, 8), f32),
             [VMEM] * 3,
             [],
             oof,
@@ -587,11 +592,10 @@
             prior_all,
             scale=1.0 / total,
         )
-        part = lax.all_to_all(part.reshape(n_smp, n_cross // n_smp, 16), "smp", 0, 0)
-        cross = jnp.sum(part, axis=0).reshape(n_cross // n_smp, 2, 8)
+        cross = jnp.sum(lax.all_to_all(part, "smp", 0, 0), axis=0)
         return (
             jnp.transpose(oof.reshape(2, 8, rows), (2, 1, 0)),
-            jnp.transpose(cross, (2, 1, 0)),
+            jnp.transpose(cross, (2, 0, 1)),
         )
 
     return local

time: 99.3 us -> 99 us (level)
  blocking collectives: 11.6 us -> 24.9 us
  waiting for transfers between devices: 28 us -> 20.6 us
  starting transfers between devices: 26.5 us -> 20.9 us
    all_to_all x0 -> x1, blocking collectives: none -> 13.4 us  [local(): betas = lax.all_to_all(beta, 'smp', 0, 0)]
    ppermute x6, waiting for transfers between devices: 20.6 us -> 14.8 us  [move(): return lax.ppermute(x, ('blk', 'smp'), pairs(bit, sends))]
    all_to_all x2 -> x1, starting transfers between devices: 8.69 us -> 3.31 us  [local(): cross = jnp.sum(lax.all_to_all(part, 'smp', 0, 0), axis=0)]
    all_to_all x2 -> x1, waiting for transfers between devices: 7.38 us -> 5.81 us  [local(): cross = jnp.sum(lax.all_to_all(part, 'smp', 0, 0), axis=0)]
  transfers between devices with their start and end apart: 8 -> 7, of which waited for: 7 -> 5; matrix products, arithmetic and copies ran while one was open for 1% -> 1% of each run, Pallas kernels for 2% -> 2%
where the time goes in v5:
time: 99 us; the launch traced here: 98.7 us
  Pallas kernels  29.9 us (30%)
  blocking collectives  24.9 us (25%)
  starting transfers between devices  20.9 us (21%)
  waiting for transfers between devices  20.6 us (21%)
    pallas_call x8, Pallas kernels, call(): pl.pallas_call(functools.partial(kernel, **static), out_shape=outs, in_sp...  29.9 us
    ppermute x6, starting transfers between devices, move(): return lax.ppermute(x, ('blk', 'smp'), pairs(bit, sends))  17.6 us
    ppermute x6, waiting for transfers between devices, move(): return lax.ppermute(x, ('blk', 'smp'), pairs(bit, sends))  14.8 us
    all_to_all x1, blocking collectives, local(): betas = lax.all_to_all(beta, 'smp', 0, 0)  13.4 us
    all_to_all x1, waiting for transfers between devices, local(): cross = jnp.sum(lax.all_to_all(part, 'smp', 0, 0), axis=0)  5.81 us
    all_gather x1, blocking collectives, local(): prior_all = lax.all_gather(early, 'blk', axis=0)  5.78 us
    all_gather x1, blocking collectives, local(): oof_all = lax.all_gather(oof, 'blk', axis=0, tiled=True)  5.78 us
    all_to_all x1, starting transfers between devices, local(): cross = jnp.sum(lax.all_to_all(part, 'smp', 0, 0), axis=0)  3.31 us
  transfers between devices with their start and end apart: 7, of which 5 were waited for; matrix products, arithmetic and copies ran while one was open for 1% of the time, Pallas kernels for 2%

profile of v5, /device:TPU:0, one launch (start us, length us, event | category | flops | bytes accessed | tf_op | source)
XLA Modules:
  0.0 98.7 jit_solution(15116707398977899033)
XLA Ops:
  0.7 3.1 %shard_map.68 = (s16[288,512]{1,0:T(8,128)(2,1)S(1)}, bf16[2048,512]{1,0:T(8,128)(2,1)S(1)}, bf16[16,2048]{1,0:T(8,128)(2,1)S(1)}, s32[1,2048]{1,0:T(1,128)S(1)}) custom-call(bf16[2048,512]{1,0:T(8,128)(2,1)} %x_hbm.1, bf16[8,2048]{1,0:T(8,128)(2,1)} %bitcast.29, s32[1,2048]{1,0:T(1,128)} %bitcast.30), custom_call_target="tpu_custom_call" | custom-call | flops 1073741824 | bytes 4194304 | tf_op jit(solution)/shard_map/pallas_call | solution.py:478
  3.9 2.7 %shard_map.69 = (s16[288,512]{1,0:T(8,128)(2,1)S(1)}, s16[288,512]{1,0:T(8,128)(2,1)S(1)}, f32[272,512]{1,0:T(8,128)S(1)}) custom-call(s32[16]{0:T(128)S(1)} %stack.51.info_ref, bf16[2048,512]{1,0:T(8,128)(2,1)S(1)} %get-tuple-element.22.x_ref, bf16[16,2048]{1,0:T(8,128)(2,1)S(1)} %get-tuple-element.23.yt_ref, s32[1,2048]{1,0:T(1,128)S(1)} %get-tuple-element.24.f_ref), custom_call_target="tpu_custom_call" | custom-call | flops 2147483648 | bytes 4194304 | tf_op jit(solution)/shard_map/pallas_call | solution.py:478
  6.7 1.3 %collective-permute-start.1 = (s16[288,512]{1,0:T(8,128)(2,1)S(1)}, s16[288,512]{1,0:T(8,128)(2,1)S(1)}, u32[]{:S(2)}, u32[]{:S(2)}) collective-permute-start(s16[288,512]{1,0:T(8,128)(2,1)S(1)} %get-tuple-element.29), channel_id=1, source_target_pairs={{1,0},{3,2},{5,4},{7,6},{8,9},{10,11},{12,13},{14,15},{17,16},{19,... | collective-permute-start | bytes 884744 | tf_op jit(solution)/shard_map/ppermute | solution.py:447
  8.0 3.1 %collective-permute-start.2 = (s16[288,512]{1,0:T(8,128)(2,1)S(1)}, s16[288,512]{1,0:T(8,128)(2,1)S(1)}, u32[]{:S(2)}, u32[]{:S(2)}) collective-permute-start(s16[288,512]{1,0:T(8,128)(2,1)S(1)} %get-tuple-element.30), channel_id=1, source_target_pairs={{0,2},{1,3},{2,0},{3,1},{4,6},{5,7},{6,4},{7,5},{8,10},{9,11},{10,... | collective-permute-start | bytes 884744 | tf_op jit(solution)/shard_map/ppermute | solution.py:447
  11.1 2.7 %collective-permute-start = (s16[288,512]{1,0:T(8,128)(2,1)S(1)}, s16[288,512]{1,0:T(8,128)(2,1)S(1)}, u32[]{:S(2)}, u32[]{:S(2)}) collective-permute-start(s16[288,512]{1,0:T(8,128)(2,1)S(1)} %get-tuple-element.28), channel_id=1, source_target_pairs={{0,1},{1,0},{2,3},{3,2},{4,5},{5,4},{6,7},{7,6},{8,9},{9,8},{10,11... | collective-permute-start | bytes 884744 | tf_op jit(solution)/shard_map/ppermute | solution.py:447
  13.7 2.4 %shard_map.70 = (f32[272,512]{1,0:T(8,128)S(1)}, f32[272,512]{1,0:T(8,128)S(1)}) custom-call(s32[16]{0:T(128)S(1)} %stack.51.info_ref, bf16[2048,512]{1,0:T(8,128)(2,1)S(1)} %get-tuple-element.22.x_ref, bf16[16,2048]{1,0:T(8,128)(2,1)S(1)} %get-tuple-element.23.yt_ref, s32[1,2048]{1,0:T(1,128)S(1)} %get-tuple-element.24.f_ref), custom_call_target="tpu_custom_call" | custom-call | flops 2147483648 | bytes 4194304 | tf_op jit(solution)/shard_map/pallas_call | solution.py:478
  16.2 1.6 %collective-permute-done.2.p3_ref = s16[288,512]{1,0:T(8,128)(2,1)S(1)} collective-permute-done((s16[288,512]{1,0:T(8,128)(2,1)S(1)}, s16[288,512]{1,0:T(8,128)(2,1)S(1)}, u32[]{:S(2)}, u32[]{:S(2)}) %collective-permute-start.2) | collective-permute-done | bytes 294944 | tf_op jit(solution)/shard_map/ppermute | solution.py:447
  17.8 4.2 %collective-permute-done.p1_ref = s16[288,512]{1,0:T(8,128)(2,1)S(1)} collective-permute-done((s16[288,512]{1,0:T(8,128)(2,1)S(1)}, s16[288,512]{1,0:T(8,128)(2,1)S(1)}, u32[]{:S(2)}, u32[]{:S(2)}) %collective-permute-start) | collective-permute-done | bytes 294944 | tf_op jit(solution)/shard_map/ppermute | solution.py:447
  22.0 1.4 %shard_map.71 = (s16[288,512]{1,0:T(8,128)(2,1)S(1)}, s16[288,512]{1,0:T(8,128)(2,1)S(1)}, f32[272,512]{1,0:T(8,128)S(1)}, f32[272,512]{1,0:T(8,128)S(1)}) custom-call(s32[16]{0:T(128)S(1)} %stack.51.info_ref, f32[272,512]{1,0:T(8,128)S(1)} %get-tuple-element.25.k1_ref, f32[272,512]{1,0:T(8,128)S(1)} %get-tuple-element.26.k2_ref, ...), custom_call_target="tpu_custom_call" | custom-call | bytes 4194304 | tf_op jit(solution)/shard_map/pallas_call | solution.py:478
  23.4 4.6 %collective-permute-start.3 = (s16[288,512]{1,0:T(8,128)(2,1)S(1)}, s16[288,512]{1,0:T(8,128)(2,1)S(1)}, u32[]{:S(2)}, u32[]{:S(2)}) collective-permute-start(s16[288,512]{1,0:T(8,128)(2,1)S(1)} %get-tuple-element.36), channel_id=1, source_target_pairs={{0,2},{1,3},{2,0},{4,6},{5,7},{6,4},{9,11},{10,8},{11,9},{13,15},{... | collective-permute-start | bytes 884744 | tf_op jit(solution)/shard_map/ppermute | solution.py:447
  28.0 1.3 %collective-permute-start.4 = (s16[288,512]{1,0:T(8,128)(2,1)S(1)}, s16[288,512]{1,0:T(8,128)(2,1)S(1)}, u32[]{:S(2)}, u32[]{:S(2)}) collective-permute-start(s16[288,512]{1,0:T(8,128)(2,1)S(1)} %get-tuple-element.38), channel_id=1, source_target_pairs={{1,0},{3,2},{5,4},{7,6},{8,9},{10,11},{12,13},{14,15},{17,16},{19,... | collective-permute-start | bytes 884744 | tf_op jit(solution)/shard_map/ppermute | solution.py:447
  29.3 5.8 %all-gather = bf16[256,512]{1,0:T(8,128)(2,1)S(1)} all-gather(bf16[64,512]{1,0:T(8,128)(2,1)S(1)} %bitcast.26), channel_id=2, replica_groups=mesh['blk'=4,'smp'=8] {'blk'}, dimensions={0}, use_global_device_ids=true | all-gather | bytes 327680 | tf_op jit(solution)/shard_map/all_gather | solution.py:555
  35.1 1.5 %collective-permute-done.4.p5_ref = s16[288,512]{1,0:T(8,128)(2,1)S(1)} collective-permute-done((s16[288,512]{1,0:T(8,128)(2,1)S(1)}, s16[288,512]{1,0:T(8,128)(2,1)S(1)}, u32[]{:S(2)}, u32[]{:S(2)}) %collective-permute-start.4) | collective-permute-done | bytes 294944 | tf_op jit(solution)/shard_map/ppermute | solution.py:447
  36.6 1.1 %shard_map.72 = (s16[288,512]{1,0:T(8,128)(2,1)S(1)}, f32[272,512]{1,0:T(8,128)S(1)}) custom-call(s32[16]{0:T(128)S(1)} %stack.51.info_ref, f32[272,512]{1,0:T(8,128)S(1)} %get-tuple-element.31.ka_ref, f32[272,512]{1,0:T(8,128)S(1)} %get-tuple-element.32.kb_ref, s16[288,512]{1,0:T(8,128)(2,1)S(1)} %collective-permute-done.3.p4_ref, ...), custom_call_target="tpu_custom_call" | custom-call | bytes 4194304 | tf_op jit(solution)/shard_map/pallas_call | solution.py:478
  37.7 4.7 %collective-permute-start.5 = (s16[288,512]{1,0:T(8,128)(2,1)S(1)}, s16[288,512]{1,0:T(8,128)(2,1)S(1)}, u32[]{:S(2)}, u32[]{:S(2)}) collective-permute-start(s16[288,512]{1,0:T(8,128)(2,1)S(1)} %get-tuple-element.40), channel_id=1, source_target_pairs={{0,4},{2,6},{4,0},{6,2},{7,3},{8,12},{9,13},{11,15},{13,9},{15,11}... | collective-permute-start | bytes 884744 | tf_op jit(solution)/shard_map/ppermute | solution.py:447
  42.4 7.5 %collective-permute-done.5.p_ref = s16[288,512]{1,0:T(8,128)(2,1)S(1)} collective-permute-done((s16[288,512]{1,0:T(8,128)(2,1)S(1)}, s16[288,512]{1,0:T(8,128)(2,1)S(1)}, u32[]{:S(2)}, u32[]{:S(2)}) %collective-permute-start.5) | collective-permute-done | bytes 294944 | tf_op jit(solution)/shard_map/ppermute | solution.py:447
  50.0 16.8 %shard_map.73 = bf16[8,16,512]{2,1,0:T(8,128)(2,1)S(1)} custom-call(f32[2]{0:T(128)S(1)} %broadcast_multiply_fusion.shift_ref, f32[272,512]{1,0:T(8,128)S(1)} %get-tuple-element.39.k_ref, s16[288,512]{1,0:T(8,128)(2,1)S(1)} %collective-permute-done.5.p_ref), custom_call_target="tpu_custom_call" | custom-call | bytes 4194304 | tf_op jit(solution)/shard_map/pallas_call | solution.py:478
  66.7 13.4 %all_to_all.10.b_ref = bf16[8,16,512]{2,1,0:T(8,128)(2,1)S(1)} all-to-all(bf16[8,16,512]{2,1,0:T(8,128)(2,1)S(1)} %shard_map.73), channel_id=1, replica_groups=mesh['blk'=4,'smp'=8] {'smp'}, dimensions={0} | all-to-all | bytes 262144 | tf_op jit(solution)/shard_map/all_to_all | solution.py:571
  80.1 1.3 %shard_map.74.o_ref = bf16[16,2048]{1,0:T(8,128)(2,1)S(1)} custom-call(s32[16]{0:T(128)S(1)} %stack.51.info_ref, bf16[2048,512]{1,0:T(8,128)(2,1)S(1)} %get-tuple-element.22.x_ref, bf16[8,16,512]{2,1,0:T(8,128)(2,1)S(1)} %all_to_all.10.b_ref, s32[1,2048]{1,0:T(1,128)S(1)} %get-tuple-element.24.f_ref), custom_call_target="tpu_custom_call" | custom-call | bytes 4194304 | tf_op jit(solution)/shard_map/pallas_call | solution.py:478
  81.4 5.8 %all_gather.11.j_ref = bf16[64,2048]{1,0:T(8,128)(2,1)S(1)} all-gather(bf16[16,2048]{1,0:T(8,128)(2,1)S(1)} %shard_map.74.o_ref), channel_id=1, replica_groups=mesh['blk'=4,'smp'=8] {'blk'}, dimensions={0}, use_global_device_ids=true | all-gather | bytes 327680 | tf_op jit(solution)/shard_map/all_gather | solution.py:583
  87.2 1.1 %shard_map.75 = f32[8,2,2,8]{3,2,1,0:T(2,128)} custom-call(bf16[16,2048]{1,0:T(8,128)(2,1)S(1)} %shard_map.74.o_ref, bf16[64,2048]{1,0:T(8,128)(2,1)S(1)} %all_gather.11.j_ref, bf16[4,64,512]{2,1,0:T(8,128)(2,1)S(1)} %bitcast.25), custom_call_target="tpu_custom_call" | custom-call | bytes 4194304 | tf_op jit(solution)/shard_map/pallas_call | solution.py:478
  88.2 3.3 %all-to-all-start.1 = ((f32[8,2,2,8]{3,2,1,0:T(2,128)}), f32[8,2,2,8]{3,2,1,0:T(2,128)S(1)}, u32[]{:S(2)}, u32[]{:S(2)}) async-start(f32[8,2,2,8]{3,2,1,0:T(2,128)} %shard_map.75), calls=%async_computation.1 | async-start | bytes 32768 | tf_op jit(solution)/shard_map/all_to_all | solution.py:595
  91.5 0.7 copy.9
  92.2 5.8 %all-to-all-done.1 = f32[8,2,2,8]{3,2,1,0:T(2,128)S(1)} async-done(((f32[8,2,2,8]{3,2,1,0:T(2,128)}), f32[8,2,2,8]{3,2,1,0:T(2,128)S(1)}, u32[]{:S(2)}, u32[]{:S(2)}) %all-to-all-start.1) | async-done | bytes 1056 | tf_op jit(solution)/shard_map/all_to_all | solution.py:595
  (9 shorter events, 0.7 us)
Async XLA Ops:
  6.7 9.5 %collective-permute-start.1 = (s16[288,512]{1,0:T(8,128)(2,1)S(1)}, s16[288,512]{1,0:T(8,128)(2,1)S(1)}, u32[]{:S(2)}, u32[]{:S(2)}) collective-permute-start(s16[288,512]{1,0:T(8,128)(2,1)S(1)} %get-tuple-element.29), channel_id=1, source_target_pairs={{1,0},{3,2},{5,4},{7,6},{8,9},{10,11},{12,13},{14,15},{17,16},{19,... | collective-permute-start | bytes 884744 | tf_op jit(solution)/shard_map/ppermute | solution.py:447
  8.0 9.8 %collective-permute-start.2 = (s16[288,512]{1,0:T(8,128)(2,1)S(1)}, s16[288,512]{1,0:T(8,128)(2,1)S(1)}, u32[]{:S(2)}, u32[]{:S(2)}) collective-permute-start(s16[288,512]{1,0:T(8,128)(2,1)S(1)} %get-tuple-element.30), channel_id=1, source_target_pairs={{0,2},{1,3},{2,0},{3,1},{4,6},{5,7},{6,4},{7,5},{8,10},{9,11},{10,... | collective-permute-start | bytes 884744 | tf_op jit(solution)/shard_map/ppermute | solution.py:447
  11.1 10.9 %collective-permute-start = (s16[288,512]{1,0:T(8,128)(2,1)S(1)}, s16[288,512]{1,0:T(8,128)(2,1)S(1)}, u32[]{:S(2)}, u32[]{:S(2)}) collective-permute-start(s16[288,512]{1,0:T(8,128)(2,1)S(1)} %get-tuple-element.28), channel_id=1, source_target_pairs={{0,1},{1,0},{2,3},{3,2},{4,5},{5,4},{6,7},{7,6},{8,9},{9,8},{10,11... | collective-permute-start | bytes 884744 | tf_op jit(solution)/shard_map/ppermute | solution.py:447
  16.2 13.1 %copy-start = (bf16[1,512,8,8]{1,3,2,0:T(8,128)(2,1)S(1)}, bf16[1,512,8,8]{1,3,2,0:T(8,128)(2,1)}, u32[]{:S(2)}) copy-start(bf16[1,512,8,8]{1,3,2,0:T(8,128)(2,1)} %param.9) | copy-start | bytes 196612
  22.0 20.4 %copy-start.1 = (f32[2]{0:T(128)S(1)}, f32[2]{0:T(128)}, u32[]{:S(2)}) copy-start(f32[2]{0:T(128)} %param.8) | copy-start | bytes 28
  23.4 11.7 %collective-permute-start.3 = (s16[288,512]{1,0:T(8,128)(2,1)S(1)}, s16[288,512]{1,0:T(8,128)(2,1)S(1)}, u32[]{:S(2)}, u32[]{:S(2)}) collective-permute-start(s16[288,512]{1,0:T(8,128)(2,1)S(1)} %get-tuple-element.36), channel_id=1, source_target_pairs={{0,2},{1,3},{2,0},{4,6},{5,7},{6,4},{9,11},{10,8},{11,9},{13,15},{... | collective-permute-start | bytes 884744 | tf_op jit(solution)/shard_map/ppermute | solution.py:447
  28.0 8.6 %collective-permute-start.4 = (s16[288,512]{1,0:T(8,128)(2,1)S(1)}, s16[288,512]{1,0:T(8,128)(2,1)S(1)}, u32[]{:S(2)}, u32[]{:S(2)}) collective-permute-start(s16[288,512]{1,0:T(8,128)(2,1)S(1)} %get-tuple-element.38), channel_id=1, source_target_pairs={{1,0},{3,2},{5,4},{7,6},{8,9},{10,11},{12,13},{14,15},{17,16},{19,... | collective-permute-start | bytes 884744 | tf_op jit(solution)/shard_map/ppermute | solution.py:447
  37.7 12.2 %collective-permute-start.5 = (s16[288,512]{1,0:T(8,128)(2,1)S(1)}, s16[288,512]{1,0:T(8,128)(2,1)S(1)}, u32[]{:S(2)}, u32[]{:S(2)}) collective-permute-start(s16[288,512]{1,0:T(8,128)(2,1)S(1)} %get-tuple-element.40), channel_id=1, source_target_pairs={{0,4},{2,6},{4,0},{6,2},{7,3},{8,12},{9,13},{11,15},{13,9},{15,11}... | collective-permute-start | bytes 884744 | tf_op jit(solution)/shard_map/ppermute | solution.py:447
  88.2 9.8 %all-to-all-start.1 = ((f32[8,2,2,8]{3,2,1,0:T(2,128)}), f32[8,2,2,8]{3,2,1,0:T(2,128)S(1)}, u32[]{:S(2)}, u32[]{:S(2)}) async-start(f32[8,2,2,8]{3,2,1,0:T(2,128)} %shard_map.75), calls=%async_computation.1 | async-start | bytes 32768 | tf_op jit(solution)/shard_map/all_to_all | solution.py:595

commit v6 on v5

--- a/solution.py
+++ b/solution.py
@@ -150,7 +150,7 @@
 
 
 def gram_first_kernel(
-    x_hbm, yt_hbm, f_hbm, msg_ref, x_ref, yt_ref, f_ref, work_ref, xt_ref, in_ref, sems, *, bound, fold_of, chunks
+    x_hbm, yt_hbm, f_hbm, msg_ref, x_ref, yt_ref, f_ref, work_ref, xt_ref, in_ref, sems, *, bound, roles, chunks
 ):
     rows = x_ref.shape[0] // chunks
     small = [pltpu.make_async_copy(yt_hbm, in_ref, sems.at[chunks]), pltpu.make_async_copy(f_hbm, f_ref, sems.at[chunks + 1])]
@@ -168,43 +168,45 @@
     for copy in small:
         copy.wait()
     yt_ref[...] = jnp.concatenate([in_ref[...], jnp.zeros_like(in_ref[...])], axis=0)
-    gram_one(fold_of(), x_ref, xt_ref, yt_ref, f_ref, work_ref, eye, low)
+    gram_one(roles()[0], x_ref, xt_ref, yt_ref, f_ref, work_ref, eye, low)
     encode(reader(work_ref), msg_ref, bound, eye, low)
 
 
-def gram_send_kernel(info_ref, x_ref, yt_ref, f_ref, m1_ref, m3_ref, keep_ref, work_ref, xt_ref, *, bound):
+def gram_send_kernel(x_ref, yt_ref, f_ref, m1_ref, m3_ref, keep_ref, work_ref, xt_ref, *, bound, roles):
     eye, low = square_masks()
+    info = roles()
     xt_ref[...] = x_ref[...].T
     for slot, dst, msg_ref in ((3, work_ref, m3_ref), (1, keep_ref, m1_ref)):
-        gram_one(info_ref[slot], x_ref, xt_ref, yt_ref, f_ref, dst, eye, low)
+        gram_one(info[slot], x_ref, xt_ref, yt_ref, f_ref, dst, eye, low)
         encode(reader(dst), msg_ref, bound, eye, low)
 
 
-def gram_keep_kernel(info_ref, x_ref, yt_ref, f_ref, k2_ref, k4_ref, xt_ref):
+def gram_keep_kernel(x_ref, yt_ref, f_ref, k2_ref, k4_ref, xt_ref, *, roles):
     eye, low = square_masks()
+    info = roles()
     xt_ref[...] = x_ref[...].T
     for slot, dst in ((2, k2_ref), (4, k4_ref)):
-        gram_one(info_ref[slot], x_ref, xt_ref, yt_ref, f_ref, dst, eye, low)
+        gram_one(info[slot], x_ref, xt_ref, yt_ref, f_ref, dst, eye, low)
 
 
 def second_kernel(
-    info_ref, k1_ref, k2_ref, k4_ref, p1_ref, p2_ref, p3_ref, ma_ref, mb_ref, ka_ref, kb_ref, s1_ref, s2_ref, *, bound
+    k1_ref, k2_ref, k4_ref, p1_ref, p2_ref, p3_ref, ma_ref, mb_ref, ka_ref, kb_ref, s1_ref, s2_ref, *, bound, roles
 ):
     eye, low = square_masks()
     add_message(s2_ref, k2_ref, p1_ref, bound, eye, low)
     add_message(s1_ref, k1_ref, p2_ref, bound, eye, low)
     add_message(kb_ref, k4_ref, p3_ref, bound, eye, low)
-    first = info_ref[5] == 1
+    first = roles()[5] == 1
     encode(lambda r, c: jnp.where(first, s1_ref[r, c], s2_ref[r, c]), ma_ref, bound, eye, low)
     encode(reader(kb_ref), mb_ref, bound, eye, low)
     ka_ref[...] = jnp.where(first, s2_ref[...], s1_ref[...])
 
 
-def third_kernel(info_ref, ka_ref, kb_ref, p4_ref, p5_ref, msg_ref, keep_ref, sa_ref, sb_ref, *, bound):
+def third_kernel(ka_ref, kb_ref, p4_ref, p5_ref, msg_ref, keep_ref, sa_ref, sb_ref, *, bound, roles):
     eye, low = square_masks()
     add_message(sa_ref, ka_ref, p4_ref, bound, eye, low)
     add_message(sb_ref, kb_ref, p5_ref, bound, eye, low)
-    upper = info_ref[6] == 1
+    upper = roles()[6] == 1
     encode(lambda r, c: jnp.where(upper, sa_ref[r, c], sb_ref[r, c]), msg_ref, bound, eye, low)
     keep_ref[...] = jnp.where(upper, sb_ref[...], sa_ref[...])
 
@@ -233,7 +235,12 @@
         def spread(t, q):
             return jnp.take_along_axis(t, index[q], axis=1)
 
-        c = [spread(tiles[g], q) for q in range(TILE)]
+        others = [(g + 1) % count] + [i for i in range(count) if i != g and i != (g + 1) % count]
+        lanes = [[None] * TILE for _ in range(count)]
+        for q in range(TILE):
+            for i in [g] + others:
+                lanes[i][q] = spread(tiles[i], q)
+        c = list(lanes[g])
         r = jnp.where(inside, jnp.where(col - g * TILE == sub, 1.0, 0.0), tiles[g])
         for p in range(0, TILE, 2):
             cp, cn = c[p], c[p + 1]
@@ -249,9 +256,8 @@
                 c[q] = eliminate(c[q])
             r = eliminate(r)
         rows = [sublane(r, p) for p in range(TILE)]
-        for i in [(g + 1) % count] + [i for i in range(count) if i != g and i != (g + 1) % count]:
-            t = tiles[i]
-            tiles[i] = jnp.where(inside, 0.0, t) - tree([spread(t, p) * rows[p] for p in range(TILE)])
+        for i in others:
+            tiles[i] = jnp.where(inside, 0.0, tiles[i]) - tree([lanes[i][p] * rows[p] for p in range(TILE)])
         tiles[g] = r
         yield
 
@@ -358,7 +364,7 @@
         x_ref[:, cs] = x
 
 
-def solve_kernel(shift_ref, k_ref, p_ref, o_ref, m_ref, w_ref, x_ref, *, bound):
+def solve_kernel(lambda_ref, k_ref, p_ref, o_ref, m_ref, w_ref, x_ref, *, bound, total):
     eye, low = square_masks()
     matrix, rest = decode(p_ref, bound, eye, low)
     n = BLOCK
@@ -386,7 +392,7 @@
         put(slice(n, n + 8), right[:, c * LANES : (c + 1) * LANES], c)
 
     lane, sub = iota((HALF, LANES), 1), iota((HALF, LANES), 0)
-    shift = jnp.where(lane % HALF == sub, jnp.where(lane < HALF, shift_ref[0], shift_ref[1]), 0.0)
+    shift = jnp.where(lane % HALF == sub, jnp.where(lane < HALF, lambda_ref[0] * total, lambda_ref[1] * total), 0.0)
     factor_solve(n, shift, m_ref, w_ref, x_ref)
     left = iota((8, LANES), 1) < HALF
     for c in range(4):
@@ -398,8 +404,9 @@
             o_ref[d, :, c * LANES : (c + 1) * LANES] = both
 
 
-def predict_kernel(info_ref, x_ref, b_ref, f_ref, o_ref, *, scale):
-    weights = jnp.concatenate([b_ref[info_ref[8 + k]] for k in range(FOLDS)], axis=0)
+def predict_kernel(x_ref, b_ref, f_ref, o_ref, *, scale, roles):
+    info = roles()
+    weights = jnp.concatenate([b_ref[info[7 + k]] for k in range(FOLDS)], axis=0)
     fitted = nt(weights, x_ref[...])
     folds = f_ref[...]
     total = jnp.zeros((16, folds.shape[1]), f32)
@@ -450,24 +457,6 @@
         rows = x.shape[0]
         total = rows * n_smp
         bound = BOUND * total
-        mirror = 7 * (lax.axis_index("blk") & 1)
-        role = lax.axis_index("smp") ^ mirror
-        b0, b1, b2 = role & 1, role >> 1 & 1, role >> 2
-        info = jnp.stack(
-            [
-                jnp.where(b0 == 0, 2, 0),
-                jnp.int32(1) + 0 * b0,
-                jnp.where(b0 == 0, 0, 2),
-                jnp.where(b1 == 0, 4, 3),
-                jnp.where(b1 == 0, 3, 4),
-                jnp.where(b0 == b1, 1, 0),
-                b2,
-                b2,
-            ]
-            + [o ^ mirror for o in OWNERS]
-            + [b2] * 3
-        ).astype(jnp.int32)
-        shift = lambdas * total
         yt = traits.T
         f_row = folds.reshape(1, rows)
         prior = jnp.transpose(guesses[0], (1, 2, 0)).reshape(-1, guesses.shape[1])
@@ -491,9 +480,11 @@
         def wire(*lead):
             return jax.ShapeDtypeStruct((*lead, WIRE, BLOCK), jnp.int16)
 
-        def first_fold():
-            s = lax.axis_index("smp") ^ (lax.axis_index("blk") & 1)
-            return jnp.where(s & 1 == 0, 2, 0)
+        def roles():
+            mirror = 7 * (lax.axis_index("blk") & 1)
+            role = lax.axis_index("smp") ^ mirror
+            b0, b1, b2 = role & 1, role >> 1 & 1, role >> 2
+            return [2 - 2 * b0, 1, 2 * b0, 4 - b1, 3 + b1, jnp.where(b0 == b1, 1, 0), b2] + [o ^ mirror for o in OWNERS]
 
         work = pltpu.VMEM((PACKED, BLOCK), f32)
         xt = pltpu.VMEM((BLOCK, rows), bf16)
@@ -511,7 +502,7 @@
             [work, xt, pltpu.VMEM(yt.shape, bf16), pltpu.SemaphoreType.DMA((chunks + 2,))],
             *(pltpu.with_memory_space_constraint(v, pltpu.HBM) for v in (x, yt, f_row)),
             bound=bound,
-            fold_of=first_fold,
+            roles=roles,
             chunks=chunks,
             mib=14,
             flops=gram_flops,
@@ -520,27 +511,26 @@
         m1, m3, k1 = call(
             gram_send_kernel,
             (wire(), wire(), packed()),
-            [SMEM, VMEM, VMEM, VMEM],
+            [VMEM, VMEM, VMEM],
             [work, xt],
-            info,
             x_near,
             yt_near,
             f_near,
             bound=bound,
+            roles=roles,
             mib=14,
             flops=2 * gram_flops,
         )
         p3 = move(m3, 2, lambda u, v, w: True)
         p2 = move(m1, 1, lambda u, v, w: u == 1)
         k2, k4 = call(
-            gram_keep_kernel, (packed(), packed()), [SMEM] + [VMEM] * 3, [xt], info, x_near, yt_near, f_near, mib=14, flops=2 * gram_flops
+            gram_keep_kernel, (packed(), packed()), [VMEM] * 3, [xt], x_near, yt_near, f_near, roles=roles, mib=14, flops=2 * gram_flops
         )
         ma, mb, ka, kb = call(
             second_kernel,
             (wire(), wire(), packed(), packed()),
-            [SMEM] + [VMEM] * 6,
+            [VMEM] * 6,
             [work, work],
-            info,
             k1,
             k2,
             k4,
@@ -548,6 +538,7 @@
             p2,
             p3,
             bound=bound,
+            roles=roles,
         )
         early, ma, mb = lax.optimization_barrier((prior, ma, mb))
         p4 = move(ma, 2, lambda u, v, w: (u, v) != (1, 1))
@@ -555,7 +546,7 @@
         prior_all = lax.all_gather(early, "blk", axis=0)
         prior_all, p4 = lax.optimization_barrier((prior_all, p4))
         msg, keep = call(
-            third_kernel, (wire(), packed()), [SMEM] + [VMEM] * 4, [work, work], info, ka, kb, p4, p5, bound=bound
+            third_kernel, (wire(), packed()), [VMEM] * 4, [work, work], ka, kb, p4, p5, bound=bound, roles=roles
         )
         p6 = move(msg, 4, lambda u, v, w: u == 0 or (u, v, w) == (1, 1, 1))
         beta = call(
@@ -563,22 +554,23 @@
             jax.ShapeDtypeStruct((n_smp, 16, BLOCK), bf16),
             [SMEM, VMEM, VMEM],
             [pltpu.VMEM((BLOCK + 8, 2 * BLOCK), f32), pltpu.VMEM((BLOCK + 8, 2 * BLOCK), f32), pltpu.VMEM((8, 2 * BLOCK), f32)],
-            shift,
+            lambdas,
             keep,
             p6,
             bound=bound,
+            total=float(total),
         )
         betas = lax.all_to_all(beta, "smp", 0, 0)
         oof = call(
             predict_kernel,
             jax.ShapeDtypeStruct((16, rows), bf16),
-            [SMEM, VMEM, VMEM, VMEM],
+            [VMEM, VMEM, VMEM],
             [],
-            info,
             x_near,
             betas,
             f_near,
             scale=math.sqrt(total / BLOCK),
+            roles=roles,
         )
         oof_all = lax.all_gather(oof, "blk", axis=0, tiled=True)
         n_cross = prior.shape[0] // 8 + 2 * n_blk

time: 99 us -> 93.6 us (0.945)
  Pallas kernels: 29.9 us -> 26.8 us
  starting transfers between devices: 20.9 us -> 18.9 us
    pallas_call x8, Pallas kernels: 29.9 us -> 26.8 us  [call(): pl.pallas_call(functools.partial(kernel, **static), out_shape=outs, in_sp...]
    ppermute x6, starting transfers between devices: 17.6 us -> 15.6 us  [move(): return lax.ppermute(x, ('blk', 'smp'), pairs(bit, sends))]
  transfers between devices with their start and end apart: 7 -> 7, of which waited for: 5 -> 6; matrix products, arithmetic and copies ran while one was open for 1% -> 1% of each run, Pallas kernels for 2% -> 4%
where the time goes in v6:
time: 93.6 us; the launch traced here: 93.2 us
  Pallas kernels  26.8 us (29%)
  blocking collectives  24.7 us (26%)
  waiting for transfers between devices  20.7 us (22%)
  starting transfers between devices  18.9 us (20%)
    pallas_call x8, Pallas kernels, call(): pl.pallas_call(functools.partial(kernel, **static), out_shape=outs, in_sp...  26.8 us
    ppermute x6, starting transfers between devices, move(): return lax.ppermute(x, ('blk', 'smp'), pairs(bit, sends))  15.6 us
    ppermute x6, waiting for transfers between devices, move(): return lax.ppermute(x, ('blk', 'smp'), pairs(bit, sends))  14.9 us
    all_to_all x1, blocking collectives, local(): betas = lax.all_to_all(beta, 'smp', 0, 0)  13.2 us
    all_to_all x1, waiting for transfers between devices, local(): cross = jnp.sum(lax.all_to_all(part, 'smp', 0, 0), axis=0)  5.81 us
    all_gather x1, blocking collectives, local(): prior_all = lax.all_gather(early, 'blk', axis=0)  5.78 us
    all_gather x1, blocking collectives, local(): oof_all = lax.all_gather(oof, 'blk', axis=0, tiled=True)  5.78 us
    all_to_all x1, starting transfers between devices, local(): cross = jnp.sum(lax.all_to_all(part, 'smp', 0, 0), axis=0)  3.31 us
  transfers between devices with their start and end apart: 7, of which 6 were waited for; matrix products, arithmetic and copies ran while one was open for 1% of the time, Pallas kernels for 4%

profile of v6, /device:TPU:0, one launch (start us, length us, event | category | flops | bytes accessed | tf_op | source)
XLA Modules:
  0.0 93.2 jit_solution(2217384656554493902)
XLA Ops:
  0.6 3.1 %shard_map.68 = (s16[288,512]{1,0:T(8,128)(2,1)S(1)}, bf16[2048,512]{1,0:T(8,128)(2,1)S(1)}, bf16[16,2048]{1,0:T(8,128)(2,1)S(1)}, s32[1,2048]{1,0:T(1,128)S(1)}) custom-call(bf16[2048,512]{1,0:T(8,128)(2,1)} %x_hbm.1, bf16[8,2048]{1,0:T(8,128)(2,1)} %bitcast.18, s32[1,2048]{1,0:T(1,128)} %bitcast.19), custom_call_target="tpu_custom_call" | custom-call | flops 1073741824 | bytes 4194304 | tf_op jit(solution)/shard_map/pallas_call | solution.py:467
  3.8 3.1 %collective-permute-start = (s16[288,512]{1,0:T(8,128)(2,1)S(1)}, s16[288,512]{1,0:T(8,128)(2,1)S(1)}, u32[]{:S(2)}, u32[]{:S(2)}) collective-permute-start(s16[288,512]{1,0:T(8,128)(2,1)S(1)} %get-tuple-element.28), channel_id=1, source_target_pairs={{0,1},{1,0},{2,3},{3,2},{4,5},{5,4},{6,7},{7,6},{8,9},{9,8},{10,11... | collective-permute-start | bytes 884744 | tf_op jit(solution)/shard_map/ppermute | solution.py:454
  6.9 2.2 %shard_map.69 = (s16[288,512]{1,0:T(8,128)(2,1)S(1)}, s16[288,512]{1,0:T(8,128)(2,1)S(1)}, f32[272,512]{1,0:T(8,128)S(1)}) custom-call(bf16[2048,512]{1,0:T(8,128)(2,1)S(1)} %get-tuple-element.22.x_ref, bf16[16,2048]{1,0:T(8,128)(2,1)S(1)} %get-tuple-element.23.yt_ref, s32[1,2048]{1,0:T(1,128)S(1)} %get-tuple-element.24.f_ref), custom_call_target="tpu_custom_call" | custom-call | flops 2147483648 | bytes 4194304 | tf_op jit(solution)/shard_map/pallas_call | solution.py:467
  9.1 1.3 %collective-permute-start.1 = (s16[288,512]{1,0:T(8,128)(2,1)S(1)}, s16[288,512]{1,0:T(8,128)(2,1)S(1)}, u32[]{:S(2)}, u32[]{:S(2)}) collective-permute-start(s16[288,512]{1,0:T(8,128)(2,1)S(1)} %get-tuple-element.29), channel_id=1, source_target_pairs={{1,0},{3,2},{5,4},{7,6},{8,9},{10,11},{12,13},{14,15},{17,16},{19,... | collective-permute-start | bytes 884744 | tf_op jit(solution)/shard_map/ppermute | solution.py:454
  10.4 1.6 %collective-permute-start.2 = (s16[288,512]{1,0:T(8,128)(2,1)S(1)}, s16[288,512]{1,0:T(8,128)(2,1)S(1)}, u32[]{:S(2)}, u32[]{:S(2)}) collective-permute-start(s16[288,512]{1,0:T(8,128)(2,1)S(1)} %get-tuple-element.30), channel_id=1, source_target_pairs={{0,2},{1,3},{2,0},{3,1},{4,6},{5,7},{6,4},{7,5},{8,10},{9,11},{10,... | collective-permute-start | bytes 884744 | tf_op jit(solution)/shard_map/ppermute | solution.py:454
  12.0 1.9 %shard_map.70 = (f32[272,512]{1,0:T(8,128)S(1)}, f32[272,512]{1,0:T(8,128)S(1)}) custom-call(bf16[2048,512]{1,0:T(8,128)(2,1)S(1)} %get-tuple-element.22.x_ref, bf16[16,2048]{1,0:T(8,128)(2,1)S(1)} %get-tuple-element.23.yt_ref, s32[1,2048]{1,0:T(1,128)S(1)} %get-tuple-element.24.f_ref), custom_call_target="tpu_custom_call" | custom-call | flops 2147483648 | bytes 4194304 | tf_op jit(solution)/shard_map/pallas_call | solution.py:467
  14.3 3.4 %collective-permute-done.1.p2_ref = s16[288,512]{1,0:T(8,128)(2,1)S(1)} collective-permute-done((s16[288,512]{1,0:T(8,128)(2,1)S(1)}, s16[288,512]{1,0:T(8,128)(2,1)S(1)}, u32[]{:S(2)}, u32[]{:S(2)}) %collective-permute-start.1) | collective-permute-done | bytes 294944 | tf_op jit(solution)/shard_map/ppermute | solution.py:454
  17.7 1.9 %collective-permute-done.2.p3_ref = s16[288,512]{1,0:T(8,128)(2,1)S(1)} collective-permute-done((s16[288,512]{1,0:T(8,128)(2,1)S(1)}, s16[288,512]{1,0:T(8,128)(2,1)S(1)}, u32[]{:S(2)}, u32[]{:S(2)}) %collective-permute-start.2) | collective-permute-done | bytes 294944 | tf_op jit(solution)/shard_map/ppermute | solution.py:454
  19.6 0.9 shard_map.71
  20.4 3.6 %collective-permute-start.3 = (s16[288,512]{1,0:T(8,128)(2,1)S(1)}, s16[288,512]{1,0:T(8,128)(2,1)S(1)}, u32[]{:S(2)}, u32[]{:S(2)}) collective-permute-start(s16[288,512]{1,0:T(8,128)(2,1)S(1)} %get-tuple-element.36), channel_id=1, source_target_pairs={{0,2},{1,3},{2,0},{4,6},{5,7},{6,4},{9,11},{10,8},{11,9},{13,15},{... | collective-permute-start | bytes 884744 | tf_op jit(solution)/shard_map/ppermute | solution.py:454
  24.1 1.3 %collective-permute-start.4 = (s16[288,512]{1,0:T(8,128)(2,1)S(1)}, s16[288,512]{1,0:T(8,128)(2,1)S(1)}, u32[]{:S(2)}, u32[]{:S(2)}) collective-permute-start(s16[288,512]{1,0:T(8,128)(2,1)S(1)} %get-tuple-element.38), channel_id=1, source_target_pairs={{1,0},{3,2},{5,4},{7,6},{8,9},{10,11},{12,13},{14,15},{17,16},{19,... | collective-permute-start | bytes 884744 | tf_op jit(solution)/shard_map/ppermute | solution.py:454
  25.4 5.8 %all-gather = bf16[256,512]{1,0:T(8,128)(2,1)S(1)} all-gather(bf16[64,512]{1,0:T(8,128)(2,1)S(1)} %bitcast.15), channel_id=2, replica_groups=mesh['blk'=4,'smp'=8] {'blk'}, dimensions={0}, use_global_device_ids=true | all-gather | bytes 327680 | tf_op jit(solution)/shard_map/all_gather | solution.py:546
  31.2 1.5 %collective-permute-done.4.p5_ref = s16[288,512]{1,0:T(8,128)(2,1)S(1)} collective-permute-done((s16[288,512]{1,0:T(8,128)(2,1)S(1)}, s16[288,512]{1,0:T(8,128)(2,1)S(1)}, u32[]{:S(2)}, u32[]{:S(2)}) %collective-permute-start.4) | collective-permute-done | bytes 294944 | tf_op jit(solution)/shard_map/ppermute | solution.py:454
  33.2 4.7 %collective-permute-start.5 = (s16[288,512]{1,0:T(8,128)(2,1)S(1)}, s16[288,512]{1,0:T(8,128)(2,1)S(1)}, u32[]{:S(2)}, u32[]{:S(2)}) collective-permute-start(s16[288,512]{1,0:T(8,128)(2,1)S(1)} %get-tuple-element.40), channel_id=1, source_target_pairs={{0,4},{2,6},{4,0},{6,2},{7,3},{8,12},{9,13},{11,15},{13,9},{15,11}... | collective-permute-start | bytes 884744 | tf_op jit(solution)/shard_map/ppermute | solution.py:454
  37.9 7.7 %collective-permute-done.5.p_ref = s16[288,512]{1,0:T(8,128)(2,1)S(1)} collective-permute-done((s16[288,512]{1,0:T(8,128)(2,1)S(1)}, s16[288,512]{1,0:T(8,128)(2,1)S(1)}, u32[]{:S(2)}, u32[]{:S(2)}) %collective-permute-start.5) | collective-permute-done | bytes 294944 | tf_op jit(solution)/shard_map/ppermute | solution.py:454
  45.7 16.3 %shard_map.73 = bf16[8,16,512]{2,1,0:T(8,128)(2,1)S(1)} custom-call(f32[2]{0:T(128)S(1)} %copy-done, f32[272,512]{1,0:T(8,128)S(1)} %get-tuple-element.39.k_ref, s16[288,512]{1,0:T(8,128)(2,1)S(1)} %collective-permute-done.5.p_ref), custom_call_target="tpu_custom_call" | custom-call | bytes 4194304 | tf_op jit(solution)/shard_map/pallas_call | solution.py:467
  62.0 13.2 %all_to_all.10.b_ref = bf16[8,16,512]{2,1,0:T(8,128)(2,1)S(1)} all-to-all(bf16[8,16,512]{2,1,0:T(8,128)(2,1)S(1)} %shard_map.73), channel_id=1, replica_groups=mesh['blk'=4,'smp'=8] {'smp'}, dimensions={0} | all-to-all | bytes 262144 | tf_op jit(solution)/shard_map/all_to_all | solution.py:563
  75.2 0.8 shard_map.74.o_ref
  76.0 5.8 %all_gather.11.j_ref = bf16[64,2048]{1,0:T(8,128)(2,1)S(1)} all-gather(bf16[16,2048]{1,0:T(8,128)(2,1)S(1)} %shard_map.74.o_ref), channel_id=1, replica_groups=mesh['blk'=4,'smp'=8] {'blk'}, dimensions={0}, use_global_device_ids=true | all-gather | bytes 327680 | tf_op jit(solution)/shard_map/all_gather | solution.py:575
  81.7 1.1 %shard_map.75 = f32[8,2,2,8]{3,2,1,0:T(2,128)} custom-call(bf16[16,2048]{1,0:T(8,128)(2,1)S(1)} %shard_map.74.o_ref, bf16[64,2048]{1,0:T(8,128)(2,1)S(1)} %all_gather.11.j_ref, bf16[4,64,512]{2,1,0:T(8,128)(2,1)S(1)} %bitcast.14), custom_call_target="tpu_custom_call" | custom-call | bytes 4194304 | tf_op jit(solution)/shard_map/pallas_call | solution.py:467
  82.8 3.3 %all-to-all-start.1 = ((f32[8,2,2,8]{3,2,1,0:T(2,128)}), f32[8,2,2,8]{3,2,1,0:T(2,128)S(1)}, u32[]{:S(2)}, u32[]{:S(2)}) async-start(f32[8,2,2,8]{3,2,1,0:T(2,128)} %shard_map.75), calls=%async_computation.1 | async-start | bytes 32768 | tf_op jit(solution)/shard_map/all_to_all | solution.py:587
  86.1 0.7 copy.9
  86.8 5.8 %all-to-all-done.1 = f32[8,2,2,8]{3,2,1,0:T(2,128)S(1)} async-done(((f32[8,2,2,8]{3,2,1,0:T(2,128)}), f32[8,2,2,8]{3,2,1,0:T(2,128)S(1)}, u32[]{:S(2)}, u32[]{:S(2)}) %all-to-all-start.1) | async-done | bytes 1056 | tf_op jit(solution)/shard_map/all_to_all | solution.py:587
  92.6 0.6 reduce_sum.9
  (7 shorter events, 0.9 us)
Async XLA Ops:
  3.8 10.5 %collective-permute-start = (s16[288,512]{1,0:T(8,128)(2,1)S(1)}, s16[288,512]{1,0:T(8,128)(2,1)S(1)}, u32[]{:S(2)}, u32[]{:S(2)}) collective-permute-start(s16[288,512]{1,0:T(8,128)(2,1)S(1)} %get-tuple-element.28), channel_id=1, source_target_pairs={{0,1},{1,0},{2,3},{3,2},{4,5},{5,4},{6,7},{7,6},{8,9},{9,8},{10,11... | collective-permute-start | bytes 884744 | tf_op jit(solution)/shard_map/ppermute | solution.py:454
  9.1 8.6 %collective-permute-start.1 = (s16[288,512]{1,0:T(8,128)(2,1)S(1)}, s16[288,512]{1,0:T(8,128)(2,1)S(1)}, u32[]{:S(2)}, u32[]{:S(2)}) collective-permute-start(s16[288,512]{1,0:T(8,128)(2,1)S(1)} %get-tuple-element.29), channel_id=1, source_target_pairs={{1,0},{3,2},{5,4},{7,6},{8,9},{10,11},{12,13},{14,15},{17,16},{19,... | collective-permute-start | bytes 884744 | tf_op jit(solution)/shard_map/ppermute | solution.py:454
  10.4 9.2 %collective-permute-start.2 = (s16[288,512]{1,0:T(8,128)(2,1)S(1)}, s16[288,512]{1,0:T(8,128)(2,1)S(1)}, u32[]{:S(2)}, u32[]{:S(2)}) collective-permute-start(s16[288,512]{1,0:T(8,128)(2,1)S(1)} %get-tuple-element.30), channel_id=1, source_target_pairs={{0,2},{1,3},{2,0},{3,1},{4,6},{5,7},{6,4},{7,5},{8,10},{9,11},{10,... | collective-permute-start | bytes 884744 | tf_op jit(solution)/shard_map/ppermute | solution.py:454
  13.9 11.5 %copy-start.1 = (bf16[1,512,8,8]{1,3,2,0:T(8,128)(2,1)S(1)}, bf16[1,512,8,8]{1,3,2,0:T(8,128)(2,1)}, u32[]{:S(2)}) copy-start(bf16[1,512,8,8]{1,3,2,0:T(8,128)(2,1)} %param.9) | copy-start | bytes 196612
  19.6 26.1 %copy-start = (f32[2]{0:T(128)S(1)}, f32[2]{0:T(128)}, u32[]{:S(2)}) copy-start(f32[2]{0:T(128)} %lambda_ref.1) | copy-start | bytes 28
  20.4 10.7 %collective-permute-start.3 = (s16[288,512]{1,0:T(8,128)(2,1)S(1)}, s16[288,512]{1,0:T(8,128)(2,1)S(1)}, u32[]{:S(2)}, u32[]{:S(2)}) collective-permute-start(s16[288,512]{1,0:T(8,128)(2,1)S(1)} %get-tuple-element.36), channel_id=1, source_target_pairs={{0,2},{1,3},{2,0},{4,6},{5,7},{6,4},{9,11},{10,8},{11,9},{13,15},{... | collective-permute-start | bytes 884744 | tf_op jit(solution)/shard_map/ppermute | solution.py:454
  24.1 8.6 %collective-permute-start.4 = (s16[288,512]{1,0:T(8,128)(2,1)S(1)}, s16[288,512]{1,0:T(8,128)(2,1)S(1)}, u32[]{:S(2)}, u32[]{:S(2)}) collective-permute-start(s16[288,512]{1,0:T(8,128)(2,1)S(1)} %get-tuple-element.38), channel_id=1, source_target_pairs={{1,0},{3,2},{5,4},{7,6},{8,9},{10,11},{12,13},{14,15},{17,16},{19,... | collective-permute-start | bytes 884744 | tf_op jit(solution)/shard_map/ppermute | solution.py:454
  33.2 12.4 %collective-permute-start.5 = (s16[288,512]{1,0:T(8,128)(2,1)S(1)}, s16[288,512]{1,0:T(8,128)(2,1)S(1)}, u32[]{:S(2)}, u32[]{:S(2)}) collective-permute-start(s16[288,512]{1,0:T(8,128)(2,1)S(1)} %get-tuple-element.40), channel_id=1, source_target_pairs={{0,4},{2,6},{4,0},{6,2},{7,3},{8,12},{9,13},{11,15},{13,9},{15,11}... | collective-permute-start | bytes 884744 | tf_op jit(solution)/shard_map/ppermute | solution.py:454
  82.8 9.8 %all-to-all-start.1 = ((f32[8,2,2,8]{3,2,1,0:T(2,128)}), f32[8,2,2,8]{3,2,1,0:T(2,128)S(1)}, u32[]{:S(2)}, u32[]{:S(2)}) async-start(f32[8,2,2,8]{3,2,1,0:T(2,128)} %shard_map.75), calls=%async_computation.1 | async-start | bytes 32768 | tf_op jit(solution)/shard_map/all_to_all | solution.py:587

commit v7 on v6

--- a/solution.py
+++ b/solution.py
@@ -14,7 +14,7 @@
 TILE = 8
 HALF = 64
 PACKED = 272
-WIRE = 288
+WIRE = 272
 DIGIT = 32766.0
 BOUND = 36.0
 OWNERS = (0, 2, 3, 4, 6)
@@ -22,7 +22,6 @@
 f32 = jnp.float32
 bf16 = jnp.bfloat16
 VMEM = pl.BlockSpec(memory_space=pltpu.VMEM)
-SMEM = pl.BlockSpec(memory_space=pltpu.SMEM)
 HBM = pl.BlockSpec(memory_space=pltpu.HBM)
 MIB = 1024 * 1024
 
@@ -87,15 +86,20 @@
         for c in range(4):
             rs, cs = place(r, c)
             msg_ref[rs, cs] = to_int(get(rs, cs) * (pair_scale(r, c, rows, cols, low) * DIGIT))
-    xh, xl = digits(get(slice(256, 264), slice(0, BLOCK)), bound)
-    msg_ref[256:272, :] = to_int(jnp.concatenate([xh, xl], axis=0))
-    spare = jnp.zeros((14, BLOCK), f32)
-    msg_ref[272:288, :] = to_int(jnp.concatenate([dh, dl, spare], axis=0))
+    xy = get(slice(256, 264), slice(0, BLOCK)) * scale
+    mh, ml = digits(jnp.max(jnp.abs(xy), axis=1, keepdims=True), bound)
+    ml = jnp.floor(ml + 0.5)
+    xy = xy * (DIGIT / (undigits(mh, ml, bound) + 1e-2))
+    wide = [jnp.broadcast_to(v, (TILE, LANES)) for v in (mh, ml)]
+    deep = [jnp.concatenate([*split(v), jnp.zeros((4, LANES), f32)], axis=0) for v in (dh, dl)]
+    msg_ref[256:272, :] = to_int(jnp.concatenate([xy, jnp.concatenate(wide + deep, axis=1)], axis=0))
 
 
 def decode(msg_ref, bound, eye, low):
-    tail = msg_ref[272:288, :].astype(f32)
-    diag = undigits(tail[0:1], tail[1:2], bound)
+    tail = msg_ref[256:272, :].astype(f32)
+    top = undigits(tail[8:16, 0:LANES], tail[8:16, LANES : 2 * LANES], bound)
+    deep = undigits(tail[8:12, 2 * LANES : 3 * LANES], tail[8:12, 3 * LANES : 4 * LANES], bound)
+    diag = jnp.concatenate([deep[i : i + 1] for i in range(4)], axis=1)
     scale = jnp.sqrt(diag + 1e-3)
     rows = split(scale)
     cols = [column(r, eye) for r in rows]
@@ -105,8 +109,7 @@
         return msg_ref[rs, cs].astype(f32) * (pair_scale(r, c, rows, cols, low) * (1.0 / DIGIT))
 
     def rest():
-        x = msg_ref[256:272, :].astype(f32)
-        return undigits(x[0:8], x[8:16], bound), diag
+        return tail[0:8] * ((top[:, 0:1] + 1e-2) * (1.0 / DIGIT)) * scale, diag
 
     return matrix, rest
 
@@ -392,7 +395,7 @@
         put(slice(n, n + 8), right[:, c * LANES : (c + 1) * LANES], c)
 
     lane, sub = iota((HALF, LANES), 1), iota((HALF, LANES), 0)
-    shift = jnp.where(lane % HALF == sub, jnp.where(lane < HALF, lambda_ref[0] * total, lambda_ref[1] * total), 0.0)
+    shift = jnp.where(lane % HALF == sub, jnp.where(lane < HALF, lambda_ref[0:1, 0:1] * total, lambda_ref[0:1, 1:2] * total), 0.0)
     factor_solve(n, shift, m_ref, w_ref, x_ref)
     left = iota((8, LANES), 1) < HALF
     for c in range(4):
@@ -552,9 +555,9 @@
         beta = call(
             solve_kernel,
             jax.ShapeDtypeStruct((n_smp, 16, BLOCK), bf16),
-            [SMEM, VMEM, VMEM],
+            [VMEM, VMEM, VMEM],
             [pltpu.VMEM((BLOCK + 8, 2 * BLOCK), f32), pltpu.VMEM((BLOCK + 8, 2 * BLOCK), f32), pltpu.VMEM((8, 2 * BLOCK), f32)],
-            lambdas,
+            lambdas.reshape(1, -1),
             keep,
             p6,
             bound=bound,

time: 93.6 us -> 92.2 us (0.985)
  transfers between devices with their start and end apart: 7 -> 7, of which waited for: 6 -> 5; matrix products, arithmetic and copies ran while one was open for 1% -> 1% of each run, Pallas kernels for 4% -> 4%
where the time goes in v7:
time: 92.2 us; the launch traced here: 91.9 us
  Pallas kernels  26.3 us (29%)
  blocking collectives  24.8 us (27%)
  waiting for transfers between devices  19.8 us (21%)
  starting transfers between devices  18.9 us (20%)
    pallas_call x8, Pallas kernels, call(): pl.pallas_call(functools.partial(kernel, **static), out_shape=outs, in_sp...  26.3 us
    ppermute x6, starting transfers between devices, move(): return lax.ppermute(x, ('blk', 'smp'), pairs(bit, sends))  15.6 us
    ppermute x6, waiting for transfers between devices, move(): return lax.ppermute(x, ('blk', 'smp'), pairs(bit, sends))  14 us
    all_to_all x1, blocking collectives, local(): betas = lax.all_to_all(beta, 'smp', 0, 0)  13.2 us
    all_to_all x1, waiting for transfers between devices, local(): cross = jnp.sum(lax.all_to_all(part, 'smp', 0, 0), axis=0)  5.81 us
    all_gather x1, blocking collectives, local(): prior_all = lax.all_gather(early, 'blk', axis=0)  5.78 us
    all_gather x1, blocking collectives, local(): oof_all = lax.all_gather(oof, 'blk', axis=0, tiled=True)  5.78 us
    all_to_all x1, starting transfers between devices, local(): cross = jnp.sum(lax.all_to_all(part, 'smp', 0, 0), axis=0)  3.31 us
  transfers between devices with their start and end apart: 7, of which 5 were waited for; matrix products, arithmetic and copies ran while one was open for 1% of the time, Pallas kernels for 4%

profile of v7, /device:TPU:0, one launch (start us, length us, event | category | flops | bytes accessed | tf_op | source)
XLA Modules:
  0.0 91.9 jit_solution(15030977572528693739)
XLA Ops:
  0.6 3.1 %shard_map.68 = (s16[272,512]{1,0:T(8,128)(2,1)S(1)}, bf16[2048,512]{1,0:T(8,128)(2,1)S(1)}, bf16[16,2048]{1,0:T(8,128)(2,1)S(1)}, s32[1,2048]{1,0:T(1,128)S(1)}) custom-call(bf16[2048,512]{1,0:T(8,128)(2,1)} %x_hbm.1, bf16[8,2048]{1,0:T(8,128)(2,1)} %bitcast.20, s32[1,2048]{1,0:T(1,128)} %bitcast.21), custom_call_target="tpu_custom_call" | custom-call | flops 1073741824 | bytes 4194304 | tf_op jit(solution)/shard_map/pallas_call | solution.py:470
  3.8 3.1 %collective-permute-start = (s16[272,512]{1,0:T(8,128)(2,1)S(1)}, s16[272,512]{1,0:T(8,128)(2,1)S(1)}, u32[]{:S(2)}, u32[]{:S(2)}) collective-permute-start(s16[272,512]{1,0:T(8,128)(2,1)S(1)} %get-tuple-element.28), channel_id=1, source_target_pairs={{0,1},{1,0},{2,3},{3,2},{4,5},{5,4},{6,7},{7,6},{8,9},{9,8},{10,11... | collective-permute-start | bytes 835592 | tf_op jit(solution)/shard_map/ppermute | solution.py:457
  6.8 2.2 %shard_map.69 = (s16[272,512]{1,0:T(8,128)(2,1)S(1)}, s16[272,512]{1,0:T(8,128)(2,1)S(1)}, f32[272,512]{1,0:T(8,128)S(1)}) custom-call(bf16[2048,512]{1,0:T(8,128)(2,1)S(1)} %get-tuple-element.22.x_ref, bf16[16,2048]{1,0:T(8,128)(2,1)S(1)} %get-tuple-element.23.yt_ref, s32[1,2048]{1,0:T(1,128)S(1)} %get-tuple-element.24.f_ref), custom_call_target="tpu_custom_call" | custom-call | flops 2147483648 | bytes 4194304 | tf_op jit(solution)/shard_map/pallas_call | solution.py:470
  9.1 1.3 %collective-permute-start.1 = (s16[272,512]{1,0:T(8,128)(2,1)S(1)}, s16[272,512]{1,0:T(8,128)(2,1)S(1)}, u32[]{:S(2)}, u32[]{:S(2)}) collective-permute-start(s16[272,512]{1,0:T(8,128)(2,1)S(1)} %get-tuple-element.29), channel_id=1, source_target_pairs={{1,0},{3,2},{5,4},{7,6},{8,9},{10,11},{12,13},{14,15},{17,16},{19,... | collective-permute-start | bytes 835592 | tf_op jit(solution)/shard_map/ppermute | solution.py:457
  10.4 1.6 %collective-permute-start.2 = (s16[272,512]{1,0:T(8,128)(2,1)S(1)}, s16[272,512]{1,0:T(8,128)(2,1)S(1)}, u32[]{:S(2)}, u32[]{:S(2)}) collective-permute-start(s16[272,512]{1,0:T(8,128)(2,1)S(1)} %get-tuple-element.30), channel_id=1, source_target_pairs={{0,2},{1,3},{2,0},{3,1},{4,6},{5,7},{6,4},{7,5},{8,10},{9,11},{10,... | collective-permute-start | bytes 835592 | tf_op jit(solution)/shard_map/ppermute | solution.py:457
  12.0 1.9 %shard_map.70 = (f32[272,512]{1,0:T(8,128)S(1)}, f32[272,512]{1,0:T(8,128)S(1)}) custom-call(bf16[2048,512]{1,0:T(8,128)(2,1)S(1)} %get-tuple-element.22.x_ref, bf16[16,2048]{1,0:T(8,128)(2,1)S(1)} %get-tuple-element.23.yt_ref, s32[1,2048]{1,0:T(1,128)S(1)} %get-tuple-element.24.f_ref), custom_call_target="tpu_custom_call" | custom-call | flops 2147483648 | bytes 4194304 | tf_op jit(solution)/shard_map/pallas_call | solution.py:470
  13.9 3.6 %collective-permute-done.1.p2_ref = s16[272,512]{1,0:T(8,128)(2,1)S(1)} collective-permute-done((s16[272,512]{1,0:T(8,128)(2,1)S(1)}, s16[272,512]{1,0:T(8,128)(2,1)S(1)}, u32[]{:S(2)}, u32[]{:S(2)}) %collective-permute-start.1) | collective-permute-done | bytes 278560 | tf_op jit(solution)/shard_map/ppermute | solution.py:457
  17.5 1.7 %collective-permute-done.2.p3_ref = s16[272,512]{1,0:T(8,128)(2,1)S(1)} collective-permute-done((s16[272,512]{1,0:T(8,128)(2,1)S(1)}, s16[272,512]{1,0:T(8,128)(2,1)S(1)}, u32[]{:S(2)}, u32[]{:S(2)}) %collective-permute-start.2) | collective-permute-done | bytes 278560 | tf_op jit(solution)/shard_map/ppermute | solution.py:457
  19.2 0.9 shard_map.71
  20.1 3.6 %collective-permute-start.3 = (s16[272,512]{1,0:T(8,128)(2,1)S(1)}, s16[272,512]{1,0:T(8,128)(2,1)S(1)}, u32[]{:S(2)}, u32[]{:S(2)}) collective-permute-start(s16[272,512]{1,0:T(8,128)(2,1)S(1)} %get-tuple-element.36), channel_id=1, source_target_pairs={{0,2},{1,3},{2,0},{4,6},{5,7},{6,4},{9,11},{10,8},{11,9},{13,15},{... | collective-permute-start | bytes 835592 | tf_op jit(solution)/shard_map/ppermute | solution.py:457
  23.8 1.3 %collective-permute-start.4 = (s16[272,512]{1,0:T(8,128)(2,1)S(1)}, s16[272,512]{1,0:T(8,128)(2,1)S(1)}, u32[]{:S(2)}, u32[]{:S(2)}) collective-permute-start(s16[272,512]{1,0:T(8,128)(2,1)S(1)} %get-tuple-element.38), channel_id=1, source_target_pairs={{1,0},{3,2},{5,4},{7,6},{8,9},{10,11},{12,13},{14,15},{17,16},{19,... | collective-permute-start | bytes 835592 | tf_op jit(solution)/shard_map/ppermute | solution.py:457
  25.1 5.8 %all-gather = bf16[256,512]{1,0:T(8,128)(2,1)S(1)} all-gather(bf16[64,512]{1,0:T(8,128)(2,1)S(1)} %bitcast.17), channel_id=2, replica_groups=mesh['blk'=4,'smp'=8] {'blk'}, dimensions={0}, use_global_device_ids=true | all-gather | bytes 327680 | tf_op jit(solution)/shard_map/all_gather | solution.py:549
  30.9 1.3 %collective-permute-done.4.p5_ref = s16[272,512]{1,0:T(8,128)(2,1)S(1)} collective-permute-done((s16[272,512]{1,0:T(8,128)(2,1)S(1)}, s16[272,512]{1,0:T(8,128)(2,1)S(1)}, u32[]{:S(2)}, u32[]{:S(2)}) %collective-permute-start.4) | collective-permute-done | bytes 278560 | tf_op jit(solution)/shard_map/ppermute | solution.py:457
  32.8 4.7 %collective-permute-start.5 = (s16[272,512]{1,0:T(8,128)(2,1)S(1)}, s16[272,512]{1,0:T(8,128)(2,1)S(1)}, u32[]{:S(2)}, u32[]{:S(2)}) collective-permute-start(s16[272,512]{1,0:T(8,128)(2,1)S(1)} %get-tuple-element.40), channel_id=1, source_target_pairs={{0,4},{2,6},{4,0},{6,2},{7,3},{8,12},{9,13},{11,15},{13,9},{15,11}... | collective-permute-start | bytes 835592 | tf_op jit(solution)/shard_map/ppermute | solution.py:457
  37.4 7.4 %collective-permute-done.5.p_ref = s16[272,512]{1,0:T(8,128)(2,1)S(1)} collective-permute-done((s16[272,512]{1,0:T(8,128)(2,1)S(1)}, s16[272,512]{1,0:T(8,128)(2,1)S(1)}, u32[]{:S(2)}, u32[]{:S(2)}) %collective-permute-start.5) | collective-permute-done | bytes 278560 | tf_op jit(solution)/shard_map/ppermute | solution.py:457
  44.8 15.8 %shard_map.73 = bf16[8,16,512]{2,1,0:T(8,128)(2,1)S(1)} custom-call(f32[1,2]{1,0:T(1,128)S(1)} %bitcast.16, f32[272,512]{1,0:T(8,128)S(1)} %get-tuple-element.39.k_ref, s16[272,512]{1,0:T(8,128)(2,1)S(1)} %collective-permute-done.5.p_ref), custom_call_target="tpu_custom_call" | custom-call | bytes 4194304 | tf_op jit(solution)/shard_map/pallas_call | solution.py:470
  60.6 13.2 %all_to_all.10.b_ref = bf16[8,16,512]{2,1,0:T(8,128)(2,1)S(1)} all-to-all(bf16[8,16,512]{2,1,0:T(8,128)(2,1)S(1)} %shard_map.73), channel_id=1, replica_groups=mesh['blk'=4,'smp'=8] {'smp'}, dimensions={0} | all-to-all | bytes 262144 | tf_op jit(solution)/shard_map/all_to_all | solution.py:566
  73.8 0.8 shard_map.74.o_ref
  74.6 5.8 %all_gather.11.j_ref = bf16[64,2048]{1,0:T(8,128)(2,1)S(1)} all-gather(bf16[16,2048]{1,0:T(8,128)(2,1)S(1)} %shard_map.74.o_ref), channel_id=1, replica_groups=mesh['blk'=4,'smp'=8] {'blk'}, dimensions={0}, use_global_device_ids=true | all-gather | bytes 327680 | tf_op jit(solution)/shard_map/all_gather | solution.py:578
  80.4 1.1 %shard_map.75 = f32[8,2,2,8]{3,2,1,0:T(2,128)} custom-call(bf16[16,2048]{1,0:T(8,128)(2,1)S(1)} %shard_map.74.o_ref, bf16[64,2048]{1,0:T(8,128)(2,1)S(1)} %all_gather.11.j_ref, bf16[4,64,512]{2,1,0:T(8,128)(2,1)S(1)} %bitcast.15), custom_call_target="tpu_custom_call" | custom-call | bytes 4194304 | tf_op jit(solution)/shard_map/pallas_call | solution.py:470
  81.4 3.3 %all-to-all-start.1 = ((f32[8,2,2,8]{3,2,1,0:T(2,128)}), f32[8,2,2,8]{3,2,1,0:T(2,128)S(1)}, u32[]{:S(2)}, u32[]{:S(2)}) async-start(f32[8,2,2,8]{3,2,1,0:T(2,128)} %shard_map.75), calls=%async_computation.1 | async-start | bytes 32768 | tf_op jit(solution)/shard_map/all_to_all | solution.py:590
  84.7 0.7 copy.9
  85.4 5.8 %all-to-all-done.1 = f32[8,2,2,8]{3,2,1,0:T(2,128)S(1)} async-done(((f32[8,2,2,8]{3,2,1,0:T(2,128)}), f32[8,2,2,8]{3,2,1,0:T(2,128)S(1)}, u32[]{:S(2)}, u32[]{:S(2)}) %all-to-all-start.1) | async-done | bytes 1056 | tf_op jit(solution)/shard_map/all_to_all | solution.py:590
  91.3 0.6 reduce_sum.9
  (7 shorter events, 0.6 us)
Async XLA Ops:
  3.8 10.1 %collective-permute-start = (s16[272,512]{1,0:T(8,128)(2,1)S(1)}, s16[272,512]{1,0:T(8,128)(2,1)S(1)}, u32[]{:S(2)}, u32[]{:S(2)}) collective-permute-start(s16[272,512]{1,0:T(8,128)(2,1)S(1)} %get-tuple-element.28), channel_id=1, source_target_pairs={{0,1},{1,0},{2,3},{3,2},{4,5},{5,4},{6,7},{7,6},{8,9},{9,8},{10,11... | collective-permute-start | bytes 835592 | tf_op jit(solution)/shard_map/ppermute | solution.py:457
  9.1 8.4 %collective-permute-start.1 = (s16[272,512]{1,0:T(8,128)(2,1)S(1)}, s16[272,512]{1,0:T(8,128)(2,1)S(1)}, u32[]{:S(2)}, u32[]{:S(2)}) collective-permute-start(s16[272,512]{1,0:T(8,128)(2,1)S(1)} %get-tuple-element.29), channel_id=1, source_target_pairs={{1,0},{3,2},{5,4},{7,6},{8,9},{10,11},{12,13},{14,15},{17,16},{19,... | collective-permute-start | bytes 835592 | tf_op jit(solution)/shard_map/ppermute | solution.py:457
  10.4 8.9 %collective-permute-start.2 = (s16[272,512]{1,0:T(8,128)(2,1)S(1)}, s16[272,512]{1,0:T(8,128)(2,1)S(1)}, u32[]{:S(2)}, u32[]{:S(2)}) collective-permute-start(s16[272,512]{1,0:T(8,128)(2,1)S(1)} %get-tuple-element.30), channel_id=1, source_target_pairs={{0,2},{1,3},{2,0},{3,1},{4,6},{5,7},{6,4},{7,5},{8,10},{9,11},{10,... | collective-permute-start | bytes 835592 | tf_op jit(solution)/shard_map/ppermute | solution.py:457
  13.9 11.2 %copy-start.1 = (bf16[1,512,8,8]{1,3,2,0:T(8,128)(2,1)S(1)}, bf16[1,512,8,8]{1,3,2,0:T(8,128)(2,1)}, u32[]{:S(2)}) copy-start(bf16[1,512,8,8]{1,3,2,0:T(8,128)(2,1)} %param.9) | copy-start | bytes 196612
  19.2 25.6 %copy-start = (f32[2]{0:T(128)S(1)}, f32[2]{0:T(128)}, u32[]{:S(2)}) copy-start(f32[2]{0:T(128)} %param.8) | copy-start | bytes 28
  20.1 10.7 %collective-permute-start.3 = (s16[272,512]{1,0:T(8,128)(2,1)S(1)}, s16[272,512]{1,0:T(8,128)(2,1)S(1)}, u32[]{:S(2)}, u32[]{:S(2)}) collective-permute-start(s16[272,512]{1,0:T(8,128)(2,1)S(1)} %get-tuple-element.36), channel_id=1, source_target_pairs={{0,2},{1,3},{2,0},{4,6},{5,7},{6,4},{9,11},{10,8},{11,9},{13,15},{... | collective-permute-start | bytes 835592 | tf_op jit(solution)/shard_map/ppermute | solution.py:457
  23.8 8.4 %collective-permute-start.4 = (s16[272,512]{1,0:T(8,128)(2,1)S(1)}, s16[272,512]{1,0:T(8,128)(2,1)S(1)}, u32[]{:S(2)}, u32[]{:S(2)}) collective-permute-start(s16[272,512]{1,0:T(8,128)(2,1)S(1)} %get-tuple-element.38), channel_id=1, source_target_pairs={{1,0},{3,2},{5,4},{7,6},{8,9},{10,11},{12,13},{14,15},{17,16},{19,... | collective-permute-start | bytes 835592 | tf_op jit(solution)/shard_map/ppermute | solution.py:457
  32.8 12.0 %collective-permute-start.5 = (s16[272,512]{1,0:T(8,128)(2,1)S(1)}, s16[272,512]{1,0:T(8,128)(2,1)S(1)}, u32[]{:S(2)}, u32[]{:S(2)}) collective-permute-start(s16[272,512]{1,0:T(8,128)(2,1)S(1)} %get-tuple-element.40), channel_id=1, source_target_pairs={{0,4},{2,6},{4,0},{6,2},{7,3},{8,12},{9,13},{11,15},{13,9},{15,11}... | collective-permute-start | bytes 835592 | tf_op jit(solution)/shard_map/ppermute | solution.py:457
  81.4 9.8 %all-to-all-start.1 = ((f32[8,2,2,8]{3,2,1,0:T(2,128)}), f32[8,2,2,8]{3,2,1,0:T(2,128)S(1)}, u32[]{:S(2)}, u32[]{:S(2)}) async-start(f32[8,2,2,8]{3,2,1,0:T(2,128)} %shard_map.75), calls=%async_computation.1 | async-start | bytes 32768 | tf_op jit(solution)/shard_map/all_to_all | solution.py:590

commit v8 on v7

--- a/solution.py
+++ b/solution.py
@@ -428,11 +428,11 @@
     t_new = iota(new.shape, 1) % 8
     old = jnp.where(t_row == t_old, old, 0.0)
     new = jnp.where(iota(new.shape, 0) % 8 == t_new, new, 0.0)
-    pick_old = jnp.where(iota((prior, old.shape[1]), 1) % prior == iota((prior, old.shape[1]), 0), 1.0, 0.0)
     features = new.shape[1] // 8
-    pick_new = jnp.where(iota((features, new.shape[1]), 1) // 8 == iota((features, new.shape[1]), 0), 1.0, 0.0)
-    high = lax.Precision.HIGHEST
-    both = jnp.concatenate([nt(pick_old, old, high), nt(pick_new, new, high)], axis=0) * scale
+    picked = jnp.concatenate([old, new], axis=1)
+    row, col = (iota((prior + features, picked.shape[1]), d) for d in (0, 1))
+    wanted = jnp.where(col < old.shape[1], col % prior, prior + (col - old.shape[1]) // 8)
+    both = nt(jnp.where(row == wanted, 1.0, 0.0), picked, lax.Precision.HIGHEST) * scale
     share = (prior + features) // c_ref.shape[0]
     for j in range(2):
         for d in range(c_ref.shape[0]):
@@ -491,7 +491,7 @@
 
         work = pltpu.VMEM((PACKED, BLOCK), f32)
         xt = pltpu.VMEM((BLOCK, rows), bf16)
-        chunks = 4
+        chunks = 8
         gram_flops = 2 * rows * BLOCK * BLOCK
         m0, x_near, yt_near, f_near = call(
             gram_first_kernel,

time: 92.2 us -> 92.4 us (level)
  no operation moved by 1% of the time
where the time goes in v8:
time: 92.4 us; the launch traced here: 92.1 us
  Pallas kernels  26.5 us (29%)
  blocking collectives  24.8 us (27%)
  waiting for transfers between devices  19.8 us (21%)
  starting transfers between devices  18.9 us (20%)
    pallas_call x8, Pallas kernels, call(): pl.pallas_call(functools.partial(kernel, **static), out_shape=outs, in_sp...  26.5 us
    ppermute x6, starting transfers between devices, move(): return lax.ppermute(x, ('blk', 'smp'), pairs(bit, sends))  15.6 us
    ppermute x6, waiting for transfers between devices, move(): return lax.ppermute(x, ('blk', 'smp'), pairs(bit, sends))  14 us
    all_to_all x1, blocking collectives, local(): betas = lax.all_to_all(beta, 'smp', 0, 0)  13.2 us
    all_to_all x1, waiting for transfers between devices, local(): cross = jnp.sum(lax.all_to_all(part, 'smp', 0, 0), axis=0)  5.81 us
    all_gather x1, blocking collectives, local(): prior_all = lax.all_gather(early, 'blk', axis=0)  5.78 us
    all_gather x1, blocking collectives, local(): oof_all = lax.all_gather(oof, 'blk', axis=0, tiled=True)  5.78 us
    all_to_all x1, starting transfers between devices, local(): cross = jnp.sum(lax.all_to_all(part, 'smp', 0, 0), axis=0)  3.31 us
  transfers between devices with their start and end apart: 7, of which 5 were waited for; matrix products, arithmetic and copies ran while one was open for 1% of the time, Pallas kernels for 4%

profile of v8, /device:TPU:0, one launch (start us, length us, event | category | flops | bytes accessed | tf_op | source)
XLA Modules:
  0.0 92.1 jit_solution(16125857937717890169)
XLA Ops:
  0.6 3.3 %shard_map.68 = (s16[272,512]{1,0:T(8,128)(2,1)S(1)}, bf16[2048,512]{1,0:T(8,128)(2,1)S(1)}, bf16[16,2048]{1,0:T(8,128)(2,1)S(1)}, s32[1,2048]{1,0:T(1,128)S(1)}) custom-call(bf16[2048,512]{1,0:T(8,128)(2,1)} %x_hbm.1, bf16[8,2048]{1,0:T(8,128)(2,1)} %bitcast.20, s32[1,2048]{1,0:T(1,128)} %bitcast.21), custom_call_target="tpu_custom_call" | custom-call | flops 1073741824 | bytes 4194304 | tf_op jit(solution)/shard_map/pallas_call | solution.py:470
  3.9 3.1 %collective-permute-start = (s16[272,512]{1,0:T(8,128)(2,1)S(1)}, s16[272,512]{1,0:T(8,128)(2,1)S(1)}, u32[]{:S(2)}, u32[]{:S(2)}) collective-permute-start(s16[272,512]{1,0:T(8,128)(2,1)S(1)} %get-tuple-element.28), channel_id=1, source_target_pairs={{0,1},{1,0},{2,3},{3,2},{4,5},{5,4},{6,7},{7,6},{8,9},{9,8},{10,11... | collective-permute-start | bytes 835592 | tf_op jit(solution)/shard_map/ppermute | solution.py:457
  7.0 2.2 %shard_map.69 = (s16[272,512]{1,0:T(8,128)(2,1)S(1)}, s16[272,512]{1,0:T(8,128)(2,1)S(1)}, f32[272,512]{1,0:T(8,128)S(1)}) custom-call(bf16[2048,512]{1,0:T(8,128)(2,1)S(1)} %get-tuple-element.22.x_ref, bf16[16,2048]{1,0:T(8,128)(2,1)S(1)} %get-tuple-element.23.yt_ref, s32[1,2048]{1,0:T(1,128)S(1)} %get-tuple-element.24.f_ref), custom_call_target="tpu_custom_call" | custom-call | flops 2147483648 | bytes 4194304 | tf_op jit(solution)/shard_map/pallas_call | solution.py:470
  9.2 1.3 %collective-permute-start.1 = (s16[272,512]{1,0:T(8,128)(2,1)S(1)}, s16[272,512]{1,0:T(8,128)(2,1)S(1)}, u32[]{:S(2)}, u32[]{:S(2)}) collective-permute-start(s16[272,512]{1,0:T(8,128)(2,1)S(1)} %get-tuple-element.29), channel_id=1, source_target_pairs={{1,0},{3,2},{5,4},{7,6},{8,9},{10,11},{12,13},{14,15},{17,16},{19,... | collective-permute-start | bytes 835592 | tf_op jit(solution)/shard_map/ppermute | solution.py:457
  10.5 1.6 %collective-permute-start.2 = (s16[272,512]{1,0:T(8,128)(2,1)S(1)}, s16[272,512]{1,0:T(8,128)(2,1)S(1)}, u32[]{:S(2)}, u32[]{:S(2)}) collective-permute-start(s16[272,512]{1,0:T(8,128)(2,1)S(1)} %get-tuple-element.30), channel_id=1, source_target_pairs={{0,2},{1,3},{2,0},{3,1},{4,6},{5,7},{6,4},{7,5},{8,10},{9,11},{10,... | collective-permute-start | bytes 835592 | tf_op jit(solution)/shard_map/ppermute | solution.py:457
  12.2 1.9 %shard_map.70 = (f32[272,512]{1,0:T(8,128)S(1)}, f32[272,512]{1,0:T(8,128)S(1)}) custom-call(bf16[2048,512]{1,0:T(8,128)(2,1)S(1)} %get-tuple-element.22.x_ref, bf16[16,2048]{1,0:T(8,128)(2,1)S(1)} %get-tuple-element.23.yt_ref, s32[1,2048]{1,0:T(1,128)S(1)} %get-tuple-element.24.f_ref), custom_call_target="tpu_custom_call" | custom-call | flops 2147483648 | bytes 4194304 | tf_op jit(solution)/shard_map/pallas_call | solution.py:470
  14.1 3.6 %collective-permute-done.1.p2_ref = s16[272,512]{1,0:T(8,128)(2,1)S(1)} collective-permute-done((s16[272,512]{1,0:T(8,128)(2,1)S(1)}, s16[272,512]{1,0:T(8,128)(2,1)S(1)}, u32[]{:S(2)}, u32[]{:S(2)}) %collective-permute-start.1) | collective-permute-done | bytes 278560 | tf_op jit(solution)/shard_map/ppermute | solution.py:457
  17.7 1.7 %collective-permute-done.2.p3_ref = s16[272,512]{1,0:T(8,128)(2,1)S(1)} collective-permute-done((s16[272,512]{1,0:T(8,128)(2,1)S(1)}, s16[272,512]{1,0:T(8,128)(2,1)S(1)}, u32[]{:S(2)}, u32[]{:S(2)}) %collective-permute-start.2) | collective-permute-done | bytes 278560 | tf_op jit(solution)/shard_map/ppermute | solution.py:457
  19.4 0.9 shard_map.71
  20.3 3.6 %collective-permute-start.3 = (s16[272,512]{1,0:T(8,128)(2,1)S(1)}, s16[272,512]{1,0:T(8,128)(2,1)S(1)}, u32[]{:S(2)}, u32[]{:S(2)}) collective-permute-start(s16[272,512]{1,0:T(8,128)(2,1)S(1)} %get-tuple-element.36), channel_id=1, source_target_pairs={{0,2},{1,3},{2,0},{4,6},{5,7},{6,4},{9,11},{10,8},{11,9},{13,15},{... | collective-permute-start | bytes 835592 | tf_op jit(solution)/shard_map/ppermute | solution.py:457
  23.9 1.3 %collective-permute-start.4 = (s16[272,512]{1,0:T(8,128)(2,1)S(1)}, s16[272,512]{1,0:T(8,128)(2,1)S(1)}, u32[]{:S(2)}, u32[]{:S(2)}) collective-permute-start(s16[272,512]{1,0:T(8,128)(2,1)S(1)} %get-tuple-element.38), channel_id=1, source_target_pairs={{1,0},{3,2},{5,4},{7,6},{8,9},{10,11},{12,13},{14,15},{17,16},{19,... | collective-permute-start | bytes 835592 | tf_op jit(solution)/shard_map/ppermute | solution.py:457
  25.2 5.8 %all-gather = bf16[256,512]{1,0:T(8,128)(2,1)S(1)} all-gather(bf16[64,512]{1,0:T(8,128)(2,1)S(1)} %bitcast.17), channel_id=2, replica_groups=mesh['blk'=4,'smp'=8] {'blk'}, dimensions={0}, use_global_device_ids=true | all-gather | bytes 327680 | tf_op jit(solution)/shard_map/all_gather | solution.py:549
  31.0 1.3 %collective-permute-done.4.p5_ref = s16[272,512]{1,0:T(8,128)(2,1)S(1)} collective-permute-done((s16[272,512]{1,0:T(8,128)(2,1)S(1)}, s16[272,512]{1,0:T(8,128)(2,1)S(1)}, u32[]{:S(2)}, u32[]{:S(2)}) %collective-permute-start.4) | collective-permute-done | bytes 278560 | tf_op jit(solution)/shard_map/ppermute | solution.py:457
  32.9 4.7 %collective-permute-start.5 = (s16[272,512]{1,0:T(8,128)(2,1)S(1)}, s16[272,512]{1,0:T(8,128)(2,1)S(1)}, u32[]{:S(2)}, u32[]{:S(2)}) collective-permute-start(s16[272,512]{1,0:T(8,128)(2,1)S(1)} %get-tuple-element.40), channel_id=1, source_target_pairs={{0,4},{2,6},{4,0},{6,2},{7,3},{8,12},{9,13},{11,15},{13,9},{15,11}... | collective-permute-start | bytes 835592 | tf_op jit(solution)/shard_map/ppermute | solution.py:457
  37.6 7.4 %collective-permute-done.5.p_ref = s16[272,512]{1,0:T(8,128)(2,1)S(1)} collective-permute-done((s16[272,512]{1,0:T(8,128)(2,1)S(1)}, s16[272,512]{1,0:T(8,128)(2,1)S(1)}, u32[]{:S(2)}, u32[]{:S(2)}) %collective-permute-start.5) | collective-permute-done | bytes 278560 | tf_op jit(solution)/shard_map/ppermute | solution.py:457
  45.0 15.8 %shard_map.73 = bf16[8,16,512]{2,1,0:T(8,128)(2,1)S(1)} custom-call(f32[1,2]{1,0:T(1,128)S(1)} %bitcast.16, f32[272,512]{1,0:T(8,128)S(1)} %get-tuple-element.39.k_ref, s16[272,512]{1,0:T(8,128)(2,1)S(1)} %collective-permute-done.5.p_ref), custom_call_target="tpu_custom_call" | custom-call | bytes 4194304 | tf_op jit(solution)/shard_map/pallas_call | solution.py:470
  60.8 13.2 %all_to_all.10.b_ref = bf16[8,16,512]{2,1,0:T(8,128)(2,1)S(1)} all-to-all(bf16[8,16,512]{2,1,0:T(8,128)(2,1)S(1)} %shard_map.73), channel_id=1, replica_groups=mesh['blk'=4,'smp'=8] {'smp'}, dimensions={0} | all-to-all | bytes 262144 | tf_op jit(solution)/shard_map/all_to_all | solution.py:566
  74.0 0.8 shard_map.74.o_ref
  74.7 5.8 %all_gather.11.j_ref = bf16[64,2048]{1,0:T(8,128)(2,1)S(1)} all-gather(bf16[16,2048]{1,0:T(8,128)(2,1)S(1)} %shard_map.74.o_ref), channel_id=1, replica_groups=mesh['blk'=4,'smp'=8] {'blk'}, dimensions={0}, use_global_device_ids=true | all-gather | bytes 327680 | tf_op jit(solution)/shard_map/all_gather | solution.py:578
  80.5 1.1 %shard_map.75 = f32[8,2,2,8]{3,2,1,0:T(2,128)} custom-call(bf16[16,2048]{1,0:T(8,128)(2,1)S(1)} %shard_map.74.o_ref, bf16[64,2048]{1,0:T(8,128)(2,1)S(1)} %all_gather.11.j_ref, bf16[4,64,512]{2,1,0:T(8,128)(2,1)S(1)} %bitcast.15), custom_call_target="tpu_custom_call" | custom-call | bytes 4194304 | tf_op jit(solution)/shard_map/pallas_call | solution.py:470
  81.7 3.3 %all-to-all-start.1 = ((f32[8,2,2,8]{3,2,1,0:T(2,128)}), f32[8,2,2,8]{3,2,1,0:T(2,128)S(1)}, u32[]{:S(2)}, u32[]{:S(2)}) async-start(f32[8,2,2,8]{3,2,1,0:T(2,128)} %shard_map.75), calls=%async_computation.1 | async-start | bytes 32768 | tf_op jit(solution)/shard_map/all_to_all | solution.py:590
  85.0 0.7 copy.9
  85.7 5.8 %all-to-all-done.1 = f32[8,2,2,8]{3,2,1,0:T(2,128)S(1)} async-done(((f32[8,2,2,8]{3,2,1,0:T(2,128)}), f32[8,2,2,8]{3,2,1,0:T(2,128)S(1)}, u32[]{:S(2)}, u32[]{:S(2)}) %all-to-all-start.1) | async-done | bytes 1056 | tf_op jit(solution)/shard_map/all_to_all | solution.py:590
  91.5 0.6 reduce_sum.9
  (7 shorter events, 0.6 us)
Async XLA Ops:
  3.9 10.1 %collective-permute-start = (s16[272,512]{1,0:T(8,128)(2,1)S(1)}, s16[272,512]{1,0:T(8,128)(2,1)S(1)}, u32[]{:S(2)}, u32[]{:S(2)}) collective-permute-start(s16[272,512]{1,0:T(8,128)(2,1)S(1)} %get-tuple-element.28), channel_id=1, source_target_pairs={{0,1},{1,0},{2,3},{3,2},{4,5},{5,4},{6,7},{7,6},{8,9},{9,8},{10,11... | collective-permute-start | bytes 835592 | tf_op jit(solution)/shard_map/ppermute | solution.py:457
  9.2 8.4 %collective-permute-start.1 = (s16[272,512]{1,0:T(8,128)(2,1)S(1)}, s16[272,512]{1,0:T(8,128)(2,1)S(1)}, u32[]{:S(2)}, u32[]{:S(2)}) collective-permute-start(s16[272,512]{1,0:T(8,128)(2,1)S(1)} %get-tuple-element.29), channel_id=1, source_target_pairs={{1,0},{3,2},{5,4},{7,6},{8,9},{10,11},{12,13},{14,15},{17,16},{19,... | collective-permute-start | bytes 835592 | tf_op jit(solution)/shard_map/ppermute | solution.py:457
  10.5 8.9 %collective-permute-start.2 = (s16[272,512]{1,0:T(8,128)(2,1)S(1)}, s16[272,512]{1,0:T(8,128)(2,1)S(1)}, u32[]{:S(2)}, u32[]{:S(2)}) collective-permute-start(s16[272,512]{1,0:T(8,128)(2,1)S(1)} %get-tuple-element.30), channel_id=1, source_target_pairs={{0,2},{1,3},{2,0},{3,1},{4,6},{5,7},{6,4},{7,5},{8,10},{9,11},{10,... | collective-permute-start | bytes 835592 | tf_op jit(solution)/shard_map/ppermute | solution.py:457
  14.1 11.2 %copy-start.1 = (bf16[1,512,8,8]{1,3,2,0:T(8,128)(2,1)S(1)}, bf16[1,512,8,8]{1,3,2,0:T(8,128)(2,1)}, u32[]{:S(2)}) copy-start(bf16[1,512,8,8]{1,3,2,0:T(8,128)(2,1)} %param.9) | copy-start | bytes 196612
  19.4 25.6 %copy-start = (f32[2]{0:T(128)S(1)}, f32[2]{0:T(128)}, u32[]{:S(2)}) copy-start(f32[2]{0:T(128)} %param.8) | copy-start | bytes 28
  20.3 10.7 %collective-permute-start.3 = (s16[272,512]{1,0:T(8,128)(2,1)S(1)}, s16[272,512]{1,0:T(8,128)(2,1)S(1)}, u32[]{:S(2)}, u32[]{:S(2)}) collective-permute-start(s16[272,512]{1,0:T(8,128)(2,1)S(1)} %get-tuple-element.36), channel_id=1, source_target_pairs={{0,2},{1,3},{2,0},{4,6},{5,7},{6,4},{9,11},{10,8},{11,9},{13,15},{... | collective-permute-start | bytes 835592 | tf_op jit(solution)/shard_map/ppermute | solution.py:457
  23.9 8.4 %collective-permute-start.4 = (s16[272,512]{1,0:T(8,128)(2,1)S(1)}, s16[272,512]{1,0:T(8,128)(2,1)S(1)}, u32[]{:S(2)}, u32[]{:S(2)}) collective-permute-start(s16[272,512]{1,0:T(8,128)(2,1)S(1)} %get-tuple-element.38), channel_id=1, source_target_pairs={{1,0},{3,2},{5,4},{7,6},{8,9},{10,11},{12,13},{14,15},{17,16},{19,... | collective-permute-start | bytes 835592 | tf_op jit(solution)/shard_map/ppermute | solution.py:457
  32.9 12.0 %collective-permute-start.5 = (s16[272,512]{1,0:T(8,128)(2,1)S(1)}, s16[272,512]{1,0:T(8,128)(2,1)S(1)}, u32[]{:S(2)}, u32[]{:S(2)}) collective-permute-start(s16[272,512]{1,0:T(8,128)(2,1)S(1)} %get-tuple-element.40), channel_id=1, source_target_pairs={{0,4},{2,6},{4,0},{6,2},{7,3},{8,12},{9,13},{11,15},{13,9},{15,11}... | collective-permute-start | bytes 835592 | tf_op jit(solution)/shard_map/ppermute | solution.py:457
  81.7 9.8 %all-to-all-start.1 = ((f32[8,2,2,8]{3,2,1,0:T(2,128)}), f32[8,2,2,8]{3,2,1,0:T(2,128)S(1)}, u32[]{:S(2)}, u32[]{:S(2)}) async-start(f32[8,2,2,8]{3,2,1,0:T(2,128)} %shard_map.75), calls=%async_computation.1 | async-start | bytes 32768 | tf_op jit(solution)/shard_map/all_to_all | solution.py:590
